TPU v7x, 256 devices: a whole 4x4x8 slice. The times are simulated.
256 devices in a mesh: wide: 32 (over z, y), slab: 8 (over x, core).
Axes of the slice: x: 4, y: 4, z: 8, core: 2. Of those that a mesh axis runs over, the one named last changes fastest.
Arguments:
- thermal_state: float32 [32, 128, 32, 1024], P('wide', 'slab'), may hold values from -5 to 5
- thermal_spreading_rate: bfloat16 [32, 128, 32, 1024], P('wide', 'slab'), may hold values from 0.5 to 1.5
- flow_speed_vector: bfloat16 [3, 32, 128, 32, 1024], P(None, 'wide', 'slab'), may hold values from -0.796875 to 0.796875
- interface_guess: float32 [32, 2048], P('wide', 'slab'), may hold values from -4 to 4
- partner_facing_rows: int32 [32, 2048], P('wide', 'slab'), may hold values from 0 to 2047, each once within a row
- mismatch_change_matrix: float32 [32, 2048, 128], P('wide', 'slab'), may hold values from -5 to 5
- output_change_matrix: float32 [32, 2048, 128], P('wide', 'slab'), may hold values from -1.8 to 1.8
Outputs:
- temperature_out: float32 [32, 128, 32, 1024], P('wide', 'slab')
- updated_interface_guess: float32 [32, 2048], P('wide', 'slab')
- unitary_basis_factor: float32 [32, 2048, 128], P('wide', 'slab')
Inputs may be any that keep to these rules, and one draw needn't show every extreme that they name: `partner_facing_rows`: each partition's rows of matching are a permutation of its partner's interface rows.
All inputs are finite; a program needn't handle non-finite values.
Results may differ from a plain program's by a relative error of at most 0.0003.
Values may be sent and summed in bfloat16 or wider, within the bound.
No kernel may reach another device: no remote copies, remote signals or barrier semaphores. Data moves between devices by JAX's collectives and lax.ppermute only.
A program may use at most 64 MiB of HBM per device.

v0:
```python
import math

import jax
import jax.numpy as jnp
from jax import lax
from jax.sharding import PartitionSpec as P

INTERFACE_STRIP = 64
SWEEPS = 4


STEP_SIZE = 0.11


def padded(cells, sides, width):
    for axis, dim in sides:
        count = lax.axis_size(axis)
        ends = count - 1
        head = lax.slice_in_dim(cells, 0, width, axis=dim)
        tail = lax.slice_in_dim(cells, cells.shape[dim] - width, cells.shape[dim], axis=dim)
        cells = jnp.concatenate(
            [
                lax.ppermute(tail, axis, [(i, (i + 1) % count) for i in range(ends)]),
                cells,
                lax.ppermute(head, axis, [((i + 1) % count, i) for i in range(ends)]),
            ],
            axis=dim,
        )
    return cells


def partner(value, axis, stride):
    mask = 2**stride
    pairs = [(source, source ^ mask) for source in range(lax.axis_size(axis))]
    return lax.ppermute(value, axis, pairs)


def surround_wrapper(block_rows, mirror_layer):
    bottom = jnp.zeros((block_rows.shape[0], 1, block_rows.shape[2]), block_rows.dtype)
    stacked = jnp.concatenate([bottom, block_rows, mirror_layer[:, None, :]], axis=1)
    return jnp.pad(stacked, ((0, 0), (0, 0), (1, 1)))


def march_forward(bordered_array, diffuse_subdomain, subdomain_flow_speed):
    centre = bordered_array[1:-1, 1:-1, 1:-1]
    plus_first = bordered_array[2:, 1:-1, 1:-1]
    minus_first = bordered_array[:-2, 1:-1, 1:-1]
    plus_second = bordered_array[1:-1, 2:, 1:-1]
    minus_second = bordered_array[1:-1, :-2, 1:-1]
    plus_third = bordered_array[1:-1, 1:-1, 2:]
    minus_third = bordered_array[1:-1, 1:-1, :-2]
    spread = (
        plus_first
        + minus_first
        + plus_second
        + minus_second
        + plus_third
        + minus_third
        - 6.0 * centre
    )
    carried = 0.5 * (
        subdomain_flow_speed[0].astype(jnp.float32) * (plus_first - minus_first)
        + subdomain_flow_speed[1].astype(jnp.float32) * (plus_second - minus_second)
        + subdomain_flow_speed[2].astype(jnp.float32) * (plus_third - minus_third)
    )
    return centre + STEP_SIZE * (diffuse_subdomain.astype(jnp.float32) * spread - carried)


def shards(
    thermal_state,
    thermal_spreading_rate,
    flow_speed_vector,
    interface_guess,
    partner_facing_rows,
    mismatch_change_matrix,
    output_change_matrix,
):
    subdomain_thermal_state = thermal_state[0]
    diffuse_subdomain = thermal_spreading_rate[0]
    subdomain_flow_speed = flow_speed_vector[:, 0]
    layer_stack = subdomain_thermal_state.shape[0]
    vertical_extent = subdomain_thermal_state.shape[1]
    rows_dev = interface_guess.shape[1]
    mirror_layer = jnp.repeat(interface_guess[0].reshape(layer_stack, -1), INTERFACE_STRIP, axis=1)
    panel = mismatch_change_matrix[0]
    gram_local = lax.dot_general(
        panel,
        panel,
        (((0,), (0,)), ((), ())),
        precision=lax.Precision.HIGHEST,
        preferred_element_type=jnp.float32,
    )
    ghost_padded = jnp.pad(mirror_layer, ((1, 1), (0, 0)))
    for sweep in range(SWEEPS):
        widened_array = padded(subdomain_thermal_state, (("slab", 0),), 1)
        subdomain_thermal_state = march_forward(
            surround_wrapper(widened_array, ghost_padded), diffuse_subdomain, subdomain_flow_speed
        )
    face_means = jnp.mean(
        subdomain_thermal_state[:, vertical_extent - 1, :].reshape(
            layer_stack, -1, INTERFACE_STRIP
        ),
        axis=2,
    )
    face_means = face_means.reshape(1, rows_dev)
    top_bit = lax.axis_size("wide").bit_length() - 2
    partner_own = partner(face_means, "wide", top_bit)
    partner_all = lax.all_gather(partner_own, "slab", axis=1, tiled=True)
    tilde = jnp.take(partner_all[0], partner_facing_rows[0], axis=0)
    resid = tilde - interface_guess[0]
    proj_local = jnp.dot(
        resid, panel, precision=lax.Precision.HIGHEST, preferred_element_type=jnp.float32
    )
    gram_matrix, projection = lax.psum((gram_local, proj_local), ("wide", "slab"))
    lower_factor = jnp.linalg.cholesky(gram_matrix)
    half_solve = lax.linalg.triangular_solve(
        lower_factor, projection[:, None], left_side=True, lower=True
    )
    coefficients = -lax.linalg.triangular_solve(
        lower_factor, half_solve, left_side=True, lower=True, transpose_a=True
    )[:, 0]
    update = jnp.dot(
        output_change_matrix[0],
        coefficients,
        precision=lax.Precision.HIGHEST,
        preferred_element_type=jnp.float32,
    )
    updated_interface_guess = tilde + update
    total_rows = rows_dev * lax.axis_size("slab") * lax.axis_size("wide")
    scaled = lax.linalg.triangular_solve(
        lower_factor, panel, left_side=False, lower=True, transpose_a=True
    )
    unitary_basis_factor = math.sqrt(total_rows) * scaled
    return (
        subdomain_thermal_state[None],
        updated_interface_guess[None],
        unitary_basis_factor[None],
    )


def solution(mesh):
    return jax.shard_map(
        shards,
        mesh=mesh,
        in_specs=(
            P("wide", "slab", None, None),
            P("wide", "slab", None, None),
            P(None, "wide", "slab", None, None),
            P("wide", "slab"),
            P("wide", "slab"),
            P("wide", "slab", None),
            P("wide", "slab", None),
        ),
        out_specs=(P("wide", "slab", None, None), P("wide", "slab"), P("wide", "slab", None)),
        check_vma=False,
    )
```

profile of v0, /device:TPU:1, one launch (start us, length us, event | category | flops | bytes accessed | tf_op | source)
XLA Modules:
  0.0 438.8 jit_solution(339822084845978649)
XLA Ops:
  7.2 1.0 slice_bitcast_fusion
  8.2 5.1 %collective-permute-start = (f32[1,32,1024]{2,1,0:T(8,128)S(1)}, f32[1,32,1024]{2,1,0:T(8,128)S(1)}, u32[]{:S(2)}, u32[]{:S(2)}) collective-permute-start(f32[1,32,1024]{2,1,0:T(8,128)S(1)} %get-tuple-element.16), channel_id=1, source_target_pairs={{1,0},{2,1},{3,2},{4,3},{5,4},{6,5},{7,6},{9,8},{10,9},{11,10},{12... | collective-permute-start | bytes 393224 | tf_op jit(solution)/shard_map/ppermute | solution.py:25
  13.4 1.9 collective-permute-start.1
  15.3 1.0 fusion.39
  17.6 1.3 reduce.11
  19.3 237.0 %all-reduce.11.cloned.1.call-done = f32[128,128]{0,1:T(8,128)} async-done(((f32[128,128]{0,1:T(8,128)}), f32[128,128]{0,1:T(8,128)}) %all-reduce.11.cloned.1.call-update) | async-done | bytes 65552 | tf_op jit(solution)/shard_map/psum | solution.py:114
  256.3 0.9 copy.14
  257.9 2.3 pad_maximum_fusion.3
  260.7 7.0 %fusion.2 = f32[16,32,1024]{2,1,0:T(8,128)S(1)} fusion(f32[16,32,1024]{2,1,0:T(8,128)} %bitcast.90, f32[18,34,1024]{2,1,0:T(8,128)S(1)} %pad_maximum_fusion.3, f32[1,32,1024]{2,1,0:T(8,128)S(1)} %collective-permute-done, f32[1,32,1024]{2,1,0:T(8,128)S(1)} %copy-done.11, f32[18,1,1024]{2,1,0:T(1,128)S(1)} %broadcast_in_dim.30, ...), kind=kLoop, calls=%fused_computation.35 | loop fusion | flops 18874368 | bytes 11231232 | tf_op jit(solution)/shard_map/add | solution.py:66
  267.8 1.3 copy-done.4
  269.8 1.9 collective-permute-start.2
  271.7 3.6 collective-permute-start.3
  276.0 12.5 %cholesky.16 = f32[128,128]{1,0:T(8,128)S(1)} custom-call(f32[128,128]{1,0:T(8,128)} %fusion.45), custom_call_target="Cholesky" | custom-call | tf_op jit(solution)/shard_map/jit(cholesky)/cholesky | solution.py:115
  288.6 2.3 pad_maximum_fusion.2
  291.1 4.6 %fusion.5 = f32[16,32,1024]{2,1,0:T(8,128)S(1)} fusion(f32[16,32,1024]{2,1,0:T(8,128)S(1)} %copy-done.5, f32[18,34,1024]{2,1,0:T(8,128)S(1)} %pad_maximum_fusion.2, f32[1,32,1024]{2,1,0:T(8,128)S(1)} %collective-permute-done.2, f32[1,32,1024]{2,1,0:T(8,128)} %collective-permute-done.3, f32[18,1,1024]{2,1,0:T(1,128)S(1)} %broadcast_in_dim.30, ...), kind=kLoop, calls=%fused_computation.38 | loop fusion | flops 18874368 | bytes 11231232 | tf_op jit(solution)/shard_map/add | solution.py:66
  295.8 1.9 collective-permute-start.4
  297.7 3.8 collective-permute-start.5
  302.2 1.1 collective-permute-done.5
  304.0 5.4 %fusion.8 = f32[16,32,1024]{2,1,0:T(8,128)S(1)} fusion(f32[16,32,1024]{2,1,0:T(8,128)S(1)} %fusion.5, f32[18,34,1024]{2,1,0:T(8,128)S(1)} %pad_maximum_fusion.1, f32[1,32,1024]{2,1,0:T(8,128)S(1)} %collective-permute-done.4, f32[1,32,1024]{2,1,0:T(8,128)S(1)} %collective-permute-done.5, f32[18,1,1024]{2,1,0:T(1,128)S(1)} %broadcast_in_dim.30, ...), kind=kLoop, calls=%fused_computation.41 | loop fusion | flops 18874368 | bytes 11231232 | tf_op jit(solution)/shard_map/add | solution.py:66
  309.4 1.3 copy-done.2
  311.4 1.9 collective-permute-start.6
  313.3 4.4 collective-permute-start.7
  317.7 1.3 fusion.41
  319.0 10.6 %custom-call.10 = f32[1,128,128]{1,2,0:T(8,128)S(1)} custom-call(f32[1,128,128]{2,1,0:T(8,128)} %fusion.41), custom_call_target="InvertDiagBlocksLowerTriangular" | custom-call | tf_op jit(solution)/shard_map/triangular_solve | solution.py:119
  329.7 2.3 pad_maximum_fusion
  332.2 4.6 %fusion.11 = f32[16,32,1024]{2,1,0:T(8,128)S(1)} fusion(f32[16,32,1024]{2,1,0:T(8,128)S(1)} %copy-done.3, f32[18,34,1024]{2,1,0:T(8,128)S(1)} %pad_maximum_fusion, f32[1,32,1024]{2,1,0:T(8,128)S(1)} %collective-permute-done.6, f32[1,32,1024]{2,1,0:T(8,128)} %collective-permute-done.7, f32[18,1,1024]{2,1,0:T(1,128)S(1)} %broadcast_in_dim.30, ...), kind=kLoop, calls=%fused_computation.44 | loop fusion | flops 18874368 | bytes 11231232 | tf_op jit(solution)/shard_map/add | solution.py:66
  336.8 1.3 copy-done.9
  338.6 0.9 collective-permute-start.8
  340.6 4.4 %collective-permute-done.8 = f32[1,256]{1,0:T(1,128)S(1)} collective-permute-done((f32[1,256]{1,0:T(1,128)S(1)}, f32[1,256]{1,0:T(1,128)S(1)}, u32[]{:S(2)}, u32[]{:S(2)}) %collective-permute-start.8) | collective-permute-done | bytes 1056 | tf_op jit(solution)/shard_map/ppermute | solution.py:35
  345.0 10.1 %all_gather.3 = f32[1,2048]{1,0:T(1,128)S(1)} all-gather(f32[1,256]{1,0:T(1,128)S(1)} %collective-permute-done.8), channel_id=1, replica_groups=mesh['wide'=32,'slab'=8] {'slab'}, dimensions={1}, use_global_device_ids=true | all-gather | bytes 9216 | tf_op jit(solution)/shard_map/all_gather | solution.py:108
  355.1 1.7 gather_fusion
  357.0 73.7 %psum.15 = f32[128]{0:T(128)S(1)} all-reduce(f32[128]{0:T(128)S(1)} %convolution_bitcast_fusion.2), channel_id=1, replica_groups=mesh['wide'=32,'slab'=8] {'wide','slab'}, use_global_device_ids=true, to_apply=%region_4.5 | all-reduce | flops 128 | bytes 1024 | tf_op jit(solution)/shard_map/psum | solution.py:114
  (70 shorter events, 9.6 us)
Async XLA Ops:
  7.2 8.2 %copy-start = (f32[1,256,128]{2,1,0:T(8,128)S(1)}, f32[1,256,128]{2,1,0:T(8,128)}, u32[]{:S(2)}) copy-start(f32[1,256,128]{2,1,0:T(8,128)} %param.12) | copy-start | bytes 393220
  7.2 249.1 %all-reduce.11.cloned.1.call-start = ((), (), s32[]{:S(2)}) async-start(), calls=%async_computation | async-start | bytes 131072 | tf_op jit(solution)/shard_map/psum | solution.py:114
  8.2 249.0 %collective-permute-start = (f32[1,32,1024]{2,1,0:T(8,128)S(1)}, f32[1,32,1024]{2,1,0:T(8,128)S(1)}, u32[]{:S(2)}, u32[]{:S(2)}) collective-permute-start(f32[1,32,1024]{2,1,0:T(8,128)S(1)} %get-tuple-element.16), channel_id=1, source_target_pairs={{1,0},{2,1},{3,2},{4,3},{5,4},{6,5},{7,6},{9,8},{10,9},{11,10},{12... | collective-permute-start | bytes 393224 | tf_op jit(solution)/shard_map/ppermute | solution.py:25
  13.4 243.8 %collective-permute-start.1 = (f32[1,32,1024]{2,1,0:T(8,128)S(1)}, f32[1,32,1024]{2,1,0:T(8,128)S(1)}, u32[]{:S(2)}, u32[]{:S(2)}) collective-permute-start(f32[1,32,1024]{2,1,0:T(8,128)S(1)} %get-tuple-element.15), channel_id=1, source_target_pairs={{0,1},{1,2},{2,3},{3,4},{4,5},{5,6},{6,7},{8,9},{9,10},{10,11},{11... | collective-permute-start | bytes 393224 | tf_op jit(solution)/shard_map/ppermute | solution.py:23
  257.2 0.7 copy-start.10
  257.9 2.6 copy-start.1
  257.9 2.8 copy-start.6
  257.9 2.8 copy-start.11
  260.7 14.6 %copy-start.12 = (f32[128,128]{0,1:T(8,128)S(1)}, f32[128,128]{0,1:T(8,128)}, u32[]{:S(2)}) copy-start(f32[128,128]{0,1:T(8,128)} %all-reduce.11.cloned.1.call-done) | copy-start | bytes 196612
  267.8 1.3 copy-start.4
  269.8 18.8 %collective-permute-start.2 = (f32[1,32,1024]{2,1,0:T(8,128)}, f32[1,32,1024]{2,1,0:T(8,128)S(1)}, u32[]{:S(2)}, u32[]{:S(2)}) collective-permute-start(f32[1,32,1024]{2,1,0:T(8,128)} %get-tuple-element.14), channel_id=1, source_target_pairs={{1,0},{2,1},{3,2},{4,3},{5,4},{6,5},{7,6},{9,8},{10,9},{11,10},{12... | collective-permute-start | bytes 393224 | tf_op jit(solution)/shard_map/ppermute | solution.py:25
  271.7 16.9 %collective-permute-start.3 = (f32[1,32,1024]{2,1,0:T(8,128)}, f32[1,32,1024]{2,1,0:T(8,128)}, u32[]{:S(2)}, u32[]{:S(2)}) collective-permute-start(f32[1,32,1024]{2,1,0:T(8,128)} %get-tuple-element.13), channel_id=1, source_target_pairs={{0,1},{1,2},{2,3},{3,4},{4,5},{5,6},{6,7},{8,9},{9,10},{10,11},{11... | collective-permute-start | bytes 393224 | tf_op jit(solution)/shard_map/ppermute | solution.py:23
  288.6 13.0 %copy-start.13 = (f32[128,128]{1,0:T(8,128)}, f32[128,128]{1,0:T(8,128)S(1)}, u32[]{:S(2)}) copy-start(f32[128,128]{1,0:T(8,128)S(1)} %cholesky.16) | copy-start | bytes 196612
  288.6 2.3 copy-start.5
  288.6 2.5 copy-start.7
  295.8 6.4 %collective-permute-start.4 = (f32[1,32,1024]{2,1,0:T(8,128)S(1)}, f32[1,32,1024]{2,1,0:T(8,128)S(1)}, u32[]{:S(2)}, u32[]{:S(2)}) collective-permute-start(f32[1,32,1024]{2,1,0:T(8,128)S(1)} %get-tuple-element.12), channel_id=1, source_target_pairs={{1,0},{2,1},{3,2},{4,3},{5,4},{6,5},{7,6},{9,8},{10,9},{11,10},{12... | collective-permute-start | bytes 393224 | tf_op jit(solution)/shard_map/ppermute | solution.py:25
  297.7 5.6 %collective-permute-start.5 = (f32[1,32,1024]{2,1,0:T(8,128)S(1)}, f32[1,32,1024]{2,1,0:T(8,128)S(1)}, u32[]{:S(2)}, u32[]{:S(2)}) collective-permute-start(f32[1,32,1024]{2,1,0:T(8,128)S(1)} %get-tuple-element.11), channel_id=1, source_target_pairs={{0,1},{1,2},{2,3},{3,4},{4,5},{5,6},{6,7},{8,9},{9,10},{10,11},{11... | collective-permute-start | bytes 393224 | tf_op jit(solution)/shard_map/ppermute | solution.py:23
  304.0 13.7 %copy-start.14 = (f32[128,128]{1,0:T(8,128)S(1)}, f32[128,128]{1,0:T(8,128)}, u32[]{:S(2)}) copy-start(f32[128,128]{1,0:T(8,128)} %copy-done.13) | copy-start | bytes 196612
  309.4 1.3 copy-start.2
  311.4 18.2 %collective-permute-start.6 = (f32[1,32,1024]{2,1,0:T(8,128)}, f32[1,32,1024]{2,1,0:T(8,128)S(1)}, u32[]{:S(2)}, u32[]{:S(2)}) collective-permute-start(f32[1,32,1024]{2,1,0:T(8,128)} %get-tuple-element.10), channel_id=1, source_target_pairs={{1,0},{2,1},{3,2},{4,3},{5,4},{6,5},{7,6},{9,8},{10,9},{11,10},{12... | collective-permute-start | bytes 393224 | tf_op jit(solution)/shard_map/ppermute | solution.py:25
  313.3 16.3 %collective-permute-start.7 = (f32[1,32,1024]{2,1,0:T(8,128)}, f32[1,32,1024]{2,1,0:T(8,128)}, u32[]{:S(2)}, u32[]{:S(2)}) collective-permute-start(f32[1,32,1024]{2,1,0:T(8,128)} %get-tuple-element.9), channel_id=1, source_target_pairs={{0,1},{1,2},{2,3},{3,4},{4,5},{5,6},{6,7},{8,9},{9,10},{10,11},{11... | collective-permute-start | bytes 393224 | tf_op jit(solution)/shard_map/ppermute | solution.py:23
  329.6 2.3 copy-start.3
  329.7 2.5 copy-start.8
  336.8 1.3 copy-start.9
  338.2 18.6 %copy-start.16 = (s32[1,256]{1,0:T(1,128)S(1)}, s32[1,256]{1,0:T(1,128)}, u32[]{:S(2)}) copy-start(s32[1,256]{1,0:T(1,128)} %param.11) | copy-start | bytes 3076
  338.2 18.6 %copy-start.17 = (f32[1,256]{1,0:T(1,128)S(1)}, f32[1,256]{1,0:T(1,128)}, u32[]{:S(2)}) copy-start(f32[1,256]{1,0:T(1,128)} %param.10) | copy-start | bytes 3076
  338.2 92.9 %copy-start.15 = (f32[1,256,128]{2,1,0:T(8,128)S(1)}, f32[1,256,128]{2,1,0:T(8,128)}, u32[]{:S(2)}) copy-start(f32[1,256,128]{2,1,0:T(8,128)} %param.13) | copy-start | bytes 393220
  338.6 6.4 %collective-permute-start.8 = (f32[1,256]{1,0:T(1,128)S(1)}, f32[1,256]{1,0:T(1,128)S(1)}, u32[]{:S(2)}, u32[]{:S(2)}) collective-permute-start(f32[1,256]{1,0:T(1,128)S(1)} %div.18), channel_id=1, source_target_pairs={{0,128},{8,136},{16,144},{24,152},{32,160},{40,168},{48,176},{56,1... | collective-permute-start | bytes 3080 | tf_op jit(solution)/shard_map/ppermute | solution.py:35
Sparse Core Ops, SparseCore 0:
  16.5 239.7 all-reduce.10
where the time goes:
time: 439 us
  waiting for transfers between devices  242 us (55%)
  blocking collectives  83.8 us (19%)
  other arithmetic  57.7 us (13%)
  starting transfers between devices  25.5 us (6%)
  between operations  14.5 us (3%)
  local copies, waits for them, and re-layouts  12.7 us (3%)
    psum x1, waiting for transfers between devices, shards(): lax.psum((gram_local, proj_local), ('wide', 'slab'))  237 us
    psum x1, blocking collectives, shards(): lax.psum((gram_local, proj_local), ('wide', 'slab'))  73.7 us
    add x4, other arithmetic, march_forward(): centre + STEP_SIZE * (diffuse_subdomain.astype(jnp.float32) * spread - ca...  21.7 us
    ppermute x4, starting transfers between devices, padded(): lax.ppermute(tail, axis, [(i, (i + 1) % count) for i in range(ends)])  13.7 us
    another operation x3, other arithmetic, shards(): lower_factor = jnp.linalg.cholesky(gram_matrix)  13.2 us
    another operation x2, other arithmetic, shards(): lax.linalg.triangular_solve(lower_factor, half_solve, left_side=True, low...  11.9 us
    ppermute x4, starting transfers between devices, padded(): lax.ppermute(head, axis, [((i + 1) % count, i) for i in range(ends)])  10.9 us
    all_gather x1, blocking collectives, shards(): partner_all = lax.all_gather(partner_own, 'slab', axis=1, tiled=True)  10.1 us
  transfers between devices with their start and end apart: 10, of which 3 were waited for; matrix products, arithmetic and copies ran while one was open for 7% of the time, Pallas kernels for 0%

commit v1 on v0

--- a/solution.py
+++ b/solution.py
@@ -33,6 +33,21 @@
     mask = 2**stride
     pairs = [(source, source ^ mask) for source in range(lax.axis_size(axis))]
     return lax.ppermute(value, axis, pairs)
+
+
+def gather_sum(value, axes):
+    count = lax.axis_size(axes)
+    copies = jnp.broadcast_to(value[None], (count, *value.shape))
+    return jnp.sum(lax.all_to_all(copies, axes, 0, 0, tiled=True), axis=0)
+
+
+def sum_everywhere(square):
+    rows = square.shape[0] // lax.axis_size("slab")
+    blocks = square.reshape(-1, rows, square.shape[1])
+    mine = jnp.sum(lax.all_to_all(blocks, "slab", 0, 0, tiled=True), axis=0)
+    mine = gather_sum(mine, "wide")
+    copies = jnp.broadcast_to(mine[None], blocks.shape)
+    return lax.all_to_all(copies, "slab", 0, 0, tiled=True).reshape(square.shape)
 
 
 def surround_wrapper(block_rows, mirror_layer):
@@ -111,7 +126,8 @@
     proj_local = jnp.dot(
         resid, panel, precision=lax.Precision.HIGHEST, preferred_element_type=jnp.float32
     )
-    gram_matrix, projection = lax.psum((gram_local, proj_local), ("wide", "slab"))
+    gram_matrix = sum_everywhere(gram_local)
+    projection = gather_sum(proj_local, ("wide", "slab"))
     lower_factor = jnp.linalg.cholesky(gram_matrix)
     half_solve = lax.linalg.triangular_solve(
         lower_factor, projection[:, None], left_side=True, lower=True

time: 439 us -> 156 us (0.36)
  waiting for transfers between devices: 242 us -> 7.42 us
  blocking collectives: 83.8 us -> 11.7 us
  starting transfers between devices: 25.5 us -> 59.9 us
  between operations: 14.5 us -> 1.12 us
    psum x1 -> x0, waiting for transfers between devices: 237 us -> none  [shards(): lax.psum((gram_local, proj_local), ('wide', 'slab'))]
    psum x1 -> x0, blocking collectives: 73.7 us -> none  [shards(): lax.psum((gram_local, proj_local), ('wide', 'slab'))]
    all_to_all x0 -> x4, starting transfers between devices: none -> 29.8 us  [the longest x2 22.6 us: gather_sum(): return jnp.sum(lax.all_to_all(copies, axes, 0, 0, tiled=True), axis=0)]
    all_to_all x0 -> x4, waiting for transfers between devices: none -> 4.69 us  [the longest x1 4.68 us: sum_everywhere(): lax.all_to_all(copies, 'slab', 0, 0, tiled=True).reshape(square.shape)]
    ppermute x1, starting transfers between devices: 0.88 us -> 5.28 us  [partner(): return lax.ppermute(value, axis, pairs)]
    unnamed x38 -> x49, local copies, waits for them, and re-layouts: 6.89 us -> 8.98 us
  transfers between devices with their start and end apart: 10 -> 13, of which waited for: 3 -> 4; matrix products, arithmetic and copies ran while one was open for 7% -> 30% of each run, Pallas kernels for 0% -> 0%
where the time goes in v1:
time: 156 us
  starting transfers between devices  59.9 us (38%)
  other arithmetic  56.9 us (36%)
  local copies, waits for them, and re-layouts  16.7 us (11%)
  blocking collectives  11.7 us (8%)
  waiting for transfers between devices  7.42 us (5%)
  matrix products  1.95 us (1%)
    all_to_all x2, starting transfers between devices, gather_sum(): return jnp.sum(lax.all_to_all(copies, axes, 0, 0, tiled=True), axis=0)  22.6 us
    add x4, other arithmetic, march_forward(): centre + STEP_SIZE * (diffuse_subdomain.astype(jnp.float32) * spread - ca...  21.2 us
    ppermute x4, starting transfers between devices, padded(): lax.ppermute(tail, axis, [(i, (i + 1) % count) for i in range(ends)])  13.4 us
    another operation x3, other arithmetic, shards(): lower_factor = jnp.linalg.cholesky(gram_matrix)  12.4 us
    all_gather x1, blocking collectives, shards(): partner_all = lax.all_gather(partner_own, 'slab', axis=1, tiled=True)  11.7 us
    ppermute x4, starting transfers between devices, padded(): lax.ppermute(head, axis, [((i + 1) % count, i) for i in range(ends)])  11.4 us
    another operation x2, other arithmetic, shards(): lax.linalg.triangular_solve(lower_factor, half_solve, left_side=True, low...  10.5 us
    concatenate x4, other arithmetic, surround_wrapper(): jnp.concatenate([bottom, block_rows, mirror_layer[:, None, :]], axis=1)  9.12 us
  transfers between devices with their start and end apart: 13, of which 4 were waited for; matrix products, arithmetic and copies ran while one was open for 30% of the time, Pallas kernels for 0%

profile of v1, /device:TPU:1, one launch (start us, length us, event | category | flops | bytes accessed | tf_op | source)
XLA Modules:
  0.0 155.6 jit_solution(3249432732262084621)
XLA Ops:
  1.7 5.1 %collective-permute-start = (f32[1,32,1024]{2,1,0:T(8,128)S(1)}, f32[1,32,1024]{2,1,0:T(8,128)S(1)}, u32[]{:S(2)}, u32[]{:S(2)}) collective-permute-start(f32[1,32,1024]{2,1,0:T(8,128)S(1)} %get-tuple-element.22), channel_id=1, source_target_pairs={{1,0},{2,1},{3,2},{4,3},{5,4},{6,5},{7,6},{9,8},{10,9},{11,10},{12... | collective-permute-start | bytes 393224 | tf_op jit(solution)/shard_map/ppermute | solution.py:25
  6.8 1.9 %collective-permute-start.1 = (f32[1,32,1024]{2,1,0:T(8,128)S(1)}, f32[1,32,1024]{2,1,0:T(8,128)S(1)}, u32[]{:S(2)}, u32[]{:S(2)}) collective-permute-start(f32[1,32,1024]{2,1,0:T(8,128)S(1)} %get-tuple-element.21), channel_id=1, source_target_pairs={{0,1},{1,2},{2,3},{3,4},{4,5},{5,6},{6,7},{8,9},{9,10},{10,11},{11... | collective-permute-start | bytes 393224 | tf_op jit(solution)/shard_map/ppermute | solution.py:23
  9.3 1.3 reduce.12
  11.7 2.3 %pad_maximum_fusion.3 = f32[18,34,1024]{2,1,0:T(8,128)S(1)} fusion(f32[18,1,1024]{2,1,0:T(1,128)S(1)} %broadcast_in_dim.48, f32[1,32,1024]{2,1,0:T(8,128)S(1)} %collective-permute-done, f32[16,32,1024]{2,1,0:T(8,128)} %bitcast.102, f32[1,32,1024]{2,1,0:T(8,128)} %copy-done.15, f32[34]{0:T(128)S(1)} %pad.74.clone), kind=kLoop, calls=%fused_computation.4 | loop fusion | flops 2506752 | bytes 4939912 | tf_op jit(solution)/shard_map/concatenate | solution.py:55
  14.6 7.1 %fusion.2 = f32[16,32,1024]{2,1,0:T(8,128)S(1)} fusion(f32[16,32,1024]{2,1,0:T(8,128)} %bitcast.103, f32[18,34,1024]{2,1,0:T(8,128)S(1)} %pad_maximum_fusion.3, f32[1,32,1024]{2,1,0:T(8,128)} %copy-done.14, f32[1,32,1024]{2,1,0:T(8,128)S(1)} %copy-done.16, f32[18,1,1024]{2,1,0:T(1,128)S(1)} %broadcast_in_dim.48, bf16[1,16,32,1024]{3,2,1,0:T(8,128)(2,1)S(1)} %copy-done.8, ...), kind=kLoop, calls=%fused_computation.35 | loop fusion | flops 18874368 | bytes 11231232 | tf_op jit(solution)/shard_map/add | solution.py:81
  21.7 1.3 copy-done.6
  23.7 2.4 %collective-permute-start.2 = (f32[1,32,1024]{2,1,0:T(8,128)}, f32[1,32,1024]{2,1,0:T(8,128)}, u32[]{:S(2)}, u32[]{:S(2)}) collective-permute-start(f32[1,32,1024]{2,1,0:T(8,128)} %get-tuple-element.20), channel_id=1, source_target_pairs={{1,0},{2,1},{3,2},{4,3},{5,4},{6,5},{7,6},{9,8},{10,9},{11,10},{12... | collective-permute-start | bytes 393224 | tf_op jit(solution)/shard_map/ppermute | solution.py:25
  26.1 3.5 %collective-permute-start.3 = (f32[1,32,1024]{2,1,0:T(8,128)}, f32[1,32,1024]{2,1,0:T(8,128)}, u32[]{:S(2)}, u32[]{:S(2)}) collective-permute-start(f32[1,32,1024]{2,1,0:T(8,128)} %get-tuple-element.19), channel_id=1, source_target_pairs={{0,1},{1,2},{2,3},{3,4},{4,5},{5,6},{6,7},{8,9},{9,10},{10,11},{11... | collective-permute-start | bytes 393224 | tf_op jit(solution)/shard_map/ppermute | solution.py:23
  31.9 2.2 %pad_maximum_fusion.2 = f32[18,34,1024]{2,1,0:T(8,128)S(1)} fusion(f32[18,1,1024]{2,1,0:T(1,128)S(1)} %broadcast_in_dim.48, f32[1,32,1024]{2,1,0:T(8,128)} %collective-permute-done.2, f32[16,32,1024]{2,1,0:T(8,128)} %copy-done.6, f32[1,32,1024]{2,1,0:T(8,128)} %collective-permute-done.3, f32[34]{0:T(128)S(1)} %pad.74.clone), kind=kLoop, calls=%fused_computation.3 | loop fusion | flops 2506752 | bytes 4939912 | tf_op jit(solution)/shard_map/concatenate | solution.py:55
  34.1 4.7 %fusion.5 = f32[16,32,1024]{2,1,0:T(8,128)S(1)} fusion(f32[16,32,1024]{2,1,0:T(8,128)S(1)} %copy-done.7, f32[18,34,1024]{2,1,0:T(8,128)S(1)} %pad_maximum_fusion.2, f32[1,32,1024]{2,1,0:T(8,128)} %collective-permute-done.2, f32[1,32,1024]{2,1,0:T(8,128)} %collective-permute-done.3, f32[18,1,1024]{2,1,0:T(1,128)S(1)} %broadcast_in_dim.48, ...), kind=kLoop, calls=%fused_computation.38 | loop fusion | flops 18874368 | bytes 11231232 | tf_op jit(solution)/shard_map/add | solution.py:81
  38.9 1.3 copy-done.4
  40.9 1.9 %collective-permute-start.4 = (f32[1,32,1024]{2,1,0:T(8,128)}, f32[1,32,1024]{2,1,0:T(8,128)}, u32[]{:S(2)}, u32[]{:S(2)}) collective-permute-start(f32[1,32,1024]{2,1,0:T(8,128)} %get-tuple-element.18), channel_id=1, source_target_pairs={{1,0},{2,1},{3,2},{4,3},{5,4},{6,5},{7,6},{9,8},{10,9},{11,10},{12... | collective-permute-start | bytes 393224 | tf_op jit(solution)/shard_map/ppermute | solution.py:25
  42.8 4.4 %collective-permute-start.5 = (f32[1,32,1024]{2,1,0:T(8,128)}, f32[1,32,1024]{2,1,0:T(8,128)}, u32[]{:S(2)}, u32[]{:S(2)}) collective-permute-start(f32[1,32,1024]{2,1,0:T(8,128)} %get-tuple-element.17), channel_id=1, source_target_pairs={{0,1},{1,2},{2,3},{3,4},{4,5},{5,6},{6,7},{8,9},{9,10},{10,11},{11... | collective-permute-start | bytes 393224 | tf_op jit(solution)/shard_map/ppermute | solution.py:23
  48.1 3.7 %all-to-all-start = ((f32[8,16,128]{2,1,0:T(8,128)}), f32[8,16,128]{2,1,0:T(8,128)S(1)}, u32[]{:S(2)}, u32[]{:S(2)}) async-start(f32[8,16,128]{2,1,0:T(8,128)} %fusion.37), calls=%async_computation | async-start | bytes 131072 | tf_op jit(solution)/shard_map/all_to_all | solution.py:47
  51.8 2.3 %pad_maximum_fusion.1 = f32[18,34,1024]{2,1,0:T(8,128)S(1)} fusion(f32[18,1,1024]{2,1,0:T(1,128)S(1)} %broadcast_in_dim.48, f32[1,32,1024]{2,1,0:T(8,128)} %collective-permute-done.4, f32[16,32,1024]{2,1,0:T(8,128)} %copy-done.4, f32[1,32,1024]{2,1,0:T(8,128)} %collective-permute-done.5, f32[34]{0:T(128)S(1)} %pad.74.clone), kind=kLoop, calls=%fused_computation.2 | loop fusion | flops 2506752 | bytes 4939912 | tf_op jit(solution)/shard_map/concatenate | solution.py:55
  54.4 4.7 %fusion.8 = f32[16,32,1024]{2,1,0:T(8,128)S(1)} fusion(f32[16,32,1024]{2,1,0:T(8,128)S(1)} %copy-done.5, f32[18,34,1024]{2,1,0:T(8,128)S(1)} %pad_maximum_fusion.1, f32[1,32,1024]{2,1,0:T(8,128)} %collective-permute-done.4, f32[1,32,1024]{2,1,0:T(8,128)} %collective-permute-done.5, f32[18,1,1024]{2,1,0:T(1,128)S(1)} %broadcast_in_dim.48, ...), kind=kLoop, calls=%fused_computation.41 | loop fusion | flops 18874368 | bytes 11231232 | tf_op jit(solution)/shard_map/add | solution.py:81
  59.1 1.3 copy-done.2
  61.1 1.9 %collective-permute-start.6 = (f32[1,32,1024]{2,1,0:T(8,128)}, f32[1,32,1024]{2,1,0:T(8,128)}, u32[]{:S(2)}, u32[]{:S(2)}) collective-permute-start(f32[1,32,1024]{2,1,0:T(8,128)} %get-tuple-element.16), channel_id=1, source_target_pairs={{1,0},{2,1},{3,2},{4,3},{5,4},{6,5},{7,6},{9,8},{10,9},{11,10},{12... | collective-permute-start | bytes 393224 | tf_op jit(solution)/shard_map/ppermute | solution.py:25
  63.0 3.6 %collective-permute-start.7 = (f32[1,32,1024]{2,1,0:T(8,128)}, f32[1,32,1024]{2,1,0:T(8,128)}, u32[]{:S(2)}, u32[]{:S(2)}) collective-permute-start(f32[1,32,1024]{2,1,0:T(8,128)} %get-tuple-element.15), channel_id=1, source_target_pairs={{0,1},{1,2},{2,3},{3,4},{4,5},{5,6},{6,7},{8,9},{9,10},{10,11},{11... | collective-permute-start | bytes 393224 | tf_op jit(solution)/shard_map/ppermute | solution.py:23
  68.0 11.3 %all-to-all-start.1 = ((f32[32,16,128]{2,1,0:T(8,128)}), f32[32,16,128]{2,1,0:T(8,128)}, u32[]{:S(2)}, u32[]{:S(2)}) async-start(f32[32,16,128]{2,1,0:T(8,128)} %broadcast_in_dim.51), calls=%async_computation.1 | async-start | bytes 524288 | tf_op jit(solution)/shard_map/all_to_all | solution.py:41
  79.4 2.3 %pad_maximum_fusion = f32[18,34,1024]{2,1,0:T(8,128)S(1)} fusion(f32[18,1,1024]{2,1,0:T(1,128)S(1)} %broadcast_in_dim.48, f32[1,32,1024]{2,1,0:T(8,128)} %collective-permute-done.6, f32[16,32,1024]{2,1,0:T(8,128)} %copy-done.2, f32[1,32,1024]{2,1,0:T(8,128)} %collective-permute-done.7, f32[34]{0:T(128)} %copy-done.20), kind=kLoop, calls=%fused_computation.1 | loop fusion | flops 2506752 | bytes 4939912 | tf_op jit(solution)/shard_map/concatenate | solution.py:55
  81.9 4.7 %fusion.11 = f32[16,32,1024]{2,1,0:T(8,128)S(1)} fusion(f32[16,32,1024]{2,1,0:T(8,128)S(1)} %copy-done.3, f32[18,34,1024]{2,1,0:T(8,128)S(1)} %pad_maximum_fusion, f32[1,32,1024]{2,1,0:T(8,128)} %collective-permute-done.6, f32[1,32,1024]{2,1,0:T(8,128)} %collective-permute-done.7, f32[18,1,1024]{2,1,0:T(1,128)S(1)} %broadcast_in_dim.48, ...), kind=kLoop, calls=%fused_computation.44 | loop fusion | flops 18874368 | bytes 11231232 | tf_op jit(solution)/shard_map/add | solution.py:81
  86.7 1.3 copy-done.12
  88.5 5.3 %collective-permute-start.8 = (f32[1,256]{1,0:T(1,128)S(1)}, f32[1,256]{1,0:T(1,128)S(1)}, u32[]{:S(2)}, u32[]{:S(2)}) collective-permute-start(f32[1,256]{1,0:T(1,128)S(1)} %div.18), channel_id=1, source_target_pairs={{0,128},{8,136},{16,144},{24,152},{32,160},{40,168},{48,176},{56,1... | collective-permute-start | bytes 3080 | tf_op jit(solution)/shard_map/ppermute | solution.py:35
  93.7 1.2 collective-permute-done.8
  95.0 11.7 %all_gather.3 = f32[1,2048]{1,0:T(1,128)S(1)} all-gather(f32[1,256]{1,0:T(1,128)S(1)} %collective-permute-done.8), channel_id=1, replica_groups=mesh['wide'=32,'slab'=8] {'slab'}, dimensions={1}, use_global_device_ids=true | all-gather | bytes 9216 | tf_op jit(solution)/shard_map/all_gather | solution.py:123
  106.6 1.7 %gather_fusion = f32[256]{0:T(256)S(1)} fusion(f32[2048]{0:T(1024)S(1)} %bitcast.101, s32[1024]{0:T(1024)S(1)} %pad_clamp_fusion), kind=kCustom, calls=%fused_computation | custom fusion | bytes 3072 | tf_op jit(solution)/shard_map/jit(_take)/gather | solution.py:124
  110.0 3.4 %all-to-all-start.2 = ((f32[8,16,128]{2,1,0:T(8,128)}), f32[8,16,128]{2,1,0:T(8,128)S(1)}, u32[]{:S(2)}, u32[]{:S(2)}) async-start(f32[8,16,128]{2,1,0:T(8,128)} %broadcast_in_dim.52), calls=%async_computation.2 | async-start | bytes 131072 | tf_op jit(solution)/shard_map/all_to_all | solution.py:50
  113.6 4.7 %all-to-all-done.2 = f32[8,16,128]{2,1,0:T(8,128)S(1)} async-done(((f32[8,16,128]{2,1,0:T(8,128)}), f32[8,16,128]{2,1,0:T(8,128)S(1)}, u32[]{:S(2)}, u32[]{:S(2)}) %all-to-all-start.2) | async-done | bytes 65568 | tf_op jit(solution)/shard_map/all_to_all | solution.py:50
  119.0 11.3 %all-to-all-start.3 = ((f32[256,1,128]{2,1,0:T(1,128)}), f32[256,1,128]{2,1,0:T(1,128)S(1)}, u32[]{:S(2)}, u32[]{:S(2)}) async-start(f32[256,1,128]{2,1,0:T(1,128)} %broadcast_in_dim.54), calls=%async_computation.3 | async-start | bytes 262144 | tf_op jit(solution)/shard_map/all_to_all | solution.py:41
  130.5 11.7 %cholesky.16 = f32[128,128]{1,0:T(8,128)S(1)} custom-call(f32[128,128]{1,0:T(8,128)S(1)} %fusion.45), custom_call_target="Cholesky" | custom-call | tf_op jit(solution)/shard_map/jit(cholesky)/cholesky | solution.py:131
  143.5 9.8 %custom-call.10 = f32[1,128,128]{1,2,0:T(8,128)S(1)} custom-call(f32[1,128,128]{2,1,0:T(8,128)S(1)} %fusion.41), custom_call_target="InvertDiagBlocksLowerTriangular" | custom-call | tf_op jit(solution)/shard_map/triangular_solve | solution.py:135
  (91 shorter events, 16.9 us)
Async XLA Ops:
  0.6 154.2 %copy-start = (f32[1,256,128]{2,1,0:T(8,128)S(1)}, f32[1,256,128]{2,1,0:T(8,128)}, u32[]{:S(2)}) copy-start(f32[1,256,128]{2,1,0:T(8,128)} %param.13) | copy-start | bytes 393220
  1.7 9.3 %collective-permute-start = (f32[1,32,1024]{2,1,0:T(8,128)S(1)}, f32[1,32,1024]{2,1,0:T(8,128)S(1)}, u32[]{:S(2)}, u32[]{:S(2)}) collective-permute-start(f32[1,32,1024]{2,1,0:T(8,128)S(1)} %get-tuple-element.22), channel_id=1, source_target_pairs={{1,0},{2,1},{3,2},{4,3},{5,4},{6,5},{7,6},{9,8},{10,9},{11,10},{12... | collective-permute-start | bytes 393224 | tf_op jit(solution)/shard_map/ppermute | solution.py:25
  6.8 4.2 %collective-permute-start.1 = (f32[1,32,1024]{2,1,0:T(8,128)S(1)}, f32[1,32,1024]{2,1,0:T(8,128)S(1)}, u32[]{:S(2)}, u32[]{:S(2)}) collective-permute-start(f32[1,32,1024]{2,1,0:T(8,128)S(1)} %get-tuple-element.21), channel_id=1, source_target_pairs={{0,1},{1,2},{2,3},{3,4},{4,5},{5,6},{6,7},{8,9},{9,10},{10,11},{11... | collective-permute-start | bytes 393224 | tf_op jit(solution)/shard_map/ppermute | solution.py:23
  11.0 40.8 %copy-start.20 = (f32[34]{0:T(128)}, f32[34]{0:T(128)S(1)}, u32[]{:S(2)}) copy-start(f32[34]{0:T(128)S(1)} %pad.74.clone) | copy-start | bytes 412
  11.7 2.6 %copy-start.1 = (bf16[3,1,16,32,1024]{4,3,2,1,0:T(8,128)(2,1)S(1)}, bf16[3,1,16,32,1024]{4,3,2,1,0:T(8,128)(2,1)}, u32[]{:S(2)}) copy-start(bf16[3,1,16,32,1024]{4,3,2,1,0:T(8,128)(2,1)} %param.9) | copy-start | bytes 9437188
  11.7 2.8 %copy-start.8 = (bf16[1,16,32,1024]{3,2,1,0:T(8,128)(2,1)S(1)}, bf16[1,16,32,1024]{3,2,1,0:T(8,128)(2,1)}, u32[]{:S(2)}) copy-start(bf16[1,16,32,1024]{3,2,1,0:T(8,128)(2,1)} %param.8) | copy-start | bytes 3145732
  11.7 2.8 %copy-start.16 = (f32[1,32,1024]{2,1,0:T(8,128)S(1)}, f32[1,32,1024]{2,1,0:T(8,128)}, u32[]{:S(2)}) copy-start(f32[1,32,1024]{2,1,0:T(8,128)} %copy-done.15) | copy-start | bytes 393220
  14.6 15.1 %copy-start.13 = (f32[1,256,128]{2,1,0:T(8,128)S(1)}, f32[1,256,128]{2,1,0:T(8,128)}, u32[]{:S(2)}) copy-start(f32[1,256,128]{2,1,0:T(8,128)} %param.12) | copy-start | bytes 393220
  21.7 1.3 copy-start.6
  23.7 6.9 %collective-permute-start.2 = (f32[1,32,1024]{2,1,0:T(8,128)}, f32[1,32,1024]{2,1,0:T(8,128)}, u32[]{:S(2)}, u32[]{:S(2)}) collective-permute-start(f32[1,32,1024]{2,1,0:T(8,128)} %get-tuple-element.20), channel_id=1, source_target_pairs={{1,0},{2,1},{3,2},{4,3},{5,4},{6,5},{7,6},{9,8},{10,9},{11,10},{12... | collective-permute-start | bytes 393224 | tf_op jit(solution)/shard_map/ppermute | solution.py:25
  26.1 5.7 %collective-permute-start.3 = (f32[1,32,1024]{2,1,0:T(8,128)}, f32[1,32,1024]{2,1,0:T(8,128)}, u32[]{:S(2)}, u32[]{:S(2)}) collective-permute-start(f32[1,32,1024]{2,1,0:T(8,128)} %get-tuple-element.19), channel_id=1, source_target_pairs={{0,1},{1,2},{2,3},{3,4},{4,5},{5,6},{6,7},{8,9},{9,10},{10,11},{11... | collective-permute-start | bytes 393224 | tf_op jit(solution)/shard_map/ppermute | solution.py:23
  30.4 3.7 %copy-start.7 = (f32[16,32,1024]{2,1,0:T(8,128)S(1)}, f32[16,32,1024]{2,1,0:T(8,128)}, u32[]{:S(2)}) copy-start(f32[16,32,1024]{2,1,0:T(8,128)} %copy-done.6) | copy-start | bytes 6291460
  30.4 3.7 %copy-start.9 = (bf16[1,16,32,1024]{3,2,1,0:T(8,128)(2,1)S(1)}, bf16[1,16,32,1024]{3,2,1,0:T(8,128)(2,1)}, u32[]{:S(2)}) copy-start(bf16[1,16,32,1024]{3,2,1,0:T(8,128)(2,1)} %param.8) | copy-start | bytes 3145732
  34.1 13.1 %copy-start.17 = (f32[1,256,128]{1,2,0:T(8,128)S(1)}, f32[1,256,128]{1,2,0:T(8,128)}, u32[]{:S(2)}) copy-start(f32[1,256,128]{1,2,0:T(8,128)} %copy.21) | copy-start | bytes 393220
  38.8 1.3 copy-start.4
  40.9 10.9 %collective-permute-start.4 = (f32[1,32,1024]{2,1,0:T(8,128)}, f32[1,32,1024]{2,1,0:T(8,128)}, u32[]{:S(2)}, u32[]{:S(2)}) collective-permute-start(f32[1,32,1024]{2,1,0:T(8,128)} %get-tuple-element.18), channel_id=1, source_target_pairs={{1,0},{2,1},{3,2},{4,3},{5,4},{6,5},{7,6},{9,8},{10,9},{11,10},{12... | collective-permute-start | bytes 393224 | tf_op jit(solution)/shard_map/ppermute | solution.py:25
  42.8 9.0 %collective-permute-start.5 = (f32[1,32,1024]{2,1,0:T(8,128)}, f32[1,32,1024]{2,1,0:T(8,128)}, u32[]{:S(2)}, u32[]{:S(2)}) collective-permute-start(f32[1,32,1024]{2,1,0:T(8,128)} %get-tuple-element.17), channel_id=1, source_target_pairs={{0,1},{1,2},{2,3},{3,4},{4,5},{5,6},{6,7},{8,9},{9,10},{10,11},{11... | collective-permute-start | bytes 393224 | tf_op jit(solution)/shard_map/ppermute | solution.py:23
  48.1 19.2 %all-to-all-start = ((f32[8,16,128]{2,1,0:T(8,128)}), f32[8,16,128]{2,1,0:T(8,128)S(1)}, u32[]{:S(2)}, u32[]{:S(2)}) async-start(f32[8,16,128]{2,1,0:T(8,128)} %fusion.37), calls=%async_computation | async-start | bytes 131072 | tf_op jit(solution)/shard_map/all_to_all | solution.py:47
  51.8 2.4 %copy-start.5 = (f32[16,32,1024]{2,1,0:T(8,128)S(1)}, f32[16,32,1024]{2,1,0:T(8,128)}, u32[]{:S(2)}) copy-start(f32[16,32,1024]{2,1,0:T(8,128)} %copy-done.4) | copy-start | bytes 6291460
  51.8 2.6 %copy-start.10 = (bf16[1,16,32,1024]{3,2,1,0:T(8,128)(2,1)S(1)}, bf16[1,16,32,1024]{3,2,1,0:T(8,128)(2,1)}, u32[]{:S(2)}) copy-start(bf16[1,16,32,1024]{3,2,1,0:T(8,128)(2,1)} %param.8) | copy-start | bytes 3145732
  54.4 12.3 %copy-start.18 = (s32[1,256]{1,0:T(1,128)S(1)}, s32[1,256]{1,0:T(1,128)}, u32[]{:S(2)}) copy-start(s32[1,256]{1,0:T(1,128)} %param.11) | copy-start | bytes 3076
  61.1 18.2 %collective-permute-start.6 = (f32[1,32,1024]{2,1,0:T(8,128)}, f32[1,32,1024]{2,1,0:T(8,128)}, u32[]{:S(2)}, u32[]{:S(2)}) collective-permute-start(f32[1,32,1024]{2,1,0:T(8,128)} %get-tuple-element.16), channel_id=1, source_target_pairs={{1,0},{2,1},{3,2},{4,3},{5,4},{6,5},{7,6},{9,8},{10,9},{11,10},{12... | collective-permute-start | bytes 393224 | tf_op jit(solution)/shard_map/ppermute | solution.py:25
  63.0 16.3 %collective-permute-start.7 = (f32[1,32,1024]{2,1,0:T(8,128)}, f32[1,32,1024]{2,1,0:T(8,128)}, u32[]{:S(2)}, u32[]{:S(2)}) collective-permute-start(f32[1,32,1024]{2,1,0:T(8,128)} %get-tuple-element.15), channel_id=1, source_target_pairs={{0,1},{1,2},{2,3},{3,4},{4,5},{5,6},{6,7},{8,9},{9,10},{10,11},{11... | collective-permute-start | bytes 393224 | tf_op jit(solution)/shard_map/ppermute | solution.py:23
  68.0 40.4 %all-to-all-start.1 = ((f32[32,16,128]{2,1,0:T(8,128)}), f32[32,16,128]{2,1,0:T(8,128)}, u32[]{:S(2)}, u32[]{:S(2)}) async-start(f32[32,16,128]{2,1,0:T(8,128)} %broadcast_in_dim.51), calls=%async_computation.1 | async-start | bytes 524288 | tf_op jit(solution)/shard_map/all_to_all | solution.py:41
  79.3 2.4 %copy-start.3 = (f32[16,32,1024]{2,1,0:T(8,128)S(1)}, f32[16,32,1024]{2,1,0:T(8,128)}, u32[]{:S(2)}) copy-start(f32[16,32,1024]{2,1,0:T(8,128)} %copy-done.2) | copy-start | bytes 6291460
  79.4 2.6 %copy-start.11 = (bf16[1,16,32,1024]{3,2,1,0:T(8,128)(2,1)S(1)}, bf16[1,16,32,1024]{3,2,1,0:T(8,128)(2,1)}, u32[]{:S(2)}) copy-start(bf16[1,16,32,1024]{3,2,1,0:T(8,128)(2,1)} %param.8) | copy-start | bytes 3145732
  81.9 11.8 %copy-start.22 = (s32[256,1]{0,1:T(1,128)S(1)}, s32[256,1]{0,1:T(1,128)}, u32[]{:S(2)}) copy-start(s32[256,1]{0,1:T(1,128)} %compare_select_fusion.1) | copy-start | bytes 3076
  81.9 31.5 %copy-start.19 = (s32[1,256]{1,0:T(1,128)S(1)}, s32[1,256]{1,0:T(1,128)}, u32[]{:S(2)}) copy-start(s32[1,256]{1,0:T(1,128)} %param.11) | copy-start | bytes 3076
  81.9 31.5 %copy-start.21 = (f32[1,256]{1,0:T(1,128)S(1)}, f32[1,256]{1,0:T(1,128)}, u32[]{:S(2)}) copy-start(f32[1,256]{1,0:T(1,128)} %param.10) | copy-start | bytes 3076
  88.5 6.5 %collective-permute-start.8 = (f32[1,256]{1,0:T(1,128)S(1)}, f32[1,256]{1,0:T(1,128)S(1)}, u32[]{:S(2)}, u32[]{:S(2)}) collective-permute-start(f32[1,256]{1,0:T(1,128)S(1)} %div.18), channel_id=1, source_target_pairs={{0,128},{8,136},{16,144},{24,152},{32,160},{40,168},{48,176},{56,1... | collective-permute-start | bytes 3080 | tf_op jit(solution)/shard_map/ppermute | solution.py:35
  110.0 8.3 %all-to-all-start.2 = ((f32[8,16,128]{2,1,0:T(8,128)}), f32[8,16,128]{2,1,0:T(8,128)S(1)}, u32[]{:S(2)}, u32[]{:S(2)}) async-start(f32[8,16,128]{2,1,0:T(8,128)} %broadcast_in_dim.52), calls=%async_computation.2 | async-start | bytes 131072 | tf_op jit(solution)/shard_map/all_to_all | solution.py:50
  119.0 35.4 %all-to-all-start.3 = ((f32[256,1,128]{2,1,0:T(1,128)}), f32[256,1,128]{2,1,0:T(1,128)S(1)}, u32[]{:S(2)}, u32[]{:S(2)}) async-start(f32[256,1,128]{2,1,0:T(1,128)} %broadcast_in_dim.54), calls=%async_computation.3 | async-start | bytes 262144 | tf_op jit(solution)/shard_map/all_to_all | solution.py:41
  (4 other events, 4.0 us)

commit v2 on v0

v2 whole, which is shorter than its diff:
```python
import math

import jax
import jax.numpy as jnp
from jax import lax
from jax.experimental import pallas as pl
from jax.experimental.pallas import tpu as pltpu
from jax.sharding import Mesh
from jax.sharding import PartitionSpec as P

INTERFACE_STRIP = 64
SWEEPS = 4
STEP_SIZE = 0.11
HALF = 16
LANES = 128
SUBS = 8
REACH = SWEEPS
COEF_REACH = SWEEPS - 1
FINE = 2
FIELDS = 4
SLOTS = REACH + FINE + FIELDS * COEF_REACH
HIGHEST = lax.Precision.HIGHEST
ANY = pl.BlockSpec(memory_space=pl.ANY)
WHOLE = pl.BlockSpec(memory_space=pltpu.VMEM)


def gather_sum(value, axes):
    count = lax.axis_size(axes)
    copies = jnp.broadcast_to(value[None], (count, *value.shape))
    return jnp.sum(lax.all_to_all(copies, axes, 0, 0, tiled=True), axis=0)


def start_all(copies):
    for copy in copies:
        copy.start()
    return copies


def wait_all(copies):
    for copy in copies:
        copy.wait()


def pack_kernel(
    state, spread, flow, ghost, right_hi, right_lo, left_hi, left_lo, planes, parts, rows, sems
):
    count = state.shape[0]
    started = []
    for side, hi, lo, first, coef_first in (
        (0, right_hi, right_lo, count - REACH, count - COEF_REACH),
        (1, left_hi, left_lo, 0, 0),
    ):
        for part, out in ((0, lo), (1, hi)):
            band = pl.ds(part * HALF, HALF)
            source = [spread.at[pl.ds(coef_first, COEF_REACH), band, :]]
            source += [flow.at[axis, pl.ds(coef_first, COEF_REACH), band, :] for axis in range(3)]
            for field in range(FIELDS):
                slot = REACH + FINE + field * COEF_REACH
                started.append(
                    pltpu.make_async_copy(
                        source[field],
                        out.at[pl.ds(slot, COEF_REACH)],
                        sems.at[side * 8 + part * 4 + field],
                    )
                )
    fetch = [
        pltpu.make_async_copy(state.at[pl.ds(count - REACH, REACH)], planes.at[0], sems.at[16]),
        pltpu.make_async_copy(state.at[pl.ds(0, REACH)], planes.at[1], sems.at[17]),
    ]
    start_all(fetch)
    start_all(started)
    wait_all(fetch)
    for side, fine_first in ((0, REACH - FINE), (1, 0)):
        for part in range(2):
            band = pl.ds(part * HALF, HALF)
            for plane in range(REACH):
                value = planes[side, plane, band, :]
                lead = value.astype(jnp.bfloat16)
                parts[side, part, plane] = lead
                if fine_first <= plane < fine_first + FINE:
                    rest = value - lead.astype(jnp.float32)
                    parts[side, part, REACH + plane - fine_first] = rest.astype(jnp.bfloat16)
    for side, first in ((0, count - COEF_REACH), (1, 0)):
        value = ghost[pl.ds(first, COEF_REACH), :]
        pieces = []
        for _ in range(3):
            lead = value.astype(jnp.bfloat16).astype(jnp.float32)
            pieces.append(lead)
            value = value - lead
        pad = jnp.zeros((HALF - 3 * COEF_REACH, value.shape[1]), jnp.float32)
        rows[side] = jnp.concatenate([*pieces, pad], axis=0).astype(jnp.bfloat16)
    push = []
    for side, hi, lo in ((0, right_hi, right_lo), (1, left_hi, left_lo)):
        for part, out in ((0, lo), (1, hi)):
            push.append(
                pltpu.make_async_copy(
                    parts.at[side, part],
                    out.at[pl.ds(0, REACH + FINE)],
                    sems.at[18 + 2 * side + part],
                )
            )
        push.append(pltpu.make_async_copy(rows.at[side], hi.at[SLOTS], sems.at[22 + side]))
    start_all(push)
    wait_all(push)
    wait_all(started)


def pack(state, spread, flow, ghost):
    depth = state.shape[2]
    upper = jax.ShapeDtypeStruct((SLOTS + 1, HALF, depth), jnp.bfloat16)
    lower = jax.ShapeDtypeStruct((SLOTS, HALF, depth), jnp.bfloat16)
    return pl.pallas_call(
        pack_kernel,
        out_shape=(upper, lower, upper, lower),
        in_specs=[ANY, ANY, ANY, WHOLE],
        out_specs=(ANY,) * 4,
        scratch_shapes=[
            pltpu.VMEM((2, REACH, *state.shape[1:]), jnp.float32),
            pltpu.VMEM((2, 2, REACH + FINE, HALF, depth), jnp.bfloat16),
            pltpu.VMEM((2, HALF, depth), jnp.bfloat16),
            pltpu.SemaphoreType.DMA((24,)),
        ],
        cost_estimate=pl.CostEstimate(flops=2_000_000, bytes_accessed=6_000_000, transcendentals=0),
        name="pack_edges",
    )(state, spread, flow, ghost)


def plane_update(below_x, centre, above_x, coefs, ghost_row, store, tile_count, lane_blocks):
    lane = lax.broadcasted_iota(jnp.int32, (SUBS, LANES), 1)
    sub = lax.broadcasted_iota(jnp.int32, (SUBS, LANES), 0)
    zero = jnp.zeros((SUBS, LANES), jnp.float32)
    kept = {}

    def once(kind, tile, block, make):
        if (kind, tile, block) not in kept:
            kept[kind, tile, block] = make()
        return kept[kind, tile, block]

    def tile_of(tile, block):
        return once("c", tile, block, lambda: centre(tile, block))

    def rolled(tile, block, shift, axis):
        return once(
            (shift, axis), tile, block, lambda: pltpu.roll(tile_of(tile, block), shift, axis)
        )

    for block in range(lane_blocks):
        for tile in range(tile_count):
            here = tile_of(tile, block)
            down = rolled(tile, block, 1, 1)
            carry = rolled(tile, block - 1, 1, 1) if block else zero
            minus_z = jnp.where(lane == 0, carry, down)
            up = rolled(tile, block, LANES - 1, 1)
            last = block + 1 == lane_blocks
            carry = zero if last else rolled(tile, block + 1, LANES - 1, 1)
            plus_z = jnp.where(lane == LANES - 1, carry, up)
            carry = rolled(tile - 1, block, 1, 0) if tile else zero
            minus_y = jnp.where(sub == 0, carry, rolled(tile, block, 1, 0))
            top = tile + 1 == tile_count
            carry = ghost_row(block) if top else rolled(tile + 1, block, SUBS - 1, 0)
            plus_y = jnp.where(sub == SUBS - 1, carry, rolled(tile, block, SUBS - 1, 0))
            plus_x, minus_x = above_x(tile, block), below_x(tile, block)
            rate, flow_x, flow_y, flow_z = (coefs(field, tile, block) for field in range(FIELDS))
            total = ((plus_x + minus_x) + (plus_y + minus_y)) + (plus_z + minus_z) - 6.0 * here
            carried = (
                flow_x * (plus_x - minus_x)
                + flow_y * (plus_y - minus_y)
                + flow_z * (plus_z - minus_z)
            )
            change = rate * total - 0.5 * carried
            store(tile, block, here + STEP_SIZE * change)


def sweep(source, target, coefs, ghost, first, stop, tiles, coef_tile):
    lane_blocks = source.shape[2] // LANES

    def body(plane, carry):
        def tile_at(which):
            return lambda tile, block: source[
                which, pl.ds(tile * SUBS, SUBS), pl.ds(block * LANES, LANES)
            ]

        kept = {}

        def coef(field, tile, block):
            pair = (tile + coef_tile) // 2
            if (field, pair, block) not in kept:
                both = coefs[
                    field, plane - 1, pl.ds(pair * HALF, HALF), pl.ds(block * LANES, LANES)
                ]
                kept[field, pair, block] = both.astype(jnp.float32)
            low = (tile + coef_tile) % 2 * SUBS
            return kept[field, pair, block][low : low + SUBS]

        def ghost_row(block):
            return jnp.broadcast_to(
                ghost[plane, :, pl.ds(block * LANES, LANES)], (SUBS, LANES)
            )

        def store(tile, block, value):
            target[plane, pl.ds(tile * SUBS, SUBS), pl.ds(block * LANES, LANES)] = value

        plane_update(
            tile_at(plane - 1),
            tile_at(plane),
            tile_at(plane + 1),
            coef,
            ghost_row,
            store,
            tiles,
            lane_blocks,
        )
        return carry

    lax.fori_loop(first, stop, body, 0)


def set_ghosts(ghost, from_left, from_right, rows):
    count = rows.shape[0]
    rows3 = rows[...]
    for plane in range(count):
        ghost[REACH + plane] = rows3[plane : plane + 1]
    for first, message in ((REACH - COEF_REACH, from_left), (REACH + count, from_right)):
        value = message[...].astype(jnp.float32)
        for plane in range(COEF_REACH):
            row = value[plane : plane + 1]
            for part in (1, 2):
                at = part * COEF_REACH + plane
                row = row + value[at : at + 1]
            ghost[first + plane] = row


def set_edges(grid, parts, count, first_row, rows):
    for side, first, fine_first in ((0, 0, REACH - FINE), (1, REACH + count, 0)):
        for plane in range(REACH):
            value = parts[side, plane, pl.ds(rows, HALF - rows), :].astype(jnp.float32)
            if fine_first <= plane < fine_first + FINE:
                rest = parts[side, REACH + plane - fine_first, pl.ds(rows, HALF - rows), :]
                value = value + rest.astype(jnp.float32)
            grid[first + plane, pl.ds(first_row, HALF - rows), :] = value


def coefficient_copies(coefs, left, right, part, band, count, sems, at):
    copies = []
    for side, message, first in ((0, left, 0), (1, right, COEF_REACH + count)):
        for field in range(FIELDS):
            copies.append(
                pltpu.make_async_copy(
                    message.at[pl.ds(REACH + FINE + field * COEF_REACH, COEF_REACH)],
                    coefs.at[field, pl.ds(first, COEF_REACH), band, :],
                    sems.at[at + side * FIELDS + field],
                )
            )
    return copies


def face_kernel(
    state, spread, flow, rows, left, right, face, grid, other, coefs, parts, tails, ghost, sems
):
    count, height = state.shape[0], state.shape[1]
    band = pl.ds(height - HALF, HALF)
    inner = pl.ds(COEF_REACH, count)
    copies = [
        pltpu.make_async_copy(
            state.at[:, pl.ds(height - SUBS, SUBS), :], grid.at[pl.ds(REACH, count)], sems.at[0]
        ),
        pltpu.make_async_copy(spread.at[:, band, :], coefs.at[0, inner], sems.at[1]),
        pltpu.make_async_copy(left.at[pl.ds(0, REACH + FINE)], parts.at[0], sems.at[2]),
        pltpu.make_async_copy(right.at[pl.ds(0, REACH + FINE)], parts.at[1], sems.at[3]),
        pltpu.make_async_copy(left.at[SLOTS], tails.at[0], sems.at[4]),
        pltpu.make_async_copy(right.at[SLOTS], tails.at[1], sems.at[5]),
    ]
    for axis in range(3):
        copies.append(
            pltpu.make_async_copy(
                flow.at[axis, :, band, :], coefs.at[1 + axis, inner], sems.at[6 + axis]
            )
        )
    copies += coefficient_copies(coefs, left, right, 1, pl.ds(0, HALF), count, sems, 9)
    start_all(copies)
    wait_all(copies)
    set_ghosts(ghost, tails.at[0], tails.at[1], rows)
    set_edges(grid, parts, count, 0, HALF - SUBS)
    pair = (grid, other)
    for step in range(SWEEPS):
        sweep(
            pair[step % 2],
            pair[(step + 1) % 2],
            coefs,
            ghost,
            step + 1,
            count + 2 * REACH - 1 - step,
            1,
            1,
        )
    last = pair[SWEEPS % 2]
    strips = state.shape[2] // INTERFACE_STRIP
    top = last[pl.ds(REACH, count), SUBS - 1, :]
    strip = lax.broadcasted_iota(jnp.int32, (state.shape[2], strips), 0) // INTERFACE_STRIP
    column = lax.broadcasted_iota(jnp.int32, (state.shape[2], strips), 1)
    member = jnp.where(strip == column, 1.0 / INTERFACE_STRIP, 0.0)
    face[...] = jnp.dot(top, member, precision=HIGHEST, preferred_element_type=jnp.float32)


def interface_face(state, spread, flow, rows, left, right):
    count, _, depth = state.shape
    extended = count + 2 * REACH
    return pl.pallas_call(
        face_kernel,
        out_shape=jax.ShapeDtypeStruct((count, depth // INTERFACE_STRIP), jnp.float32),
        in_specs=[ANY, ANY, ANY, WHOLE, ANY, ANY],
        out_specs=WHOLE,
        scratch_shapes=[
            pltpu.VMEM((extended, SUBS, depth), jnp.float32),
            pltpu.VMEM((extended, SUBS, depth), jnp.float32),
            pltpu.VMEM((FIELDS, extended - 2, HALF, depth), jnp.bfloat16),
            pltpu.VMEM((2, REACH + FINE, HALF, depth), jnp.bfloat16),
            pltpu.VMEM((2, HALF, depth), jnp.bfloat16),
            pltpu.VMEM((extended, 1, depth), jnp.float32),
            pltpu.SemaphoreType.DMA((17,)),
        ],
        cost_estimate=pl.CostEstimate(
            flops=20_000_000, bytes_accessed=6_000_000, transcendentals=0
        ),
        name="interface_face",
    )(state, spread, flow, rows, left, right)


def field_kernel(
    state,
    spread,
    flow,
    rows,
    left_hi,
    left_lo,
    right_hi,
    right_lo,
    out,
    grid,
    other,
    coefs,
    parts,
    tails,
    ghost,
    sems,
):
    count, height = state.shape[0], state.shape[1]
    inner = pl.ds(COEF_REACH, count)
    copies = [
        pltpu.make_async_copy(state, grid.at[pl.ds(REACH, count)], sems.at[0]),
        pltpu.make_async_copy(spread, coefs.at[0, inner], sems.at[1]),
        pltpu.make_async_copy(left_lo.at[pl.ds(0, REACH + FINE)], parts.at[0, 0], sems.at[2]),
        pltpu.make_async_copy(right_lo.at[pl.ds(0, REACH + FINE)], parts.at[0, 1], sems.at[3]),
        pltpu.make_async_copy(left_hi.at[pl.ds(0, REACH + FINE)], parts.at[1, 0], sems.at[4]),
        pltpu.make_async_copy(right_hi.at[pl.ds(0, REACH + FINE)], parts.at[1, 1], sems.at[5]),
        pltpu.make_async_copy(left_hi.at[SLOTS], tails.at[0], sems.at[6]),
        pltpu.make_async_copy(right_hi.at[SLOTS], tails.at[1], sems.at[7]),
    ]
    for axis in range(3):
        copies.append(
            pltpu.make_async_copy(flow.at[axis], coefs.at[1 + axis, inner], sems.at[8 + axis])
        )
    copies += coefficient_copies(coefs, left_lo, right_lo, 0, pl.ds(0, HALF), count, sems, 11)
    copies += coefficient_copies(coefs, left_hi, right_hi, 1, pl.ds(HALF, HALF), count, sems, 19)
    start_all(copies)
    wait_all(copies)
    set_ghosts(ghost, tails.at[0], tails.at[1], rows)
    for part in range(2):
        set_edges(grid, parts.at[part], count, part * HALF, 0)
    pair = (grid, other)
    for step in range(SWEEPS):
        sweep(
            pair[step % 2],
            pair[(step + 1) % 2],
            coefs,
            ghost,
            step + 1,
            count + 2 * REACH - 1 - step,
            height // SUBS,
            0,
        )
    done = pltpu.make_async_copy(pair[SWEEPS % 2].at[pl.ds(REACH, count)], out, sems.at[0])
    done.start()
    done.wait()


def field(state, spread, flow, rows, left_hi, left_lo, right_hi, right_lo):
    count, height, depth = state.shape
    extended = count + 2 * REACH
    return pl.pallas_call(
        field_kernel,
        out_shape=jax.ShapeDtypeStruct(state.shape, jnp.float32),
        in_specs=[ANY, ANY, ANY, WHOLE, ANY, ANY, ANY, ANY],
        out_specs=ANY,
        scratch_shapes=[
            pltpu.VMEM((extended, height, depth), jnp.float32),
            pltpu.VMEM((extended, height, depth), jnp.float32),
            pltpu.VMEM((FIELDS, extended - 2, height, depth), jnp.bfloat16),
            pltpu.VMEM((2, 2, REACH + FINE, HALF, depth), jnp.bfloat16),
            pltpu.VMEM((2, HALF, depth), jnp.bfloat16),
            pltpu.VMEM((extended, 1, depth), jnp.float32),
            pltpu.SemaphoreType.DMA((27,)),
        ],
        compiler_params=pltpu.CompilerParams(vmem_limit_bytes=40 * 2**20),
        cost_estimate=pl.CostEstimate(
            flops=80_000_000, bytes_accessed=30_000_000, transcendentals=0
        ),
        name="field",
    )(state, spread, flow, rows, left_hi, left_lo, right_hi, right_lo)


def tilde_kernel(faces, partner_rows, guess, panel, tilde, projection):
    strips = faces.shape[1]
    wanted = partner_rows[...]
    line = lax.broadcasted_iota(jnp.int32, (faces.shape[0], wanted.shape[1]), 0)
    chosen = jnp.where(line == wanted // strips, 1.0, 0.0)
    picked = lax.dot_general(
        faces[...],
        chosen,
        (((0,), (0,)), ((), ())),
        precision=HIGHEST,
        preferred_element_type=jnp.float32,
    )
    spot = lax.broadcasted_iota(jnp.int32, picked.shape, 0)
    values = jnp.sum(jnp.where(spot == wanted % strips, picked, 0.0), axis=0, keepdims=True)
    tilde[...] = values
    projection[...] = jnp.dot(
        values - guess[...],
        panel[...],
        precision=HIGHEST,
        preferred_element_type=jnp.float32,
    )


def tilde_and_projection(faces, partner_rows, guess, panel):
    return pl.pallas_call(
        tilde_kernel,
        out_shape=(
            jax.ShapeDtypeStruct(guess.shape, jnp.float32),
            jax.ShapeDtypeStruct((1, panel.shape[1]), jnp.float32),
        ),
        in_specs=[WHOLE] * 4,
        out_specs=(WHOLE,) * 2,
        cost_estimate=pl.CostEstimate(flops=9_000_000, bytes_accessed=200_000, transcendentals=0),
        name="tilde",
    )(faces, partner_rows, guess, panel)


def shards(
    thermal_state,
    thermal_spreading_rate,
    flow_speed_vector,
    interface_guess,
    partner_facing_rows,
    mismatch_change_matrix,
    output_change_matrix,
):
    state = thermal_state[0]
    spread = thermal_spreading_rate[0]
    flow = flow_speed_vector[:, 0]
    panel = mismatch_change_matrix[0]
    layers = state.shape[0]
    slabs = lax.axis_size("slab")
    rows = jnp.repeat(interface_guess[0].reshape(layers, -1), INTERFACE_STRIP, axis=1)

    gram_local = lax.dot_general(
        panel,
        panel,
        (((0,), (0,)), ((), ())),
        precision=HIGHEST,
        preferred_element_type=jnp.float32,
    )
    blocks = gram_local.reshape(slabs, -1, gram_local.shape[1])
    gram_rows = jnp.sum(lax.all_to_all(blocks, "slab", 0, 0, tiled=True), axis=0)

    right_hi, right_lo, left_hi, left_lo = pack(state, spread, flow, rows)
    onward = [(i, i + 1) for i in range(slabs - 1)]
    back = [(i + 1, i) for i in range(slabs - 1)]
    from_left_hi = lax.ppermute(right_hi, "slab", onward)
    from_right_hi = lax.ppermute(left_hi, "slab", back)
    from_left_lo = lax.ppermute(right_lo, "slab", onward)
    from_right_lo = lax.ppermute(left_lo, "slab", back)
    face = interface_face(state, spread, flow, rows, from_left_hi, from_right_hi)

    both = 2 * slabs
    faces = lax.all_to_all(
        jnp.broadcast_to(face[None], (both, *face.shape)), ("half", "slab"), 0, 0, tiled=True
    )
    other = slabs * (1 - lax.axis_index("half"))
    faces = lax.dynamic_slice_in_dim(faces, other, slabs, axis=0).reshape(-1, face.shape[1])
    tilde, proj_local = tilde_and_projection(faces, partner_facing_rows, interface_guess, panel)

    gram_rows = gather_sum(gram_rows, ("half", "pair"))
    copies = jnp.broadcast_to(gram_rows[None], blocks.shape)
    gram_matrix = lax.all_to_all(copies, "slab", 0, 0, tiled=True).reshape(gram_local.shape)
    projection = gather_sum(proj_local[0], ("half", "pair", "slab"))
    temperature = field(
        state, spread, flow, rows, from_left_hi, from_left_lo, from_right_hi, from_right_lo
    )

    lower_factor = jnp.linalg.cholesky(gram_matrix)
    half_solve = lax.linalg.triangular_solve(
        lower_factor, projection[:, None], left_side=True, lower=True
    )
    coefficients = -lax.linalg.triangular_solve(
        lower_factor, half_solve, left_side=True, lower=True, transpose_a=True
    )[:, 0]
    update = jnp.dot(
        output_change_matrix[0],
        coefficients,
        precision=HIGHEST,
        preferred_element_type=jnp.float32,
    )
    total_rows = (
        interface_guess.shape[1] * slabs * lax.axis_size("half") * lax.axis_size("pair")
    )
    scaled = lax.linalg.triangular_solve(
        lower_factor, panel, left_side=False, lower=True, transpose_a=True
    )
    return (
        temperature[None],
        tilde + update[None],
        (math.sqrt(total_rows) * scaled)[None],
    )


def solution(mesh):
    wide, slab = mesh.shape["wide"], mesh.shape["slab"]
    fine = Mesh(mesh.devices.reshape(2, wide // 2, slab), ("half", "pair", "slab"))
    parts = ("half", "pair")
    return jax.shard_map(
        shards,
        mesh=fine,
        in_specs=(
            P(parts, "slab", None, None),
            P(parts, "slab", None, None),
            P(None, parts, "slab", None, None),
            P(parts, "slab"),
            P(parts, "slab"),
            P(parts, "slab", None),
            P(parts, "slab", None),
        ),
        out_specs=(P(parts, "slab", None, None), P(parts, "slab"), P(parts, "slab", None)),
        check_vma=False,
    )
```

time: 439 us -> 183 us (0.42)
  waiting for transfers between devices: 242 us -> 1.4 us
  Pallas kernels: 0 us -> 78.3 us
  blocking collectives: 83.8 us -> 22.8 us
  other arithmetic: 57.7 us -> 25.1 us
  starting transfers between devices: 25.5 us -> 39.5 us
  between operations: 14.5 us -> 0.87 us
    psum x1 -> x0, waiting for transfers between devices: 237 us -> none  [shards(): lax.psum((gram_local, proj_local), ('wide', 'slab'))]
    pallas_call x0 -> x4, Pallas kernels: none -> 78.3 us  [the longest x1 49.8 us: pack(): pl.pallas_call(pack_kernel, out_shape=(upper, lower, upper, lower), in_sp...]
    psum x1 -> x0, blocking collectives: 73.7 us -> none  [shards(): lax.psum((gram_local, proj_local), ('wide', 'slab'))]
    all_to_all x0 -> x4, starting transfers between devices: none -> 26.8 us  [the longest x1 11.1 us: gather_sum(): return jnp.sum(lax.all_to_all(copies, axes, 0, 0, tiled=True), axis=0)]
    all_to_all x0 -> x1, blocking collectives: none -> 22.8 us  [gather_sum(): return jnp.sum(lax.all_to_all(copies, axes, 0, 0, tiled=True), axis=0)]
    add x5 -> x0, other arithmetic: 22.3 us -> none  [the longest x4 21.7 us: march_forward(): centre + STEP_SIZE * (diffuse_subdomain.astype(jnp.float32) * spread - ca...]
    ppermute x9 -> x4, starting transfers between devices: 25.5 us -> 12.7 us  [the longest x1 4.51 us: shards(): from_left_hi = lax.ppermute(right_hi, 'slab', onward)]
    all_gather x1 -> x0, blocking collectives: 10.1 us -> none  [shards(): partner_all = lax.all_gather(partner_own, 'slab', axis=1, tiled=True)]
  transfers between devices with their start and end apart: 10 -> 8, of which waited for: 3 -> 1; matrix products, arithmetic and copies ran while one was open for 7% -> 16% of each run, Pallas kernels for 0% -> 14%
where the time goes in v2:
time: 183 us; the launch traced here: 182 us
  Pallas kernels  78.3 us (43%)
  starting transfers between devices  39.5 us (22%)
  other arithmetic  25.1 us (14%)
  blocking collectives  22.8 us (12%)
  local copies, waits for them, and re-layouts  11.5 us (6%)
  matrix products  3.07 us (2%)
    pallas_call x1, Pallas kernels, pack(): pl.pallas_call(pack_kernel, out_shape=(upper, lower, upper, lower), in_sp...  49.8 us
    all_to_all x1, blocking collectives, gather_sum(): return jnp.sum(lax.all_to_all(copies, axes, 0, 0, tiled=True), axis=0)  22.8 us
    pallas_call x1, Pallas kernels, field(): pl.pallas_call(field_kernel, out_shape=jax.ShapeDtypeStruct(state.shape,...  15.1 us
    another operation x3, other arithmetic, shards(): lower_factor = jnp.linalg.cholesky(gram_matrix)  12.5 us
    pallas_call x1, Pallas kernels, interface_face(): pl.pallas_call(face_kernel, out_shape=jax.ShapeDtypeStruct((count, depth...  11.3 us
    all_to_all x1, starting transfers between devices, gather_sum(): return jnp.sum(lax.all_to_all(copies, axes, 0, 0, tiled=True), axis=0)  11.1 us
    another operation x2, other arithmetic, shards(): lax.linalg.triangular_solve(lower_factor, half_solve, left_side=True, low...  10.5 us
    all_to_all x1, starting transfers between devices, shards(): lax.all_to_all(copies, 'slab', 0, 0, tiled=True).reshape(gram_local.shape)  5.93 us
  transfers between devices with their start and end apart: 8, of which 1 were waited for; matrix products, arithmetic and copies ran while one was open for 16% of the time, Pallas kernels for 14%

profile of v2, /device:TPU:1, one launch (start us, length us, event | category | flops | bytes accessed | tf_op | source)
XLA Modules:
  0.0 182.5 jit_solution(15255565940558641846)
XLA Ops:
  0.6 0.5 broadcast.83
  1.2 1.3 reduce.10
  2.7 0.7 reshape.47.ghost.rows
  3.4 49.8 %pack_edges.1 = (bf16[19,16,1024]{2,1,0:T(8,128)(2,1)}, bf16[18,16,1024]{2,1,0:T(8,128)(2,1)}, bf16[19,16,1024]{2,1,0:T(8,128)(2,1)}, bf16[18,16,1024]{2,1,0:T(8,128)(2,1)}) custom-call(f32[16,32,1024]{2,1,0:T(8,128)} %bitcast.59, bf16[16,32,1024]{2,1,0:T(8,128)(2,1)} %bitcast.62, bf16[3,16,32,1024]{3,2,1,0:T(8,128)(2,1)} %bitcast.56, ...), custom_call_target="tpu_custom_call" | custom-call | flops 2000000 | bytes 6000000 | tf_op jit(solution)/shard_map/pack_edges/pallas_call | solution.py:112
  53.2 4.5 %collective-permute-start = (bf16[19,16,1024]{2,1,0:T(8,128)(2,1)}, bf16[19,16,1024]{2,1,0:T(8,128)(2,1)}, u32[]{:S(2)}, u32[]{:S(2)}) collective-permute-start(bf16[19,16,1024]{2,1,0:T(8,128)(2,1)} %get-tuple-element.9), channel_id=1, source_target_pairs={{0,1},{1,2},{2,3},{3,4},{4,5},{5,6},{6,7},{8,9},{9,10},{10,11},{11... | collective-permute-start | bytes 1867784 | tf_op jit(solution)/shard_map/ppermute | solution.py:479
  57.8 2.7 %collective-permute-start.2 = (bf16[19,16,1024]{2,1,0:T(8,128)(2,1)}, bf16[19,16,1024]{2,1,0:T(8,128)(2,1)}, u32[]{:S(2)}, u32[]{:S(2)}) collective-permute-start(bf16[19,16,1024]{2,1,0:T(8,128)(2,1)} %get-tuple-element.11), channel_id=1, source_target_pairs={{1,0},{2,1},{3,2},{4,3},{5,4},{6,5},{7,6},{9,8},{10,9},{11,10},{12... | collective-permute-start | bytes 1867784 | tf_op jit(solution)/shard_map/ppermute | solution.py:480
  60.6 0.9 fusion.4
  61.5 4.1 %all-to-all-start.1 = ((f32[8,16,128]{2,1,0:T(8,128)}), f32[8,16,128]{2,1,0:T(8,128)S(1)}, u32[]{:S(2)}, u32[]{:S(2)}) async-start(f32[8,16,128]{2,1,0:T(8,128)} %fusion.4), calls=%async_computation.1 | async-start | bytes 131072 | tf_op jit(solution)/shard_map/all_to_all | solution.py:474
  65.6 3.5 %collective-permute-start.1 = (bf16[18,16,1024]{2,1,0:T(8,128)(2,1)}, bf16[18,16,1024]{2,1,0:T(8,128)(2,1)}, u32[]{:S(2)}, u32[]{:S(2)}) collective-permute-start(bf16[18,16,1024]{2,1,0:T(8,128)(2,1)} %get-tuple-element.10), channel_id=1, source_target_pairs={{0,1},{1,2},{2,3},{3,4},{4,5},{5,6},{6,7},{8,9},{9,10},{10,11},{11... | collective-permute-start | bytes 1769480 | tf_op jit(solution)/shard_map/ppermute | solution.py:481
  69.2 1.9 %collective-permute-start.3 = (bf16[18,16,1024]{2,1,0:T(8,128)(2,1)}, bf16[18,16,1024]{2,1,0:T(8,128)(2,1)}, u32[]{:S(2)}, u32[]{:S(2)}) collective-permute-start(bf16[18,16,1024]{2,1,0:T(8,128)(2,1)} %get-tuple-element.12), channel_id=1, source_target_pairs={{1,0},{2,1},{3,2},{4,3},{5,4},{6,5},{7,6},{9,8},{10,9},{11,10},{12... | collective-permute-start | bytes 1769480 | tf_op jit(solution)/shard_map/ppermute | solution.py:482
  71.2 22.8 %all_to_all.26 = f32[32,16,128]{2,1,0:T(8,128)S(1)} all-to-all(f32[32,16,128]{2,1,0:T(8,128)S(1)} %broadcast_in_dim.21), channel_id=1, replica_groups=mesh['half'=2,'pair'=16,'slab'=8] {'half','pair'}, dimensions={0} | all-to-all | bytes 524288 | tf_op jit(solution)/shard_map/all_to_all | solution.py:30
  94.0 0.6 broadcast_in_dim.42
  94.7 5.9 %all-to-all-start.3 = ((f32[8,16,128]{2,1,0:T(8,128)}), f32[8,16,128]{2,1,0:T(8,128)S(1)}, u32[]{:S(2)}, u32[]{:S(2)}) async-start(f32[8,16,128]{2,1,0:T(8,128)} %broadcast_in_dim.42), calls=%async_computation.3 | async-start | bytes 131072 | tf_op jit(solution)/shard_map/all_to_all | solution.py:495
  100.6 11.3 %interface_face.1 = f32[16,16]{1,0:T(8,128)} custom-call(f32[16,32,1024]{2,1,0:T(8,128)} %bitcast.60, bf16[16,32,1024]{2,1,0:T(8,128)(2,1)} %bitcast.63, bf16[3,16,32,1024]{3,2,1,0:T(8,128)(2,1)} %bitcast.57, f32[16,1024]{1,0:T(8,128)} %reshape.47.ghost.rows, bf16[19,16,1024]{2,1,0:T(8,128)(2,1)} %collective-permute-done.left_hi.left, ...), custom_call_target="tpu_custom_call" | custom-call | flops 20000000 | bytes 6000000 | tf_op jit(solution)/shard_map/interface_face/pallas_call | solution.py:308
  111.9 1.4 broadcast_in_dim.20
  113.3 1.6 reshape.66
  115.0 1.6 copy-done.2
  116.6 1.2 copy-done.3
  117.8 15.1 %field.1 = f32[16,32,1024]{2,1,0:T(8,128)} custom-call(f32[16,32,1024]{2,1,0:T(8,128)S(1)} %bitcast.61, bf16[16,32,1024]{2,1,0:T(8,128)(2,1)S(1)} %bitcast.64, bf16[3,16,32,1024]{3,2,1,0:T(8,128)(2,1)S(1)} %bitcast.58, f32[16,1024]{1,0:T(8,128)S(1)} %copy-done.4, bf16[19,16,1024]{2,1,0:T(8,128)(2,1)} %collective-permute-done.left_hi.left, ...), custom_call_target="tpu_custom_call" | custom-call | flops 80000000 | bytes 30000000 | tf_op jit(solution)/shard_map/field/pallas_call | solution.py:390
  132.9 5.6 %all-to-all-start = ((f32[16,1,256]{2,1,0:T(1,128)}), f32[16,1,256]{2,1,0:T(1,128)S(1)}, u32[]{:S(2)}, u32[]{:S(2)}) async-start(f32[16,1,256]{2,1,0:T(1,128)} %reshape.66), calls=%async_computation | async-start | bytes 32768 | tf_op jit(solution)/shard_map/all_to_all | solution.py:486
  138.7 11.7 %cholesky.16 = f32[128,128]{1,0:T(8,128)S(1)} custom-call(f32[128,128]{1,0:T(8,128)S(1)} %fusion.10), custom_call_target="Cholesky" | custom-call | tf_op jit(solution)/shard_map/jit(cholesky)/cholesky | solution.py:501
  150.4 0.7 compare_reduce_fusion
  151.6 0.7 reduce.11
  152.4 0.6 constant_dynamic-slice_fusion
  153.1 2.0 %tilde.1 = (f32[1,256]{1,0:T(1,128)}, f32[1,128]{1,0:T(1,128)}) custom-call(f32[128,16]{1,0:T(8,128)} %bitcast.71, s32[1,256]{1,0:T(1,128)} %partner_rows.1, f32[1,256]{1,0:T(1,128)} %guess.1, f32[256,128]{1,0:T(8,128)} %bitcast.65), custom_call_target="tpu_custom_call" | custom-call | flops 9000000 | bytes 200000 | tf_op jit(solution)/shard_map/tilde/pallas_call | solution.py:436
  155.1 1.4 broadcast_in_dim.43
  156.5 11.1 %all-to-all-start.4 = ((f32[256,1,128]{2,1,0:T(1,128)}), f32[256,1,128]{2,1,0:T(1,128)S(1)}, u32[]{:S(2)}, u32[]{:S(2)}) async-start(f32[256,1,128]{2,1,0:T(1,128)} %broadcast_in_dim.43), calls=%async_computation.4 | async-start | bytes 262144 | tf_op jit(solution)/shard_map/all_to_all | solution.py:30
  167.6 0.7 fusion.6
  168.3 9.8 %custom-call.10 = f32[1,128,128]{1,2,0:T(8,128)S(1)} custom-call(f32[1,128,128]{2,1,0:T(8,128)S(1)} %fusion.6), custom_call_target="InvertDiagBlocksLowerTriangular" | custom-call | tf_op jit(solution)/shard_map/triangular_solve | solution.py:505
  178.4 0.8 copy.22
  179.2 1.4 all-to-all-done.4
  181.0 1.5 convolution_add_fusion
  (34 shorter events, 1.8 us)
Async XLA Ops:
  0.6 180.3 %copy-start = (f32[1,256,128]{2,1,0:T(8,128)S(1)}, f32[1,256,128]{2,1,0:T(8,128)}, u32[]{:S(2)}) copy-start(f32[1,256,128]{2,1,0:T(8,128)} %param.13) | copy-start | bytes 393220
  3.4 57.1 %copy-start.5 = (f32[1,256,128]{2,1,0:T(8,128)S(1)}, f32[1,256,128]{2,1,0:T(8,128)}, u32[]{:S(2)}) copy-start(f32[1,256,128]{2,1,0:T(8,128)} %param.12) | copy-start | bytes 393220
  53.2 47.4 %collective-permute-start = (bf16[19,16,1024]{2,1,0:T(8,128)(2,1)}, bf16[19,16,1024]{2,1,0:T(8,128)(2,1)}, u32[]{:S(2)}, u32[]{:S(2)}) collective-permute-start(bf16[19,16,1024]{2,1,0:T(8,128)(2,1)} %get-tuple-element.9), channel_id=1, source_target_pairs={{0,1},{1,2},{2,3},{3,4},{4,5},{5,6},{6,7},{8,9},{9,10},{10,11},{11... | collective-permute-start | bytes 1867784 | tf_op jit(solution)/shard_map/ppermute | solution.py:479
  57.8 42.9 %collective-permute-start.2 = (bf16[19,16,1024]{2,1,0:T(8,128)(2,1)}, bf16[19,16,1024]{2,1,0:T(8,128)(2,1)}, u32[]{:S(2)}, u32[]{:S(2)}) collective-permute-start(bf16[19,16,1024]{2,1,0:T(8,128)(2,1)} %get-tuple-element.11), channel_id=1, source_target_pairs={{1,0},{2,1},{3,2},{4,3},{5,4},{6,5},{7,6},{9,8},{10,9},{11,10},{12... | collective-permute-start | bytes 1867784 | tf_op jit(solution)/shard_map/ppermute | solution.py:480
  61.5 9.6 %all-to-all-start.1 = ((f32[8,16,128]{2,1,0:T(8,128)}), f32[8,16,128]{2,1,0:T(8,128)S(1)}, u32[]{:S(2)}, u32[]{:S(2)}) async-start(f32[8,16,128]{2,1,0:T(8,128)} %fusion.4), calls=%async_computation.1 | async-start | bytes 131072 | tf_op jit(solution)/shard_map/all_to_all | solution.py:474
  65.6 49.3 %collective-permute-start.1 = (bf16[18,16,1024]{2,1,0:T(8,128)(2,1)}, bf16[18,16,1024]{2,1,0:T(8,128)(2,1)}, u32[]{:S(2)}, u32[]{:S(2)}) collective-permute-start(bf16[18,16,1024]{2,1,0:T(8,128)(2,1)} %get-tuple-element.10), channel_id=1, source_target_pairs={{0,1},{1,2},{2,3},{3,4},{4,5},{5,6},{6,7},{8,9},{9,10},{10,11},{11... | collective-permute-start | bytes 1769480 | tf_op jit(solution)/shard_map/ppermute | solution.py:481
  69.2 45.8 %collective-permute-start.3 = (bf16[18,16,1024]{2,1,0:T(8,128)(2,1)}, bf16[18,16,1024]{2,1,0:T(8,128)(2,1)}, u32[]{:S(2)}, u32[]{:S(2)}) collective-permute-start(bf16[18,16,1024]{2,1,0:T(8,128)(2,1)} %get-tuple-element.12), channel_id=1, source_target_pairs={{1,0},{2,1},{3,2},{4,3},{5,4},{6,5},{7,6},{9,8},{10,9},{11,10},{12... | collective-permute-start | bytes 1769480 | tf_op jit(solution)/shard_map/ppermute | solution.py:482
  94.7 38.2 %all-to-all-start.3 = ((f32[8,16,128]{2,1,0:T(8,128)}), f32[8,16,128]{2,1,0:T(8,128)S(1)}, u32[]{:S(2)}, u32[]{:S(2)}) async-start(f32[8,16,128]{2,1,0:T(8,128)} %broadcast_in_dim.42), calls=%async_computation.3 | async-start | bytes 131072 | tf_op jit(solution)/shard_map/all_to_all | solution.py:495
  100.6 14.4 %copy-start.1 = (bf16[3,1,16,32,1024]{4,3,2,1,0:T(8,128)(2,1)S(1)}, bf16[3,1,16,32,1024]{4,3,2,1,0:T(8,128)(2,1)}, u32[]{:S(2)}) copy-start(bf16[3,1,16,32,1024]{4,3,2,1,0:T(8,128)(2,1)} %param.9) | copy-start | bytes 9437188
  100.6 14.4 %copy-start.4 = (f32[16,1024]{1,0:T(8,128)S(1)}, f32[16,1024]{1,0:T(8,128)}, u32[]{:S(2)}) copy-start(f32[16,1024]{1,0:T(8,128)} %reshape.47.ghost.rows) | copy-start | bytes 196612
  113.3 64.8 %copy-start.6 = (f32[1,256,128]{2,1,0:T(8,128)S(1)}, f32[1,256,128]{2,1,0:T(8,128)}, u32[]{:S(2)}) copy-start(f32[1,256,128]{2,1,0:T(8,128)} %param.12) | copy-start | bytes 393220
  115.0 1.6 copy-start.2
  116.6 1.2 copy-start.3
  132.9 18.2 %all-to-all-start = ((f32[16,1,256]{2,1,0:T(1,128)}), f32[16,1,256]{2,1,0:T(1,128)S(1)}, u32[]{:S(2)}, u32[]{:S(2)}) async-start(f32[16,1,256]{2,1,0:T(1,128)} %reshape.66), calls=%async_computation | async-start | bytes 32768 | tf_op jit(solution)/shard_map/all_to_all | solution.py:486
  156.5 24.1 %all-to-all-start.4 = ((f32[256,1,128]{2,1,0:T(1,128)}), f32[256,1,128]{2,1,0:T(1,128)S(1)}, u32[]{:S(2)}, u32[]{:S(2)}) async-start(f32[256,1,128]{2,1,0:T(1,128)} %broadcast_in_dim.43), calls=%async_computation.4 | async-start | bytes 262144 | tf_op jit(solution)/shard_map/all_to_all | solution.py:30

commit v3 on v2

v3 whole, which is shorter than its diff:
```python
import functools
import math

import jax
import jax.numpy as jnp
from jax import lax
from jax.experimental import pallas as pl
from jax.experimental.pallas import tpu as pltpu
from jax.sharding import Mesh
from jax.sharding import PartitionSpec as P

INTERFACE_STRIP = 64
SWEEPS = 4
STEP_SIZE = 0.11
HALF = 16
LANES = 128
SUBS = 8
REACH = SWEEPS
COEF_REACH = SWEEPS - 1
FINE = 2
FIELDS = 4
SLOTS = REACH + FINE + FIELDS * COEF_REACH
HIGHEST = lax.Precision.HIGHEST
ANY = pl.BlockSpec(memory_space=pl.ANY)
WHOLE = pl.BlockSpec(memory_space=pltpu.VMEM)
SMALL = pltpu.CompilerParams(vmem_limit_bytes=8 * 2**20)
SCALARS = pl.BlockSpec(memory_space=pltpu.SMEM)


def start_all(copies):
    for copy in copies:
        copy.start()


def wait_all(copies):
    for copy in copies:
        copy.wait()


def ghost_line(guess, first, block):
    lane = lax.broadcasted_iota(jnp.int32, (1, LANES), 1)
    strips = LANES // INTERFACE_STRIP
    at = first + block * strips
    row = jnp.full((1, LANES), guess[0, at], jnp.float32)
    for strip in range(1, strips):
        row = jnp.where(lane < strip * INTERFACE_STRIP, row, guess[0, at + strip])
    return row


def pack_kernel(state, spread, flow, guess, right_hi, right_lo, left_hi, left_lo, planes, sems):
    count = state.shape[0]
    lane_blocks = state.shape[2] // LANES
    per_plane = guess.shape[1] // count
    fetch = [
        pltpu.make_async_copy(state.at[pl.ds(count - REACH, REACH)], planes.at[0], sems.at[16]),
        pltpu.make_async_copy(state.at[pl.ds(0, REACH)], planes.at[1], sems.at[17]),
    ]
    started = []
    for side, hi, lo, coef_first in (
        (0, right_hi, right_lo, count - COEF_REACH),
        (1, left_hi, left_lo, 0),
    ):
        for part, out in ((1, hi), (0, lo)):
            band = pl.ds(part * HALF, HALF)
            source = [spread.at[pl.ds(coef_first, COEF_REACH), band, :]]
            source += [flow.at[axis, pl.ds(coef_first, COEF_REACH), band, :] for axis in range(3)]
            for field in range(FIELDS):
                slot = REACH + FINE + field * COEF_REACH
                started.append(
                    pltpu.make_async_copy(
                        source[field],
                        out.at[pl.ds(slot, COEF_REACH)],
                        sems.at[side * 8 + part * 4 + field],
                    )
                )
    start_all(fetch)
    start_all(started)
    for side, out, first in ((0, right_hi, count - COEF_REACH), (1, left_hi, 0)):
        for block in range(lane_blocks):
            lines = [
                ghost_line(guess, (first + plane) * per_plane, block)
                for plane in range(COEF_REACH)
            ]
            pieces = []
            for _ in range(3):
                leads = [line.astype(jnp.bfloat16).astype(jnp.float32) for line in lines]
                lines = [line - lead for line, lead in zip(lines, leads)]
                pieces += leads
            pad = jnp.zeros((HALF - 3 * COEF_REACH, LANES), jnp.float32)
            whole = jnp.concatenate([*pieces, pad], axis=0).astype(jnp.bfloat16)
            out[SLOTS, :, pl.ds(block * LANES, LANES)] = whole
    wait_all(fetch)
    for side, outs, fine_first in (
        (0, (right_lo, right_hi), REACH - FINE),
        (1, (left_lo, left_hi), 0),
    ):
        for part, out in enumerate(outs):
            for plane in range(REACH):
                value = planes[side, plane, pl.ds(part * HALF, HALF), :]
                lead = value.astype(jnp.bfloat16)
                out[plane] = lead
                if fine_first <= plane < fine_first + FINE:
                    rest = value - lead.astype(jnp.float32)
                    out[REACH + plane - fine_first] = rest.astype(jnp.bfloat16)
    wait_all(started)


def pack(state, spread, flow, guess):
    depth = state.shape[2]
    upper = jax.ShapeDtypeStruct((SLOTS + 1, HALF, depth), jnp.bfloat16)
    lower = jax.ShapeDtypeStruct((SLOTS, HALF, depth), jnp.bfloat16)
    return pl.pallas_call(
        pack_kernel,
        out_shape=(upper, lower, upper, lower),
        in_specs=[ANY, ANY, ANY, SCALARS],
        out_specs=(WHOLE,) * 4,
        scratch_shapes=[
            pltpu.VMEM((2, REACH, *state.shape[1:]), jnp.float32),
            pltpu.SemaphoreType.DMA((18,)),
        ],
        cost_estimate=pl.CostEstimate(flops=2_000_000, bytes_accessed=6_000_000, transcendentals=0),
        compiler_params=pltpu.CompilerParams(vmem_limit_bytes=16 * 2**20),
        name="pack_edges",
    )(state, spread, flow, guess)


def weights_of(rate, flow_x, flow_y, flow_z):
    rate = STEP_SIZE * rate
    flow_x, flow_y, flow_z = (0.5 * STEP_SIZE * flow for flow in (flow_x, flow_y, flow_z))
    return (
        rate + flow_x,
        rate - flow_x,
        rate + flow_y,
        rate - flow_y,
        rate + flow_z,
        rate - flow_z,
        1.0 - 6.0 * rate,
    )


def plane_update(below_x, centre, above_x, weights, ghost_row, store, tile_count, lane_blocks):
    lane = lax.broadcasted_iota(jnp.int32, (SUBS, LANES), 1)
    sub = lax.broadcasted_iota(jnp.int32, (SUBS, LANES), 0)
    zero = jnp.zeros((SUBS, LANES), jnp.float32)
    kept = {}

    def rolled(tile, block, shift, axis):
        key = (tile, block, shift, axis)
        if key not in kept:
            kept[key] = pltpu.roll(centre(tile, block), shift, axis)
        return kept[key]

    for block in range(lane_blocks):
        for tile in range(tile_count):
            carry = rolled(tile, block - 1, 1, 1) if block else zero
            minus_z = jnp.where(lane == 0, carry, rolled(tile, block, 1, 1))
            last = block + 1 == lane_blocks
            carry = zero if last else rolled(tile, block + 1, LANES - 1, 1)
            plus_z = jnp.where(lane == LANES - 1, carry, rolled(tile, block, LANES - 1, 1))
            carry = rolled(tile - 1, block, 1, 0) if tile else zero
            minus_y = jnp.where(sub == 0, carry, rolled(tile, block, 1, 0))
            top = tile + 1 == tile_count
            carry = ghost_row(block) if top else rolled(tile + 1, block, SUBS - 1, 0)
            plus_y = jnp.where(sub == SUBS - 1, carry, rolled(tile, block, SUBS - 1, 0))
            weight = weights(tile, block)
            minus_x, plus_x, here = below_x(tile, block), above_x(tile, block), centre(tile, block)
            if len(weight) == FIELDS:
                rate, flow_x, flow_y, flow_z = weight
                total = ((plus_x + minus_x) + (plus_y + minus_y)) + (plus_z + minus_z)
                carried = (
                    flow_x * (plus_x - minus_x)
                    + flow_y * (plus_y - minus_y)
                    + flow_z * (plus_z - minus_z)
                )
                change = rate * (total - 6.0 * here) - 0.5 * carried
                store(tile, block, here + STEP_SIZE * change)
                continue
            total_x = weight[0] * minus_x + weight[1] * plus_x
            total_y = weight[2] * minus_y + weight[3] * plus_y
            total_z = weight[4] * minus_z + weight[5] * plus_z
            store(tile, block, (total_x + total_y) + (total_z + weight[6] * here))


def sweep(source, target, coefs, held, ghost, first, stop, tiles, coef_tile, unroll):
    lane_blocks = source.shape[2] // LANES

    def one(plane):
        def tile_at(which):
            loaded = {}

            def load(tile, block):
                if (tile, block) not in loaded:
                    loaded[tile, block] = source[
                        which, pl.ds(tile * SUBS, SUBS), pl.ds(block * LANES, LANES)
                    ]
                return loaded[tile, block]

            return load

        pairs = {}

        def coef(field, tile, block):
            pair = (tile + coef_tile) // 2
            if (field, pair, block) not in pairs:
                both = coefs[
                    field, plane - 1, pl.ds(pair * HALF, HALF), pl.ds(block * LANES, LANES)
                ]
                pairs[field, pair, block] = both.astype(jnp.float32)
            low = (tile + coef_tile) % 2 * SUBS
            return pairs[field, pair, block][low : low + SUBS]

        def weights(tile, block):
            spot = (plane - 1, pl.ds(tile * SUBS, SUBS), pl.ds(block * LANES, LANES))
            if coefs is None:
                return [held[index, *spot] for index in range(held.shape[0])]
            fields = [coef(field, tile, block) for field in range(FIELDS)]
            if held is None:
                return fields
            values = weights_of(*fields)
            for index, value in enumerate(values):
                held[index, *spot] = value
            return values

        def ghost_row(block):
            return jnp.broadcast_to(
                ghost[plane, :, pl.ds(block * LANES, LANES)], (SUBS, LANES)
            )

        def store(tile, block, value):
            target[plane, pl.ds(tile * SUBS, SUBS), pl.ds(block * LANES, LANES)] = value

        plane_update(
            tile_at(plane - 1),
            tile_at(plane),
            tile_at(plane + 1),
            weights,
            ghost_row,
            store,
            tiles,
            lane_blocks,
        )

    def body(step, carry):
        for inner in range(unroll):
            one(first + step * unroll + inner)
        return carry

    assert (stop - first) % unroll == 0
    lax.fori_loop(0, (stop - first) // unroll, body, 0)


def set_ghosts(ghost, from_left, from_right, guess, count):
    per_plane = guess.shape[1] // count
    for plane in range(count):
        for block in range(ghost.shape[2] // LANES):
            line = ghost_line(guess, plane * per_plane, block)
            ghost[REACH + plane, :, pl.ds(block * LANES, LANES)] = line
    for first, message in ((REACH - COEF_REACH, from_left), (REACH + count, from_right)):
        value = message[...].astype(jnp.float32)
        for plane in range(COEF_REACH):
            row = value[plane : plane + 1]
            for part in (1, 2):
                at = part * COEF_REACH + plane
                row = row + value[at : at + 1]
            ghost[first + plane] = row


def set_edges(grid, parts, count, first_row, rows):
    for side, first, fine_first in ((0, 0, REACH - FINE), (1, REACH + count, 0)):
        for plane in range(REACH):
            value = parts[side, plane, pl.ds(rows, HALF - rows), :].astype(jnp.float32)
            if fine_first <= plane < fine_first + FINE:
                rest = parts[side, REACH + plane - fine_first, pl.ds(rows, HALF - rows), :]
                value = value + rest.astype(jnp.float32)
            grid[first + plane, pl.ds(first_row, HALF - rows), :] = value


def coefficient_copies(coefs, left, right, part, band, count, sems, at):
    copies = []
    for side, message, first in ((0, left, 0), (1, right, COEF_REACH + count)):
        for field in range(FIELDS):
            copies.append(
                pltpu.make_async_copy(
                    message.at[pl.ds(REACH + FINE + field * COEF_REACH, COEF_REACH)],
                    coefs.at[field, pl.ds(first, COEF_REACH), band, :],
                    sems.at[at + side * FIELDS + field],
                )
            )
    return copies


def face_kernel(
    state, spread, flow, guess, left, right, face, grid, other, coefs, held, parts, tails, ghost, sems
):
    count, height = state.shape[0], state.shape[1]
    band = pl.ds(height - HALF, HALF)
    inner = pl.ds(COEF_REACH, count)
    copies = [
        pltpu.make_async_copy(
            state.at[:, pl.ds(height - SUBS, SUBS), :], grid.at[pl.ds(REACH, count)], sems.at[0]
        ),
        pltpu.make_async_copy(spread.at[:, band, :], coefs.at[0, inner], sems.at[1]),
        pltpu.make_async_copy(left.at[pl.ds(0, REACH + FINE)], parts.at[0], sems.at[2]),
        pltpu.make_async_copy(right.at[pl.ds(0, REACH + FINE)], parts.at[1], sems.at[3]),
        pltpu.make_async_copy(left.at[SLOTS], tails.at[0], sems.at[4]),
        pltpu.make_async_copy(right.at[SLOTS], tails.at[1], sems.at[5]),
    ]
    for axis in range(3):
        copies.append(
            pltpu.make_async_copy(
                flow.at[axis, :, band, :], coefs.at[1 + axis, inner], sems.at[6 + axis]
            )
        )
    copies += coefficient_copies(coefs, left, right, 1, pl.ds(0, HALF), count, sems, 9)
    start_all(copies)
    wait_all(copies)
    set_ghosts(ghost, tails.at[0], tails.at[1], guess, count)
    set_edges(grid, parts, count, 0, HALF - SUBS)
    pair = (grid, other)
    for step in range(SWEEPS):
        sweep(
            pair[step % 2],
            pair[(step + 1) % 2],
            None if step else coefs,
            held,
            ghost,
            step + 1,
            count + 2 * REACH - 1 - step,
            1,
            1,
            2,
        )
    last = pair[SWEEPS % 2]
    lane = lax.broadcasted_iota(jnp.int32, (count, LANES), 1)
    means = jnp.zeros((count, LANES), jnp.float32)
    strips = LANES // INTERFACE_STRIP
    for block in range(state.shape[2] // LANES):
        top = last[pl.ds(REACH, count), SUBS - 1, pl.ds(block * LANES, LANES)]
        for strip in range(strips):
            mine = (lane >= strip * INTERFACE_STRIP) & (lane < (strip + 1) * INTERFACE_STRIP)
            total = jnp.sum(jnp.where(mine, top, 0.0), axis=1, keepdims=True)
            means = jnp.where(lane == block * strips + strip, total / INTERFACE_STRIP, means)
    line = lax.broadcasted_iota(jnp.int32, (LANES, LANES), 0)
    column = lax.broadcasted_iota(jnp.int32, (LANES, LANES), 1)
    across = state.shape[2] // INTERFACE_STRIP
    spread_out = jnp.dot(
        means,
        jnp.where(column % across == line, 1.0, 0.0),
        precision=HIGHEST,
        preferred_element_type=jnp.float32,
    )
    per_row = LANES // across
    plane = lax.broadcasted_iota(jnp.int32, (per_row, LANES), 0)
    spot = lax.broadcasted_iota(jnp.int32, (per_row, LANES), 1) // across
    for row in range(face.shape[0]):
        mine = spread_out[row * per_row : (row + 1) * per_row]
        face[row] = jnp.sum(jnp.where(plane == spot, mine, 0.0), axis=0)


def interface_face(state, spread, flow, guess, left, right):
    count, _, depth = state.shape
    extended = count + 2 * REACH
    return pl.pallas_call(
        face_kernel,
        out_shape=jax.ShapeDtypeStruct((guess.shape[1] // LANES, LANES), jnp.float32),
        in_specs=[ANY, ANY, ANY, SCALARS, ANY, ANY],
        out_specs=WHOLE,
        scratch_shapes=[
            pltpu.VMEM((extended, SUBS, depth), jnp.float32),
            pltpu.VMEM((extended, SUBS, depth), jnp.float32),
            pltpu.VMEM((FIELDS, extended - 2, HALF, depth), jnp.bfloat16),
            pltpu.VMEM((2 * FIELDS - 1, extended - 2, SUBS, depth), jnp.float32),
            pltpu.VMEM((2, REACH + FINE, HALF, depth), jnp.bfloat16),
            pltpu.VMEM((2, HALF, depth), jnp.bfloat16),
            pltpu.VMEM((extended, 1, depth), jnp.float32),
            pltpu.SemaphoreType.DMA((17,)),
        ],
        cost_estimate=pl.CostEstimate(
            flops=20_000_000, bytes_accessed=6_000_000, transcendentals=0
        ),
        compiler_params=pltpu.CompilerParams(vmem_limit_bytes=16 * 2**20),
        name="interface_face",
    )(state, spread, flow, guess, left, right)


def field_kernel(
    state,
    spread,
    flow,
    guess,
    left_hi,
    left_lo,
    right_hi,
    right_lo,
    out,
    grid,
    other,
    coefs,
    parts,
    tails,
    ghost,
    sems,
):
    count, height = state.shape[0], state.shape[1]
    inner = pl.ds(COEF_REACH, count)
    copies = [
        pltpu.make_async_copy(state, grid.at[pl.ds(REACH, count)], sems.at[0]),
        pltpu.make_async_copy(spread, coefs.at[0, inner], sems.at[1]),
        pltpu.make_async_copy(left_lo.at[pl.ds(0, REACH + FINE)], parts.at[0, 0], sems.at[2]),
        pltpu.make_async_copy(right_lo.at[pl.ds(0, REACH + FINE)], parts.at[0, 1], sems.at[3]),
        pltpu.make_async_copy(left_hi.at[pl.ds(0, REACH + FINE)], parts.at[1, 0], sems.at[4]),
        pltpu.make_async_copy(right_hi.at[pl.ds(0, REACH + FINE)], parts.at[1, 1], sems.at[5]),
        pltpu.make_async_copy(left_hi.at[SLOTS], tails.at[0], sems.at[6]),
        pltpu.make_async_copy(right_hi.at[SLOTS], tails.at[1], sems.at[7]),
    ]
    for axis in range(3):
        copies.append(
            pltpu.make_async_copy(flow.at[axis], coefs.at[1 + axis, inner], sems.at[8 + axis])
        )
    copies += coefficient_copies(coefs, left_lo, right_lo, 0, pl.ds(0, HALF), count, sems, 11)
    copies += coefficient_copies(coefs, left_hi, right_hi, 1, pl.ds(HALF, HALF), count, sems, 19)
    start_all(copies)
    wait_all(copies)
    set_ghosts(ghost, tails.at[0], tails.at[1], guess, count)
    for part in range(2):
        set_edges(grid, parts.at[part], count, part * HALF, 0)
    pair = (grid, other)
    for step in range(SWEEPS):
        sweep(
            pair[step % 2],
            pair[(step + 1) % 2],
            coefs,
            None,
            ghost,
            step + 1,
            count + 2 * REACH - 1 - step,
            height // SUBS,
            0,
            1,
        )
    done = pltpu.make_async_copy(pair[SWEEPS % 2].at[pl.ds(REACH, count)], out, sems.at[0])
    done.start()
    done.wait()


def field(state, spread, flow, guess, left_hi, left_lo, right_hi, right_lo):
    count, height, depth = state.shape
    extended = count + 2 * REACH
    return pl.pallas_call(
        field_kernel,
        out_shape=jax.ShapeDtypeStruct(state.shape, jnp.float32),
        in_specs=[ANY, ANY, ANY, SCALARS, ANY, ANY, ANY, ANY],
        out_specs=ANY,
        scratch_shapes=[
            pltpu.VMEM((extended, height, depth), jnp.float32),
            pltpu.VMEM((extended, height, depth), jnp.float32),
            pltpu.VMEM((FIELDS, extended - 2, height, depth), jnp.bfloat16),
            pltpu.VMEM((2, 2, REACH + FINE, HALF, depth), jnp.bfloat16),
            pltpu.VMEM((2, HALF, depth), jnp.bfloat16),
            pltpu.VMEM((extended, 1, depth), jnp.float32),
            pltpu.SemaphoreType.DMA((27,)),
        ],
        cost_estimate=pl.CostEstimate(
            flops=80_000_000, bytes_accessed=30_000_000, transcendentals=0
        ),
        compiler_params=pltpu.CompilerParams(vmem_limit_bytes=20 * 2**20),
        name="field",
    )(state, spread, flow, guess, left_hi, left_lo, right_hi, right_lo)


def gram_kernel(panel, gram):
    value = panel[...]
    gram[...] = lax.dot_general(
        value,
        value,
        (((0,), (0,)), ((), ())),
        precision=HIGHEST,
        preferred_element_type=jnp.float32,
    )


def local_gram(panel):
    columns = panel.shape[1]
    return pl.pallas_call(
        gram_kernel,
        out_shape=jax.ShapeDtypeStruct((columns, columns), jnp.float32),
        in_specs=[WHOLE],
        out_specs=WHOLE,
        compiler_params=SMALL,
        cost_estimate=pl.CostEstimate(flops=9_000_000, bytes_accessed=200_000, transcendentals=0),
        name="gram",
    )(panel)


def sum_kernel(parts, *rest):
    *extra, sent = rest
    total = jnp.sum(parts[...], axis=0)
    if extra:
        lines = extra[0][...]
        pad = jnp.zeros((SUBS - lines.shape[0], lines.shape[1]), jnp.float32)
        total = jnp.concatenate([total, lines, pad], axis=0)
    for copy in range(sent.shape[0]):
        sent[copy] = total


def sum_and_copy(name, receivers, parts, *extra):
    _, rows, columns = parts.shape
    rows += SUBS if extra else 0
    return pl.pallas_call(
        sum_kernel,
        out_shape=jax.ShapeDtypeStruct((receivers, rows, columns), jnp.float32),
        in_specs=[WHOLE] * (1 + len(extra)),
        out_specs=WHOLE,
        compiler_params=SMALL,
        cost_estimate=pl.CostEstimate(flops=100_000, bytes_accessed=500_000, transcendentals=0),
        name=name,
    )(parts, *extra)


def tilde_kernel(gathered, partner_rows, guess, panel, tilde, sent):
    lines = guess.shape[1] // LANES
    first = gathered.shape[1] - SUBS
    table = jnp.concatenate(
        [gathered[slab, pl.ds(first, lines), :] for slab in range(gathered.shape[0])], axis=0
    )
    wanted = partner_rows[...]
    line = lax.broadcasted_iota(jnp.int32, (table.shape[0], wanted.shape[1]), 0)
    chosen = jnp.where(line == wanted // LANES, 1.0, 0.0)
    picked = lax.dot_general(
        table,
        chosen,
        (((0,), (0,)), ((), ())),
        precision=HIGHEST,
        preferred_element_type=jnp.float32,
    )
    spot = lax.broadcasted_iota(jnp.int32, picked.shape, 0)
    values = jnp.sum(jnp.where(spot == wanted % LANES, picked, 0.0), axis=0, keepdims=True)
    tilde[...] = values
    projection = jnp.dot(
        values - guess[...],
        panel[...],
        precision=HIGHEST,
        preferred_element_type=jnp.float32,
    )
    sent[...] = jnp.broadcast_to(projection[None], sent.shape)


def tilde_and_projection(gathered, partner_rows, guess, panel, receivers):
    return pl.pallas_call(
        tilde_kernel,
        out_shape=(
            jax.ShapeDtypeStruct(guess.shape, jnp.float32),
            jax.ShapeDtypeStruct((receivers, 1, panel.shape[1]), jnp.float32),
        ),
        in_specs=[WHOLE] * 4,
        out_specs=(WHOLE,) * 2,
        compiler_params=SMALL,
        cost_estimate=pl.CostEstimate(flops=9_000_000, bytes_accessed=900_000, transcendentals=0),
        name="tilde",
    )(gathered, partner_rows, guess, panel)


def small_inverse(block):
    size = len(block)
    left = [list(row) for row in block]
    unit = [[None] * size for _ in range(size)]
    reciprocals = []
    for a in range(size):
        reciprocal = 1.0 / left[a][a]
        reciprocals.append(reciprocal)
        for row in range(a + 1, size):
            factor = left[row][a] * reciprocal
            for column in range(a + 1, row + 1):
                left[row][column] = left[row][column] - factor * left[column][a]
            for column in range(a):
                known = unit[row][column]
                change = factor * unit[a][column]
                unit[row][column] = -change if known is None else known - change
            unit[row][a] = -factor
    return unit, reciprocals


def column_of(entries):
    sub = lax.broadcasted_iota(jnp.int32, (SUBS, LANES), 0)
    column = jnp.zeros((SUBS, LANES), jnp.float32)
    for row, entry in enumerate(entries):
        if entry is not None:
            column = jnp.where(sub == row, entry, column)
    return column


def inverse_factor(tiles):
    shape = (SUBS, LANES)
    lane = lax.broadcasted_iota(jnp.int32, shape, 1)
    sub = lax.broadcasted_iota(jnp.int32, shape, 0)
    tiles = list(tiles)
    done = []
    for home in range(len(tiles)):
        first = home * SUBS
        columns = [
            [
                jnp.broadcast_to(tile[:, first + b : first + b + 1], shape)
                for b in range(SUBS)
            ]
            for tile in tiles[home:]
        ]
        block = [
            [jnp.broadcast_to(columns[0][b][a : a + 1], shape) for b in range(a + 1)]
            for a in range(SUBS)
        ]
        panel = (lane >= first) & (lane < first + SUBS)
        own = jnp.where(panel, jnp.where(lane - first == sub, 1.0, 0.0), tiles[home])
        lines = [jnp.broadcast_to(own[a : a + 1], shape) for a in range(SUBS)]
        unit, reciprocals = small_inverse(block)
        result = own
        for b in range(SUBS - 1):
            result = result + column_of([unit[a][b] for a in range(SUBS)]) * lines[b]
        roots = jnp.sqrt(column_of(reciprocals))
        done.append(jnp.where(lane <= sub + first, result, 0.0) * roots)
        if home + 1 == len(tiles):
            break
        answers = [
            jnp.broadcast_to(result[a : a + 1], shape) * reciprocals[a] for a in range(SUBS)
        ]
        for index in range(home + 1, len(tiles)):
            tile = jnp.where(panel, 0.0, tiles[index])
            raw = columns[index - home]
            parts = []
            for a in range(SUBS):
                factor = raw[a]
                for b in range(a):
                    factor = factor + unit[a][b] * raw[b]
                parts.append(factor * answers[a])
            while len(parts) > 1:
                parts = [one + two for one, two in zip(parts[::2], parts[1::2])]
            tiles[index] = tile - parts[0]
    return done


def factor_kernel(total_rows, gathered, panel, inverse_out, basis):
    slabs, rows, _ = gathered.shape
    tiles = [
        gathered[slab, pl.ds(first, SUBS), :]
        for slab in range(slabs)
        for first in range(0, rows - SUBS, SUBS)
    ]
    inverse = jnp.concatenate(inverse_factor(tiles), axis=0)
    inverse_out[...] = inverse
    basis[...] = lax.dot_general(
        panel[...],
        inverse * math.sqrt(total_rows),
        (((1,), (1,)), ((), ())),
        precision=HIGHEST,
        preferred_element_type=jnp.float32,
    )


def factor_and_basis(total_rows, gathered, panel):
    columns = panel.shape[1]
    return pl.pallas_call(
        functools.partial(factor_kernel, total_rows),
        out_shape=(
            jax.ShapeDtypeStruct((columns, columns), jnp.float32),
            jax.ShapeDtypeStruct(panel.shape, jnp.float32),
        ),
        in_specs=[WHOLE] * 2,
        out_specs=(WHOLE,) * 2,
        compiler_params=SMALL,
        cost_estimate=pl.CostEstimate(flops=30_000_000, bytes_accessed=9_000_000, transcendentals=0),
        name="factor",
    )(gathered, panel)


def update_kernel(parts, inverse, changes, tilde, guess):
    projection = jnp.sum(parts[...], axis=0)
    across = (((1,), (1,)), ((), ()))
    half = lax.dot_general(
        projection, inverse[...], across, precision=HIGHEST, preferred_element_type=jnp.float32
    )
    coefficients = -jnp.dot(
        half, inverse[...], precision=HIGHEST, preferred_element_type=jnp.float32
    )
    guess[...] = tilde[...] + lax.dot_general(
        coefficients,
        changes[...],
        across,
        precision=HIGHEST,
        preferred_element_type=jnp.float32,
    )


def update(parts, inverse, changes, tilde):
    return pl.pallas_call(
        update_kernel,
        out_shape=jax.ShapeDtypeStruct(tilde.shape, jnp.float32),
        in_specs=[WHOLE] * 4,
        out_specs=WHOLE,
        compiler_params=SMALL,
        cost_estimate=pl.CostEstimate(flops=9_000_000, bytes_accessed=400_000, transcendentals=0),
        name="update",
    )(parts, inverse, changes, tilde)


def shards(
    thermal_state,
    thermal_spreading_rate,
    flow_speed_vector,
    interface_guess,
    partner_facing_rows,
    mismatch_change_matrix,
    output_change_matrix,
):
    state = thermal_state[0]
    spread = thermal_spreading_rate[0]
    flow = flow_speed_vector[:, 0]
    panel = mismatch_change_matrix[0]
    state, spread, flow = (
        pltpu.with_memory_space_constraint(value, pltpu.HBM) for value in (state, spread, flow)
    )
    slabs = lax.axis_size("slab")
    wide = lax.axis_size("half") * lax.axis_size("pair")

    everyone = ("half", "pair", "slab")
    onward = [(i, i + 1) for i in range(slabs - 1)]
    back = [(i + 1, i) for i in range(slabs - 1)]

    gram = local_gram(panel).reshape(slabs, -1, panel.shape[1])
    gram, early_guess = lax.optimization_barrier((gram, interface_guess))
    right_hi, right_lo, left_hi, left_lo = pack(state, spread, flow, early_guess)
    gram_parts = lax.all_to_all(gram, "slab", 0, 0, tiled=True)
    from_left_hi = lax.ppermute(right_hi, "slab", onward)
    from_right_hi = lax.ppermute(left_hi, "slab", back)
    from_left_lo = lax.ppermute(right_lo, "slab", onward)
    from_right_lo = lax.ppermute(left_lo, "slab", back)
    gram_parts = lax.all_to_all(
        sum_and_copy("sum_slab", wide, gram_parts), ("half", "pair"), 0, 0, tiled=True
    )
    face = interface_face(state, spread, flow, interface_guess, from_left_hi, from_right_hi)
    face = lax.ppermute(face, "half", [(0, 1), (1, 0)])
    gathered = lax.all_to_all(
        sum_and_copy("sum_wide", slabs, gram_parts, face), "slab", 0, 0, tiled=True
    )
    tilde, share = tilde_and_projection(
        gathered, partner_facing_rows, interface_guess, panel, slabs * wide
    )
    share = lax.all_to_all(share, everyone, 0, 0, tiled=True)
    temperature = field(
        state,
        spread,
        flow,
        interface_guess,
        from_left_hi,
        from_left_lo,
        from_right_hi,
        from_right_lo,
    )
    inverse, basis = factor_and_basis(panel.shape[0] * slabs * wide, gathered, panel)
    updated = update(share, inverse, output_change_matrix[0], tilde)
    return temperature[None], updated, basis[None]


def solution(mesh):
    wide, slab = mesh.shape["wide"], mesh.shape["slab"]
    fine = Mesh(mesh.devices.reshape(2, wide // 2, slab), ("half", "pair", "slab"))
    parts = ("half", "pair")
    return jax.shard_map(
        shards,
        mesh=fine,
        in_specs=(
            P(parts, "slab", None, None),
            P(parts, "slab", None, None),
            P(None, parts, "slab", None, None),
            P(parts, "slab"),
            P(parts, "slab"),
            P(parts, "slab", None),
            P(parts, "slab", None),
        ),
        out_specs=(P(parts, "slab", None, None), P(parts, "slab"), P(parts, "slab", None)),
        check_vma=False,
    )
```

time: 183 us -> 103 us (0.56)
  Pallas kernels: 78.3 us -> 37.2 us
  other arithmetic: 25.1 us -> 0 us
  local copies, waits for them, and re-layouts: 11.5 us -> 1.6 us
  matrix products: 3.07 us -> 0 us
  blocking collectives: 22.8 us -> 20.1 us
  starting transfers between devices: 39.5 us -> 41.5 us
    pallas_call x1, Pallas kernels: 49.8 us -> 3.59 us  [pack(): pl.pallas_call(pack_kernel, out_shape=(upper, lower, upper, lower), in_sp...]
    another operation x5 -> x0, other arithmetic: 23 us -> none  [the longest x3 12.5 us: shards(): lower_factor = jnp.linalg.cholesky(gram_matrix)]
    ppermute x0 -> x1, starting transfers between devices: none -> 5.51 us  [shards(): face = lax.ppermute(face, 'half', [(0, 1), (1, 0)])]
    unnamed x18 -> x12, local copies, waits for them, and re-layouts: 5.84 us -> 1.6 us
    all_to_all x4 -> x2, starting transfers between devices: 26.8 us -> 22.6 us  [the longest x1 11.4 us: shards(): share = lax.all_to_all(share, everyone, 0, 0, tiled=True)]
    pallas_call x1 -> x6, Pallas kernels: 11.3 us -> 15.4 us  [the longest x1 7.19 us: interface_face(): pl.pallas_call(face_kernel, out_shape=jax.ShapeDtypeStruct((guess.shape[1...]
    broadcast_in_dim x5 -> x0, local copies, waits for them, and re-layouts: 3.48 us -> none  [the longest x2 1.39 us: gather_sum(): copies = jnp.broadcast_to(value[None], (count, *value.shape))]
    all_to_all x1 -> x2, blocking collectives: 22.8 us -> 20.1 us  [the longest x1 10.2 us: shards(): gram_parts = lax.all_to_all(gram, 'slab', 0, 0, tiled=True)]
  transfers between devices with their start and end apart: 8 -> 7, of which waited for: 1 -> 1; matrix products, arithmetic and copies ran while one was open for 16% -> 0% of each run, Pallas kernels for 14% -> 31%
where the time goes in v3:
time: 103 us; the launch traced here: 102 us
  starting transfers between devices  41.5 us (40%)
  Pallas kernels  37.2 us (36%)
  blocking collectives  20.1 us (20%)
  local copies, waits for them, and re-layouts  1.6 us (2%)
    pallas_call x1, Pallas kernels, field(): pl.pallas_call(field_kernel, out_shape=jax.ShapeDtypeStruct(state.shape,...  16.9 us
    all_to_all x1, starting transfers between devices, shards(): share = lax.all_to_all(share, everyone, 0, 0, tiled=True)  11.4 us
    all_to_all x1, starting transfers between devices, shards(): lax.all_to_all(sum_and_copy('sum_slab', wide, gram_parts), ('half', 'pair...  11.2 us
    all_to_all x1, blocking collectives, shards(): gram_parts = lax.all_to_all(gram, 'slab', 0, 0, tiled=True)  10.2 us
    all_to_all x1, blocking collectives, shards(): lax.all_to_all(sum_and_copy('sum_wide', slabs, gram_parts, face), 'slab',...  9.82 us
    pallas_call x1, Pallas kernels, interface_face(): pl.pallas_call(face_kernel, out_shape=jax.ShapeDtypeStruct((guess.shape[1...  7.19 us
    pallas_call x1, Pallas kernels, factor_and_basis(): pl.pallas_call(functools.partial(factor_kernel, total_rows), out_shape=(j...  5.58 us
    ppermute x1, starting transfers between devices, shards(): face = lax.ppermute(face, 'half', [(0, 1), (1, 0)])  5.51 us
  transfers between devices with their start and end apart: 7, of which 1 were waited for; matrix products, arithmetic and copies ran while one was open for 0% of the time, Pallas kernels for 31%

profile of v3, /device:TPU:1, one launch (start us, length us, event | category | flops | bytes accessed | tf_op | source)
XLA Modules:
  0.0 102.2 jit_solution(13967999179092434482)
XLA Ops:
  0.6 0.0 copy-start
  0.6 0.9 copy-done
  1.5 0.3 gram.1
  1.9 0.0 copy-start.3
  1.9 0.7 copy-done.3
  2.5 3.6 %pack_edges.1 = (bf16[19,16,1024]{2,1,0:T(8,128)(2,1)}, bf16[18,16,1024]{2,1,0:T(8,128)(2,1)}, bf16[19,16,1024]{2,1,0:T(8,128)(2,1)}, bf16[18,16,1024]{2,1,0:T(8,128)(2,1)S(1)}) custom-call(f32[16,32,1024]{2,1,0:T(8,128)} %bitcast.16, bf16[16,32,1024]{2,1,0:T(8,128)(2,1)} %bitcast.19, bf16[3,16,32,1024]{3,2,1,0:T(8,128)(2,1)} %bitcast.13, f32[1,256]{1,0:T(1,128)S(1)} %copy-done.3), custom_call_target="tpu_custom_call" | custom-call | flops 2000000 | bytes 6000000 | tf_op jit(solution)/shard_map/pack_edges/pallas_call | solution.py:112
  6.1 4.5 %collective-permute-start = (bf16[19,16,1024]{2,1,0:T(8,128)(2,1)}, bf16[19,16,1024]{2,1,0:T(8,128)(2,1)S(1)}, u32[]{:S(2)}, u32[]{:S(2)}) collective-permute-start(bf16[19,16,1024]{2,1,0:T(8,128)(2,1)} %get-tuple-element.14), channel_id=1, source_target_pairs={{0,1},{1,2},{2,3},{3,4},{4,5},{5,6},{6,7},{8,9},{9,10},{10,11},{11... | collective-permute-start | bytes 1867784 | tf_op jit(solution)/shard_map/ppermute | solution.py:731
  10.7 2.0 %collective-permute-start.2 = (bf16[19,16,1024]{2,1,0:T(8,128)(2,1)}, bf16[19,16,1024]{2,1,0:T(8,128)(2,1)S(1)}, u32[]{:S(2)}, u32[]{:S(2)}) collective-permute-start(bf16[19,16,1024]{2,1,0:T(8,128)(2,1)} %get-tuple-element.16), channel_id=1, source_target_pairs={{1,0},{2,1},{3,2},{4,3},{5,4},{6,5},{7,6},{9,8},{10,9},{11,10},{12... | collective-permute-start | bytes 1867784 | tf_op jit(solution)/shard_map/ppermute | solution.py:732
  12.6 10.2 %all_to_all.20.parts = f32[8,16,128]{2,1,0:T(8,128)S(1)} all-to-all(f32[8,16,128]{2,1,0:T(8,128)S(1)} %bitcast.11), channel_id=1, replica_groups=mesh['half'=2,'pair'=16,'slab'=8] {'slab'}, dimensions={0} | all-to-all | bytes 131072 | tf_op jit(solution)/shard_map/all_to_all | solution.py:730
  22.9 0.7 sum_slab.1
  23.6 11.2 %all-to-all-start.1 = ((f32[32,16,128]{2,1,0:T(8,128)}), f32[32,16,128]{2,1,0:T(8,128)S(1)}, u32[]{:S(2)}, u32[]{:S(2)}) async-start(f32[32,16,128]{2,1,0:T(8,128)} %sum_slab.1), calls=%async_computation.1 | async-start | bytes 524288 | tf_op jit(solution)/shard_map/all_to_all | solution.py:735
  34.8 4.9 %collective-permute-start.1 = (bf16[18,16,1024]{2,1,0:T(8,128)(2,1)}, bf16[18,16,1024]{2,1,0:T(8,128)(2,1)S(1)}, u32[]{:S(2)}, u32[]{:S(2)}) collective-permute-start(bf16[18,16,1024]{2,1,0:T(8,128)(2,1)} %get-tuple-element.15), channel_id=1, source_target_pairs={{0,1},{1,2},{2,3},{3,4},{4,5},{5,6},{6,7},{8,9},{9,10},{10,11},{11... | collective-permute-start | bytes 1769480 | tf_op jit(solution)/shard_map/ppermute | solution.py:733
  39.7 0.0 copy-start.1
  39.7 0.0 copy-start.5
  39.7 2.1 %collective-permute-start.3 = (bf16[18,16,1024]{2,1,0:T(8,128)(2,1)S(1)}, bf16[18,16,1024]{2,1,0:T(8,128)(2,1)S(1)}, u32[]{:S(2)}, u32[]{:S(2)}) collective-permute-start(bf16[18,16,1024]{2,1,0:T(8,128)(2,1)S(1)} %get-tuple-element.17), channel_id=1, source_target_pairs={{1,0},{2,1},{3,2},{4,3},{5,4},{6,5},{7,6},{9,8},{10,9},{11,10},{12... | collective-permute-start | bytes 1769480 | tf_op jit(solution)/shard_map/ppermute | solution.py:734
  41.7 0.0 collective-permute-done.left_hi.left
  41.8 0.0 collective-permute-done.2.right_hi.right
  41.8 7.2 %interface_face.1 = f32[2,128]{1,0:T(2,128)S(1)} custom-call(f32[16,32,1024]{2,1,0:T(8,128)} %bitcast.17, bf16[16,32,1024]{2,1,0:T(8,128)(2,1)} %bitcast.20, bf16[3,16,32,1024]{3,2,1,0:T(8,128)(2,1)} %bitcast.14, f32[1,256]{1,0:T(1,128)S(1)} %copy-done.4, bf16[19,16,1024]{2,1,0:T(8,128)(2,1)S(1)} %collective-permute-done.left_hi.left, ...), custom_call_target="tpu_custom_call" | custom-call | flops 20000000 | bytes 6000000 | tf_op jit(solution)/shard_map/interface_face/pallas_call | solution.py:363
  49.0 5.5 %collective-permute-start.4 = (f32[2,128]{1,0:T(2,128)S(1)}, f32[2,128]{1,0:T(2,128)S(1)}, u32[]{:S(2)}, u32[]{:S(2)}) collective-permute-start(f32[2,128]{1,0:T(2,128)S(1)} %interface_face.1), channel_id=1, source_target_pairs={{0,128},{128,0},{1,129},{129,1},{2,130},{130,2},{3,131},{131,3},{4... | collective-permute-start | bytes 3080 | tf_op jit(solution)/shard_map/ppermute | solution.py:739
  54.5 0.0 all-to-all-done.1.parts
  54.5 1.0 collective-permute-done.4.rest_0_
  55.5 9.8 %all_to_all.21.gathered = f32[8,24,128]{2,1,0:T(8,128)S(1)} all-to-all(f32[8,24,128]{2,1,0:T(8,128)S(1)} %sum_wide.1), channel_id=1, replica_groups=mesh['half'=2,'pair'=16,'slab'=8] {'slab'}, dimensions={0} | all-to-all | bytes 196608 | tf_op jit(solution)/shard_map/all_to_all | solution.py:740
  65.3 0.0 copy-done.1
  65.3 1.3 %tilde.1 = (f32[1,256]{1,0:T(1,128)S(1)}, f32[256,1,128]{2,1,0:T(1,128)}) custom-call(f32[8,24,128]{2,1,0:T(8,128)S(1)} %all_to_all.21.gathered, s32[1,256]{1,0:T(1,128)S(1)} %copy-done.5, f32[1,256]{1,0:T(1,128)S(1)} %copy-done.4, f32[256,128]{1,0:T(8,128)S(1)} %bitcast.9), custom_call_target="tpu_custom_call" | custom-call | flops 9000000 | bytes 900000 | tf_op jit(solution)/shard_map/tilde/pallas_call | solution.py:549
  66.6 11.4 %all-to-all-start.3 = ((f32[256,1,128]{2,1,0:T(1,128)}), f32[256,1,128]{2,1,0:T(1,128)S(1)}, u32[]{:S(2)}, u32[]{:S(2)}) async-start(f32[256,1,128]{2,1,0:T(1,128)} %get-tuple-element.19), calls=%async_computation.3 | async-start | bytes 262144 | tf_op jit(solution)/shard_map/all_to_all | solution.py:746
  78.0 0.0 copy-start.2
  78.0 0.0 collective-permute-done.1.left_lo
  78.0 0.0 collective-permute-done.3.right_lo
  78.1 16.9 %field.1 = f32[16,32,1024]{2,1,0:T(8,128)} custom-call(f32[16,32,1024]{2,1,0:T(8,128)} %bitcast.18, bf16[16,32,1024]{2,1,0:T(8,128)(2,1)} %bitcast.21, bf16[3,16,32,1024]{3,2,1,0:T(8,128)(2,1)} %bitcast.15, f32[1,256]{1,0:T(1,128)S(1)} %copy-done.4, bf16[19,16,1024]{2,1,0:T(8,128)(2,1)S(1)} %collective-permute-done.left_hi.left, ...), custom_call_target="tpu_custom_call" | custom-call | flops 80000000 | bytes 30000000 | tf_op jit(solution)/shard_map/field/pallas_call | solution.py:449
  95.0 5.6 %factor.1 = (f32[128,128]{1,0:T(8,128)S(1)}, f32[256,128]{1,0:T(8,128)}) custom-call(f32[8,24,128]{2,1,0:T(8,128)S(1)} %all_to_all.21.gathered, f32[256,128]{1,0:T(8,128)S(1)} %bitcast.10), custom_call_target="tpu_custom_call" | custom-call | flops 30000000 | bytes 9000000 | tf_op jit(solution)/shard_map/factor/pallas_call | solution.py:660
  100.6 0.0 all-to-all-done.3.parts
  100.6 1.6 %update.1 = f32[1,256]{1,0:T(1,128)} custom-call(f32[256,1,128]{2,1,0:T(1,128)S(1)} %all-to-all-done.3.parts, f32[128,128]{1,0:T(8,128)S(1)} %get-tuple-element.20.inverse, f32[256,128]{1,0:T(8,128)S(1)} %bitcast.12, f32[1,256]{1,0:T(1,128)S(1)} %get-tuple-element.21.tilde), custom_call_target="tpu_custom_call" | custom-call | flops 9000000 | bytes 400000 | tf_op jit(solution)/shard_map/update/pallas_call | solution.py:693
  (5 shorter events, 0.0 us)
Async XLA Ops:
  0.6 0.9 copy-start
  1.9 0.7 copy-start.3
  2.5 39.2 %copy-start.4 = (f32[1,256]{1,0:T(1,128)S(1)}, f32[1,256]{1,0:T(1,128)}, u32[]{:S(2)}) copy-start(f32[1,256]{1,0:T(1,128)} %guess.6) | copy-start | bytes 3076
  6.1 35.6 %collective-permute-start = (bf16[19,16,1024]{2,1,0:T(8,128)(2,1)}, bf16[19,16,1024]{2,1,0:T(8,128)(2,1)S(1)}, u32[]{:S(2)}, u32[]{:S(2)}) collective-permute-start(bf16[19,16,1024]{2,1,0:T(8,128)(2,1)} %get-tuple-element.14), channel_id=1, source_target_pairs={{0,1},{1,2},{2,3},{3,4},{4,5},{5,6},{6,7},{8,9},{9,10},{10,11},{11... | collective-permute-start | bytes 1867784 | tf_op jit(solution)/shard_map/ppermute | solution.py:731
  10.7 31.1 %collective-permute-start.2 = (bf16[19,16,1024]{2,1,0:T(8,128)(2,1)}, bf16[19,16,1024]{2,1,0:T(8,128)(2,1)S(1)}, u32[]{:S(2)}, u32[]{:S(2)}) collective-permute-start(bf16[19,16,1024]{2,1,0:T(8,128)(2,1)} %get-tuple-element.16), channel_id=1, source_target_pairs={{1,0},{2,1},{3,2},{4,3},{5,4},{6,5},{7,6},{9,8},{10,9},{11,10},{12... | collective-permute-start | bytes 1867784 | tf_op jit(solution)/shard_map/ppermute | solution.py:732
  23.6 30.9 %all-to-all-start.1 = ((f32[32,16,128]{2,1,0:T(8,128)}), f32[32,16,128]{2,1,0:T(8,128)S(1)}, u32[]{:S(2)}, u32[]{:S(2)}) async-start(f32[32,16,128]{2,1,0:T(8,128)} %sum_slab.1), calls=%async_computation.1 | async-start | bytes 524288 | tf_op jit(solution)/shard_map/all_to_all | solution.py:735
  34.8 43.3 %collective-permute-start.1 = (bf16[18,16,1024]{2,1,0:T(8,128)(2,1)}, bf16[18,16,1024]{2,1,0:T(8,128)(2,1)S(1)}, u32[]{:S(2)}, u32[]{:S(2)}) collective-permute-start(bf16[18,16,1024]{2,1,0:T(8,128)(2,1)} %get-tuple-element.15), channel_id=1, source_target_pairs={{0,1},{1,2},{2,3},{3,4},{4,5},{5,6},{6,7},{8,9},{9,10},{10,11},{11... | collective-permute-start | bytes 1769480 | tf_op jit(solution)/shard_map/ppermute | solution.py:733
  39.7 25.6 %copy-start.1 = (f32[1,256,128]{2,1,0:T(8,128)S(1)}, f32[1,256,128]{2,1,0:T(8,128)}, u32[]{:S(2)}) copy-start(f32[1,256,128]{2,1,0:T(8,128)} %param.12) | copy-start | bytes 393220
  39.7 25.6 %copy-start.5 = (s32[1,256]{1,0:T(1,128)S(1)}, s32[1,256]{1,0:T(1,128)}, u32[]{:S(2)}) copy-start(s32[1,256]{1,0:T(1,128)} %partner_rows.1) | copy-start | bytes 3076
  39.7 38.4 %collective-permute-start.3 = (bf16[18,16,1024]{2,1,0:T(8,128)(2,1)S(1)}, bf16[18,16,1024]{2,1,0:T(8,128)(2,1)S(1)}, u32[]{:S(2)}, u32[]{:S(2)}) collective-permute-start(bf16[18,16,1024]{2,1,0:T(8,128)(2,1)S(1)} %get-tuple-element.17), channel_id=1, source_target_pairs={{1,0},{2,1},{3,2},{4,3},{5,4},{6,5},{7,6},{9,8},{10,9},{11,10},{12... | collective-permute-start | bytes 1769480 | tf_op jit(solution)/shard_map/ppermute | solution.py:734
  49.0 6.5 %collective-permute-start.4 = (f32[2,128]{1,0:T(2,128)S(1)}, f32[2,128]{1,0:T(2,128)S(1)}, u32[]{:S(2)}, u32[]{:S(2)}) collective-permute-start(f32[2,128]{1,0:T(2,128)S(1)} %interface_face.1), channel_id=1, source_target_pairs={{0,128},{128,0},{1,129},{129,1},{2,130},{130,2},{3,131},{131,3},{4... | collective-permute-start | bytes 3080 | tf_op jit(solution)/shard_map/ppermute | solution.py:739
  66.6 34.0 %all-to-all-start.3 = ((f32[256,1,128]{2,1,0:T(1,128)}), f32[256,1,128]{2,1,0:T(1,128)S(1)}, u32[]{:S(2)}, u32[]{:S(2)}) async-start(f32[256,1,128]{2,1,0:T(1,128)} %get-tuple-element.19), calls=%async_computation.3 | async-start | bytes 262144 | tf_op jit(solution)/shard_map/all_to_all | solution.py:746
  78.0 22.6 %copy-start.2 = (f32[1,256,128]{2,1,0:T(8,128)S(1)}, f32[1,256,128]{2,1,0:T(8,128)}, u32[]{:S(2)}) copy-start(f32[1,256,128]{2,1,0:T(8,128)} %param.13) | copy-start | bytes 393220

commit v4 on v3

v4 whole, which is shorter than its diff:
```python
import functools
import math

import jax
import jax.numpy as jnp
from jax import lax
from jax.experimental import pallas as pl
from jax.experimental.pallas import tpu as pltpu
from jax.sharding import Mesh
from jax.sharding import PartitionSpec as P

INTERFACE_STRIP = 64
SWEEPS = 4
STEP_SIZE = 0.11
PACKED = 16
LANES = 128
SUBS = 8
REACH = SWEEPS
COEF_REACH = SWEEPS - 1
FINE = 0
FIELDS = 4
SLOTS = REACH + FINE + FIELDS * COEF_REACH
HIGHEST = lax.Precision.HIGHEST
ANY = pl.BlockSpec(memory_space=pl.ANY)
WHOLE = pl.BlockSpec(memory_space=pltpu.VMEM)
SMALL = pltpu.CompilerParams(vmem_limit_bytes=8 * 2**20)
SCALARS = pl.BlockSpec(memory_space=pltpu.SMEM)


def start_all(copies):
    for copy in copies:
        copy.start()


def wait_all(copies):
    for copy in copies:
        copy.wait()


def ghost_line(guess, first, block):
    lane = lax.broadcasted_iota(jnp.int32, (1, LANES), 1)
    strips = LANES // INTERFACE_STRIP
    at = first + block * strips
    row = jnp.full((1, LANES), guess[0, at], jnp.float32)
    for strip in range(1, strips):
        row = jnp.where(lane < strip * INTERFACE_STRIP, row, guess[0, at + strip])
    return row


def pack_kernel(state, spread, flow, guess, right, left, planes, sems):
    count = state.shape[0]
    lane_blocks = state.shape[2] // LANES
    per_plane = guess.shape[1] // count
    fetch = [
        pltpu.make_async_copy(state.at[pl.ds(count - REACH, REACH)], planes.at[0], sems.at[8]),
        pltpu.make_async_copy(state.at[pl.ds(0, REACH)], planes.at[1], sems.at[9]),
    ]
    started = []
    for side, out, first in ((0, right, count - COEF_REACH), (1, left, 0)):
        source = [spread.at[pl.ds(first, COEF_REACH)]]
        source += [flow.at[axis, pl.ds(first, COEF_REACH)] for axis in range(3)]
        for field in range(FIELDS):
            slot = REACH + FINE + field * COEF_REACH
            started.append(
                pltpu.make_async_copy(
                    source[field],
                    out.at[pl.ds(slot, COEF_REACH)],
                    sems.at[side * FIELDS + field],
                )
            )
    start_all(fetch)
    start_all(started)
    for out, first in ((right, count - COEF_REACH), (left, 0)):
        for block in range(lane_blocks):
            lines = [
                ghost_line(guess, (first + plane) * per_plane, block)
                for plane in range(COEF_REACH)
            ]
            pieces = []
            for _ in range(3):
                leads = [line.astype(jnp.bfloat16).astype(jnp.float32) for line in lines]
                lines = [line - lead for line, lead in zip(lines, leads)]
                pieces += leads
            pad = jnp.zeros((PACKED - 3 * COEF_REACH, LANES), jnp.float32)
            whole = jnp.concatenate([*pieces, pad], axis=0).astype(jnp.bfloat16)
            out[SLOTS, pl.ds(0, PACKED), pl.ds(block * LANES, LANES)] = whole
        unused = state.shape[1] - PACKED
        out[SLOTS, pl.ds(PACKED, unused), :] = jnp.zeros((unused, state.shape[2]), jnp.bfloat16)
    wait_all(fetch)
    for side, out, fine_first in ((0, right, REACH - FINE), (1, left, 0)):
        for plane in range(REACH):
            value = planes[side, plane]
            lead = value.astype(jnp.bfloat16)
            out[plane] = lead
            if fine_first <= plane < fine_first + FINE:
                rest = value - lead.astype(jnp.float32)
                out[REACH + plane - fine_first] = rest.astype(jnp.bfloat16)
    wait_all(started)


def pack(state, spread, flow, guess):
    message = jax.ShapeDtypeStruct((SLOTS + 1, *state.shape[1:]), jnp.bfloat16)
    return pl.pallas_call(
        pack_kernel,
        out_shape=(message, message),
        in_specs=[ANY, ANY, ANY, SCALARS],
        out_specs=(WHOLE,) * 2,
        scratch_shapes=[
            pltpu.VMEM((2, REACH, *state.shape[1:]), jnp.float32),
            pltpu.SemaphoreType.DMA((10,)),
        ],
        compiler_params=pltpu.CompilerParams(vmem_limit_bytes=16 * 2**20),
        cost_estimate=pl.CostEstimate(flops=2_000_000, bytes_accessed=9_000_000, transcendentals=0),
        name="pack_edges",
    )(state, spread, flow, guess)


def weights_of(mode, rate, flow_x, flow_y, flow_z):
    rate = STEP_SIZE * rate
    flow_x, flow_y, flow_z = (0.5 * STEP_SIZE * flow for flow in (flow_x, flow_y, flow_z))
    if mode == 4:
        return rate, flow_x, flow_y, flow_z
    return (
        rate + flow_x,
        rate - flow_x,
        rate + flow_y,
        rate - flow_y,
        rate + flow_z,
        rate - flow_z,
        1.0 - 6.0 * rate,
    )


def swept(here, minus, plus, weight):
    if len(weight) == 4:
        total = ((plus[0] + minus[0]) + (plus[1] + minus[1])) + (plus[2] + minus[2])
        carried = (
            weight[1] * (plus[0] - minus[0])
            + weight[2] * (plus[1] - minus[1])
            + weight[3] * (plus[2] - minus[2])
        )
        return here + (weight[0] * (total - 6.0 * here) - carried)
    x, y, z = (
        weight[2 * axis] * minus[axis] + weight[2 * axis + 1] * plus[axis] for axis in range(3)
    )
    return (x + y) + (z + weight[6] * here)


FLOOR = 8
UNROLL = 2


def sweep(source, target, coefs, held, height, first, stop):
    lane_blocks = source.shape[1]
    lane = lax.broadcasted_iota(jnp.int32, (SUBS, LANES), 1)
    zero = jnp.zeros((SUBS, LANES), jnp.float32)

    def pair(step, carry):
        low = first + step * UNROLL
        kept = {}

        def load(offset, tile, block, shift=0):
            key = (offset, tile, block, shift)
            if key not in kept:
                rows = pl.ds(FLOOR + tile * SUBS + shift, SUBS)
                kept[key] = source[low + offset, block, rows, :]
            return kept[key]

        def rolled(offset, tile, block, shift):
            key = ("rolled", offset, tile, block, shift)
            if key not in kept:
                kept[key] = pltpu.roll(load(offset, tile, block), shift, 1)
            return kept[key]

        for block in range(lane_blocks):
            for tile in range(height // SUBS):
                for offset in range(UNROLL):
                    plane = low + offset
                    carry_in = rolled(offset, tile, block - 1, 1) if block else zero
                    minus_z = jnp.where(lane == 0, carry_in, rolled(offset, tile, block, 1))
                    last = block + 1 == lane_blocks
                    carry_in = zero if last else rolled(offset, tile, block + 1, LANES - 1)
                    moved = rolled(offset, tile, block, LANES - 1)
                    plus_z = jnp.where(lane == LANES - 1, carry_in, moved)
                    minus = (load(offset - 1, tile, block), load(offset, tile, block, -1), minus_z)
                    plus = (load(offset + 1, tile, block), load(offset, tile, block, 1), plus_z)
                    rows = pl.ds(tile * SUBS, SUBS)
                    if coefs is None:
                        weight = [
                            held[index, plane - 1, block, rows, :]
                            for index in range(held.shape[0])
                        ]
                    else:
                        half = tile * SUBS % PACKED
                        key = ("coef", offset, tile * SUBS // PACKED, block)
                        if key not in kept:
                            packed = pl.ds(tile * SUBS - half, PACKED)
                            lanes = pl.ds(block * LANES, LANES)
                            kept[key] = [
                                coefs[field, plane - 1, packed, lanes].astype(jnp.float32)
                                for field in range(FIELDS)
                            ]
                        mode = FIELDS if held is None else held.shape[0]
                        fields = [field[half : half + SUBS] for field in kept[key]]
                        weight = weights_of(mode, *fields)
                        if held is not None:
                            for index, value in enumerate(weight):
                                held[index, plane - 1, block, rows, :] = value
                    value = swept(load(offset, tile, block), minus, plus, weight)
                    if len(target.shape) == 4:
                        target[plane, block, pl.ds(FLOOR + tile * SUBS, SUBS), :] = value
                    else:
                        target[plane - REACH, rows, pl.ds(block * LANES, LANES)] = value
        return carry

    assert (stop - first) % UNROLL == 0
    lax.fori_loop(0, (stop - first) // UNROLL, pair, 0)


def set_rims(grids, guess, count, height):
    per_plane = guess.shape[1] // count
    for grid in grids:
        for block in range(grid.shape[1]):
            grid[:, block, pl.ds(0, FLOOR), :] = jnp.zeros(
                (grid.shape[0], FLOOR, LANES), jnp.float32
            )
    for plane in range(count):
        for block in range(grids[0].shape[1]):
            line = ghost_line(guess, plane * per_plane, block)
            for grid in grids:
                grid[REACH + plane, block, pl.ds(FLOOR + height, 1), :] = line


def set_edges(grids, parts, count, height):
    for side, first, fine_first in ((0, 0, REACH - FINE), (1, REACH + count, 0)):
        near = first + REACH - COEF_REACH if side == 0 else first
        for block in range(grids[0].shape[1]):
            lanes = pl.ds(block * LANES, LANES)
            for plane in range(REACH):
                value = parts[side, plane, :, lanes].astype(jnp.float32)
                if fine_first <= plane < fine_first + FINE:
                    rest = parts[side, REACH + plane - fine_first, :, lanes]
                    value = value + rest.astype(jnp.float32)
                grids[0][first + plane, block, pl.ds(FLOOR, height), :] = value
            tail = parts[side, REACH + FINE, pl.ds(0, PACKED), lanes].astype(jnp.float32)
            for plane in range(COEF_REACH):
                row = tail[plane : plane + 1]
                for part in (1, 2):
                    at = part * COEF_REACH + plane
                    row = row + tail[at : at + 1]
                for grid in grids:
                    grid[near + plane, block, pl.ds(FLOOR + height, 1), :] = row


def face_means(last, face, count, height):
    lane_blocks = last.shape[2] // LANES
    lane = lax.broadcasted_iota(jnp.int32, (count, LANES), 1)
    means = jnp.zeros((count, LANES), jnp.float32)
    strips = LANES // INTERFACE_STRIP
    for block in range(lane_blocks):
        top = last[:, height - 1, pl.ds(block * LANES, LANES)]
        for strip in range(strips):
            mine = (lane >= strip * INTERFACE_STRIP) & (lane < (strip + 1) * INTERFACE_STRIP)
            total = jnp.sum(jnp.where(mine, top, 0.0), axis=1, keepdims=True)
            means = jnp.where(lane == block * strips + strip, total / INTERFACE_STRIP, means)
    line = lax.broadcasted_iota(jnp.int32, (LANES, LANES), 0)
    column = lax.broadcasted_iota(jnp.int32, (LANES, LANES), 1)
    across = lane_blocks * strips
    spread_out = jnp.dot(
        means,
        jnp.where(column % across == line, 1.0, 0.0),
        precision=HIGHEST,
        preferred_element_type=jnp.float32,
    )
    per_row = LANES // across
    plane = lax.broadcasted_iota(jnp.int32, (per_row, LANES), 0)
    spot = lax.broadcasted_iota(jnp.int32, (per_row, LANES), 1) // across
    for row in range(face.shape[0]):
        mine = spread_out[row * per_row : (row + 1) * per_row]
        face[row] = jnp.sum(jnp.where(plane == spot, mine, 0.0), axis=0)


HELD = 4


def field_kernel(
    state, spread, flow, guess, left, right, out, face, grid, other, plain, coefs, parts, *rest
):
    *held, sems = rest
    held = held[0] if held else None
    count, height = state.shape[0], state.shape[1]
    lane_blocks = grid.shape[1]
    inner = pl.ds(COEF_REACH, count)
    parted = pl.ds(0, REACH + FINE)
    early = [
        pltpu.make_async_copy(state, plain, sems.at[0]),
        pltpu.make_async_copy(left.at[parted], parts.at[0, parted], sems.at[1]),
        pltpu.make_async_copy(right.at[parted], parts.at[1, parted], sems.at[2]),
        pltpu.make_async_copy(left.at[SLOTS], parts.at[0, REACH + FINE], sems.at[3]),
        pltpu.make_async_copy(right.at[SLOTS], parts.at[1, REACH + FINE], sems.at[4]),
    ]
    later = [pltpu.make_async_copy(spread, coefs.at[0, inner], sems.at[5])]
    for axis in range(3):
        later.append(
            pltpu.make_async_copy(flow.at[axis], coefs.at[1 + axis, inner], sems.at[6 + axis])
        )
    for side, message, first in ((0, left, 0), (1, right, COEF_REACH + count)):
        for field in range(FIELDS):
            later.append(
                pltpu.make_async_copy(
                    message.at[pl.ds(REACH + FINE + field * COEF_REACH, COEF_REACH)],
                    coefs.at[field, pl.ds(first, COEF_REACH)],
                    sems.at[9 + side * FIELDS + field],
                )
            )
    start_all(early)
    start_all(later)
    set_rims((grid, other), guess, count, height)
    wait_all(early)
    set_edges((grid, other), parts, count, height)
    for plane in range(count):
        for block in range(lane_blocks):
            grid[REACH + plane, block, pl.ds(FLOOR, height), :] = plain[
                plane, :, pl.ds(block * LANES, LANES)
            ]
    wait_all(later)
    pair = (grid, other)
    for step in range(SWEEPS - 1):
        sweep(
            pair[step % 2],
            pair[(step + 1) % 2],
            None if step and held is not None else coefs,
            held,
            height,
            step + 1,
            count + 2 * REACH - 1 - step,
        )
    pushes = []
    pieces = 2
    for piece in range(pieces):
        first = piece * count // pieces
        planes = pl.ds(first, count // pieces)
        sweep(
            pair[(SWEEPS - 1) % 2],
            plain,
            None if held is not None else coefs,
            held,
            height,
            REACH + first,
            REACH + first + count // pieces,
        )
        pushes.append(pltpu.make_async_copy(plain.at[planes], out.at[planes], sems.at[piece]))
        pushes[-1].start()
    face_means(plain, face, count, height)
    wait_all(pushes)


def field_and_face(state, spread, flow, guess, left, right):
    count, height, depth = state.shape
    extended = count + 2 * REACH
    lane_blocks = depth // LANES
    tall = FLOOR + height + SUBS
    held = [pltpu.VMEM((HELD, extended - 2, lane_blocks, height, LANES), jnp.float32)]
    return pl.pallas_call(
        field_kernel,
        out_shape=(
            jax.ShapeDtypeStruct(state.shape, jnp.float32),
            jax.ShapeDtypeStruct((guess.shape[1] // LANES, LANES), jnp.float32),
        ),
        in_specs=[ANY, ANY, ANY, SCALARS, ANY, ANY],
        out_specs=(pl.BlockSpec(memory_space=pltpu.HBM), WHOLE),
        scratch_shapes=[
            pltpu.VMEM((extended, lane_blocks, tall, LANES), jnp.float32),
            pltpu.VMEM((extended, lane_blocks, tall, LANES), jnp.float32),
            pltpu.VMEM(state.shape, jnp.float32),
            pltpu.VMEM((FIELDS, extended - 2, height, depth), jnp.bfloat16),
            pltpu.VMEM((2, REACH + FINE + 1, height, depth), jnp.bfloat16),
            *(held if HELD else []),
            pltpu.SemaphoreType.DMA((17,)),
        ],
        compiler_params=pltpu.CompilerParams(vmem_limit_bytes=(24 + 3 * HELD) * 2**20),
        cost_estimate=pl.CostEstimate(
            flops=80_000_000, bytes_accessed=30_000_000, transcendentals=0
        ),
        name="field",
    )(state, spread, flow, guess, left, right)


def gram_kernel(panel, gram):
    value = panel[...]
    gram[...] = lax.dot_general(
        value,
        value,
        (((0,), (0,)), ((), ())),
        precision=HIGHEST,
        preferred_element_type=jnp.float32,
    )


def local_gram(panel):
    columns = panel.shape[1]
    return pl.pallas_call(
        gram_kernel,
        out_shape=jax.ShapeDtypeStruct((columns, columns), jnp.float32),
        in_specs=[WHOLE],
        out_specs=WHOLE,
        compiler_params=SMALL,
        cost_estimate=pl.CostEstimate(flops=9_000_000, bytes_accessed=200_000, transcendentals=0),
        name="gram",
    )(panel)


def sum_kernel(parts, *rest):
    *extra, sent = rest
    total = jnp.sum(parts[...], axis=0)
    if extra:
        lines = extra[0][...]
        pad = jnp.zeros((SUBS - lines.shape[0], lines.shape[1]), jnp.float32)
        total = jnp.concatenate([total, lines, pad], axis=0)
    for copy in range(sent.shape[0]):
        sent[copy] = total


def sum_and_copy(name, receivers, parts, *extra):
    _, rows, columns = parts.shape
    rows += SUBS if extra else 0
    return pl.pallas_call(
        sum_kernel,
        out_shape=jax.ShapeDtypeStruct((receivers, rows, columns), jnp.float32),
        in_specs=[WHOLE] * (1 + len(extra)),
        out_specs=WHOLE,
        compiler_params=SMALL,
        cost_estimate=pl.CostEstimate(flops=100_000, bytes_accessed=500_000, transcendentals=0),
        name=name,
    )(parts, *extra)


def tilde_kernel(gathered, partner_rows, guess, panel, tilde, sent):
    lines = guess.shape[1] // LANES
    first = gathered.shape[1] - SUBS
    table = jnp.concatenate(
        [gathered[slab, pl.ds(first, lines), :] for slab in range(gathered.shape[0])], axis=0
    )
    wanted = partner_rows[...]
    line = lax.broadcasted_iota(jnp.int32, (table.shape[0], wanted.shape[1]), 0)
    chosen = jnp.where(line == wanted // LANES, 1.0, 0.0)
    picked = lax.dot_general(
        table,
        chosen,
        (((0,), (0,)), ((), ())),
        precision=HIGHEST,
        preferred_element_type=jnp.float32,
    )
    spot = lax.broadcasted_iota(jnp.int32, picked.shape, 0)
    values = jnp.sum(jnp.where(spot == wanted % LANES, picked, 0.0), axis=0, keepdims=True)
    tilde[...] = values
    projection = jnp.dot(
        values - guess[...],
        panel[...],
        precision=HIGHEST,
        preferred_element_type=jnp.float32,
    )
    sent[...] = jnp.broadcast_to(projection[None], sent.shape)


def tilde_and_projection(gathered, partner_rows, guess, panel, receivers):
    return pl.pallas_call(
        tilde_kernel,
        out_shape=(
            jax.ShapeDtypeStruct(guess.shape, jnp.float32),
            jax.ShapeDtypeStruct((receivers, 1, panel.shape[1]), jnp.float32),
        ),
        in_specs=[WHOLE] * 4,
        out_specs=(WHOLE,) * 2,
        compiler_params=SMALL,
        cost_estimate=pl.CostEstimate(flops=9_000_000, bytes_accessed=900_000, transcendentals=0),
        name="tilde",
    )(gathered, partner_rows, guess, panel)


def small_inverse(block):
    size = len(block)
    left = [list(row) for row in block]
    unit = [[None] * size for _ in range(size)]
    reciprocals = []
    for a in range(size):
        reciprocal = 1.0 / left[a][a]
        reciprocals.append(reciprocal)
        for row in range(a + 1, size):
            factor = left[row][a] * reciprocal
            for column in range(a + 1, row + 1):
                left[row][column] = left[row][column] - factor * left[column][a]
            for column in range(a):
                known = unit[row][column]
                change = factor * unit[a][column]
                unit[row][column] = -change if known is None else known - change
            unit[row][a] = -factor
    return unit, reciprocals


def column_of(entries):
    sub = lax.broadcasted_iota(jnp.int32, (SUBS, LANES), 0)
    column = jnp.zeros((SUBS, LANES), jnp.float32)
    for row, entry in enumerate(entries):
        if entry is not None:
            column = jnp.where(sub == row, entry, column)
    return column


def inverse_factor(tiles):
    shape = (SUBS, LANES)
    lane = lax.broadcasted_iota(jnp.int32, shape, 1)
    sub = lax.broadcasted_iota(jnp.int32, shape, 0)
    tiles = list(tiles)
    done = []
    for home in range(len(tiles)):
        first = home * SUBS
        columns = [
            [
                jnp.broadcast_to(tile[:, first + b : first + b + 1], shape)
                for b in range(SUBS)
            ]
            for tile in tiles[home:]
        ]
        block = [
            [jnp.broadcast_to(columns[0][b][a : a + 1], shape) for b in range(a + 1)]
            for a in range(SUBS)
        ]
        panel = (lane >= first) & (lane < first + SUBS)
        own = jnp.where(panel, jnp.where(lane - first == sub, 1.0, 0.0), tiles[home])
        lines = [jnp.broadcast_to(own[a : a + 1], shape) for a in range(SUBS)]
        unit, reciprocals = small_inverse(block)
        result = own
        for b in range(SUBS - 1):
            result = result + column_of([unit[a][b] for a in range(SUBS)]) * lines[b]
        roots = jnp.sqrt(column_of(reciprocals))
        done.append(jnp.where(lane <= sub + first, result, 0.0) * roots)
        if home + 1 == len(tiles):
            break
        answers = [
            jnp.broadcast_to(result[a : a + 1], shape) * reciprocals[a] for a in range(SUBS)
        ]
        for index in range(home + 1, len(tiles)):
            tile = jnp.where(panel, 0.0, tiles[index])
            raw = columns[index - home]
            parts = []
            for a in range(SUBS):
                factor = raw[a]
                for b in range(a):
                    factor = factor + unit[a][b] * raw[b]
                parts.append(factor * answers[a])
            while len(parts) > 1:
                parts = [one + two for one, two in zip(parts[::2], parts[1::2])]
            tiles[index] = tile - parts[0]
    return done


def factor_kernel(total_rows, gathered, panel, inverse_out, basis):
    slabs, rows, _ = gathered.shape
    tiles = [
        gathered[slab, pl.ds(first, SUBS), :]
        for slab in range(slabs)
        for first in range(0, rows - SUBS, SUBS)
    ]
    inverse = jnp.concatenate(inverse_factor(tiles), axis=0)
    inverse_out[...] = inverse
    basis[...] = lax.dot_general(
        panel[...],
        inverse * math.sqrt(total_rows),
        (((1,), (1,)), ((), ())),
        precision=HIGHEST,
        preferred_element_type=jnp.float32,
    )


def factor_and_basis(total_rows, gathered, panel):
    columns = panel.shape[1]
    return pl.pallas_call(
        functools.partial(factor_kernel, total_rows),
        out_shape=(
            jax.ShapeDtypeStruct((columns, columns), jnp.float32),
            jax.ShapeDtypeStruct(panel.shape, jnp.float32),
        ),
        in_specs=[WHOLE] * 2,
        out_specs=(WHOLE,) * 2,
        compiler_params=SMALL,
        cost_estimate=pl.CostEstimate(flops=30_000_000, bytes_accessed=9_000_000, transcendentals=0),
        name="factor",
    )(gathered, panel)


def update_kernel(parts, inverse, changes, tilde, guess):
    projection = jnp.sum(parts[...], axis=0)
    across = (((1,), (1,)), ((), ()))
    half = lax.dot_general(
        projection, inverse[...], across, precision=HIGHEST, preferred_element_type=jnp.float32
    )
    coefficients = -jnp.dot(
        half, inverse[...], precision=HIGHEST, preferred_element_type=jnp.float32
    )
    guess[...] = tilde[...] + lax.dot_general(
        coefficients,
        changes[...],
        across,
        precision=HIGHEST,
        preferred_element_type=jnp.float32,
    )


def update(parts, inverse, changes, tilde):
    return pl.pallas_call(
        update_kernel,
        out_shape=jax.ShapeDtypeStruct(tilde.shape, jnp.float32),
        in_specs=[WHOLE] * 4,
        out_specs=WHOLE,
        compiler_params=SMALL,
        cost_estimate=pl.CostEstimate(flops=9_000_000, bytes_accessed=400_000, transcendentals=0),
        name="update",
    )(parts, inverse, changes, tilde)


def shards(
    thermal_state,
    thermal_spreading_rate,
    flow_speed_vector,
    interface_guess,
    partner_facing_rows,
    mismatch_change_matrix,
    output_change_matrix,
):
    state = thermal_state[0]
    spread = thermal_spreading_rate[0]
    flow = flow_speed_vector[:, 0]
    panel = mismatch_change_matrix[0]
    state, spread, flow = (
        pltpu.with_memory_space_constraint(value, pltpu.HBM) for value in (state, spread, flow)
    )
    slabs = lax.axis_size("slab")
    wide = lax.axis_size("half") * lax.axis_size("pair")

    everyone = ("half", "pair", "slab")
    onward = [(i, i + 1) for i in range(slabs - 1)]
    back = [(i + 1, i) for i in range(slabs - 1)]

    gram = local_gram(panel).reshape(slabs, -1, panel.shape[1])
    gram, early_guess = lax.optimization_barrier((gram, interface_guess))
    right, left = pack(state, spread, flow, early_guess)
    gram_parts = lax.all_to_all(gram, "slab", 0, 0, tiled=True)
    right, left, gram_parts = lax.optimization_barrier((right, left, gram_parts))
    from_left = lax.ppermute(right, "slab", onward)
    from_right = lax.ppermute(left, "slab", back)
    gram_parts = lax.all_to_all(
        sum_and_copy("sum_slab", wide, gram_parts), ("half", "pair"), 0, 0, tiled=True
    )
    temperature, face = field_and_face(
        state, spread, flow, interface_guess, from_left, from_right
    )
    face = lax.ppermute(face, "half", [(0, 1), (1, 0)])
    gathered = lax.all_to_all(
        sum_and_copy("sum_wide", slabs, gram_parts, face), "slab", 0, 0, tiled=True
    )
    tilde, share = tilde_and_projection(
        gathered, partner_facing_rows, interface_guess, panel, slabs * wide
    )
    share = lax.all_to_all(share, everyone, 0, 0, tiled=True)
    inverse, basis = factor_and_basis(panel.shape[0] * slabs * wide, gathered, panel)
    updated = update(share, inverse, output_change_matrix[0], tilde)
    return temperature[None], updated, basis[None]


def solution(mesh):
    wide, slab = mesh.shape["wide"], mesh.shape["slab"]
    fine = Mesh(mesh.devices.reshape(2, wide // 2, slab), ("half", "pair", "slab"))
    parts = ("half", "pair")
    return jax.shard_map(
        shards,
        mesh=fine,
        in_specs=(
            P(parts, "slab", None, None),
            P(parts, "slab", None, None),
            P(None, parts, "slab", None, None),
            P(parts, "slab"),
            P(parts, "slab"),
            P(parts, "slab", None),
            P(parts, "slab", None),
        ),
        out_specs=(P(parts, "slab", None, None), P(parts, "slab"), P(parts, "slab", None)),
        check_vma=False,
    )
```

time: 103 us -> 92.7 us (0.900)
  waiting for transfers between devices: 0.97 us -> 12.5 us
  blocking collectives: 20.1 us -> 8.84 us
  Pallas kernels: 37.2 us -> 27.2 us
  starting transfers between devices: 41.5 us -> 40.3 us
    pallas_call x3 -> x2, Pallas kernels: 27.7 us -> 17.1 us  [the longest x1 13.8 us: field_and_face(): pl.pallas_call(field_kernel, out_shape=(jax.ShapeDtypeStruct(state.shape,...]
    all_to_all x1 -> x0, blocking collectives: 10.2 us -> none  [shards(): gram_parts = lax.all_to_all(gram, 'slab', 0, 0, tiled=True)]
    ppermute x4 -> x2, starting transfers between devices: 13.4 us -> 5.45 us  [the longest x1 3.53 us: shards(): from_left = lax.ppermute(right, 'slab', onward)]
    all_to_all x1, waiting for transfers between devices: 0.01 us -> 7.4 us  [shards(): share = lax.all_to_all(share, everyone, 0, 0, tiled=True)]
    all_to_all x0 -> x1, starting transfers between devices: none -> 6.49 us  [shards(): gram_parts = lax.all_to_all(gram, 'slab', 0, 0, tiled=True)]
    ppermute x4 -> x2, waiting for transfers between devices: 0.01 us -> 4.13 us  [the longest x1 4.13 us: shards(): from_right = lax.ppermute(left, 'slab', back)]
    unnamed x12 -> x14, local copies, waits for them, and re-layouts: 1.6 us -> 2.61 us
  transfers between devices with their start and end apart: 7 -> 6, of which waited for: 1 -> 3; matrix products, arithmetic and copies ran while one was open for 0% -> 0% of each run, Pallas kernels for 31% -> 25%
where the time goes in v4:
time: 92.7 us; the launch traced here: 92.3 us
  starting transfers between devices  40.3 us (43%)
  Pallas kernels  27.2 us (29%)
  waiting for transfers between devices  12.5 us (13%)
  blocking collectives  8.84 us (10%)
  local copies, waits for them, and re-layouts  2.61 us (3%)
    pallas_call x1, Pallas kernels, field_and_face(): pl.pallas_call(field_kernel, out_shape=(jax.ShapeDtypeStruct(state.shape,...  13.8 us
    all_to_all x1, starting transfers between devices, shards(): share = lax.all_to_all(share, everyone, 0, 0, tiled=True)  11.6 us
    all_to_all x1, starting transfers between devices, shards(): lax.all_to_all(sum_and_copy('sum_slab', wide, gram_parts), ('half', 'pair...  10.5 us
    all_to_all x1, blocking collectives, shards(): lax.all_to_all(sum_and_copy('sum_wide', slabs, gram_parts, face), 'slab',...  8.84 us
    all_to_all x1, waiting for transfers between devices, shards(): share = lax.all_to_all(share, everyone, 0, 0, tiled=True)  7.4 us
    all_to_all x1, starting transfers between devices, shards(): gram_parts = lax.all_to_all(gram, 'slab', 0, 0, tiled=True)  6.49 us
    ppermute x1, starting transfers between devices, shards(): face = lax.ppermute(face, 'half', [(0, 1), (1, 0)])  6.29 us
    pallas_call x1, Pallas kernels, factor_and_basis(): pl.pallas_call(functools.partial(factor_kernel, total_rows), out_shape=(j...  5.58 us
  transfers between devices with their start and end apart: 6, of which 3 were waited for; matrix products, arithmetic and copies ran while one was open for 0% of the time, Pallas kernels for 25%

profile of v4, /device:TPU:1, one launch (start us, length us, event | category | flops | bytes accessed | tf_op | source)
XLA Modules:
  0.0 92.3 jit_solution(13343002792105005092)
XLA Ops:
  0.6 0.0 copy-start
  0.6 0.9 copy-done
  1.5 0.9 %gram.1 = f32[128,128]{1,0:T(8,128)} custom-call(f32[256,128]{1,0:T(8,128)S(1)} %bitcast.8), custom_call_target="tpu_custom_call" | custom-call | flops 9000000 | bytes 200000 | tf_op jit(solution)/shard_map/gram/pallas_call | solution.py:402
  2.5 6.5 %all-to-all-start = ((f32[8,16,128]{2,1,0:T(8,128)}), f32[8,16,128]{2,1,0:T(8,128)S(1)}, u32[]{:S(2)}, u32[]{:S(2)}) async-start(f32[8,16,128]{2,1,0:T(8,128)} %bitcast.4), calls=%async_computation | async-start | bytes 131072 | tf_op jit(solution)/shard_map/all_to_all | solution.py:648
  9.0 0.7 copy-done.3
  9.7 3.3 %pack_edges.1 = (bf16[17,32,1024]{2,1,0:T(8,128)(2,1)}, bf16[17,32,1024]{2,1,0:T(8,128)(2,1)S(1)}) custom-call(f32[16,32,1024]{2,1,0:T(8,128)} %bitcast.14, bf16[16,32,1024]{2,1,0:T(8,128)(2,1)} %bitcast.16, bf16[3,16,32,1024]{3,2,1,0:T(8,128)(2,1)} %bitcast.12, f32[1,256]{1,0:T(1,128)S(1)} %copy-done.3), custom_call_target="tpu_custom_call" | custom-call | flops 2000000 | bytes 9000000 | tf_op jit(solution)/shard_map/pack_edges/pallas_call | solution.py:103
  12.9 0.0 copy-start.6
  13.0 1.0 %copy-done.6 = bf16[17,32,1024]{2,1,0:T(8,128)(2,1)} copy-done((bf16[17,32,1024]{2,1,0:T(8,128)(2,1)}, bf16[17,32,1024]{2,1,0:T(8,128)(2,1)S(1)}, u32[]{:S(2)}) %copy-start.6) | copy-done | bytes 1114136
  14.0 0.0 all-to-all-done.parts
  14.0 3.5 %collective-permute-start = (bf16[17,32,1024]{2,1,0:T(8,128)(2,1)}, bf16[17,32,1024]{2,1,0:T(8,128)(2,1)S(1)}, u32[]{:S(2)}, u32[]{:S(2)}) collective-permute-start(bf16[17,32,1024]{2,1,0:T(8,128)(2,1)} %get-tuple-element.20), channel_id=1, source_target_pairs={{0,1},{1,2},{2,3},{3,4},{4,5},{5,6},{6,7},{8,9},{9,10},{10,11},{11... | collective-permute-start | bytes 3342344 | tf_op jit(solution)/shard_map/ppermute | solution.py:650
  17.5 1.9 %collective-permute-start.1 = (bf16[17,32,1024]{2,1,0:T(8,128)(2,1)}, bf16[17,32,1024]{2,1,0:T(8,128)(2,1)S(1)}, u32[]{:S(2)}, u32[]{:S(2)}) collective-permute-start(bf16[17,32,1024]{2,1,0:T(8,128)(2,1)} %copy-done.6), channel_id=1, source_target_pairs={{1,0},{2,1},{3,2},{4,3},{5,4},{6,5},{7,6},{9,8},{10,9},{11,10},{12... | collective-permute-start | bytes 3342344 | tf_op jit(solution)/shard_map/ppermute | solution.py:651
  19.4 0.7 sum_slab.1
  20.2 10.5 %all-to-all-start.1 = ((f32[32,16,128]{2,1,0:T(8,128)}), f32[32,16,128]{2,1,0:T(8,128)S(1)}, u32[]{:S(2)}, u32[]{:S(2)}) async-start(f32[32,16,128]{2,1,0:T(8,128)} %sum_slab.1), calls=%async_computation.1 | async-start | bytes 524288 | tf_op jit(solution)/shard_map/all_to_all | solution.py:652
  30.7 0.0 copy-start.1
  30.7 0.0 copy-start.5
  30.7 0.0 collective-permute-done.left
  30.7 4.1 %collective-permute-done.1.right = bf16[17,32,1024]{2,1,0:T(8,128)(2,1)S(1)} collective-permute-done((bf16[17,32,1024]{2,1,0:T(8,128)(2,1)}, bf16[17,32,1024]{2,1,0:T(8,128)(2,1)S(1)}, u32[]{:S(2)}, u32[]{:S(2)}) %collective-permute-start.1) | collective-permute-done | bytes 1114144 | tf_op jit(solution)/shard_map/ppermute | solution.py:651
  34.8 0.0 copy-done.4
  34.8 13.8 %field.1 = (f32[16,32,1024]{2,1,0:T(8,128)}, f32[2,128]{1,0:T(2,128)S(1)}) custom-call(f32[16,32,1024]{2,1,0:T(8,128)} %bitcast.15, bf16[16,32,1024]{2,1,0:T(8,128)(2,1)} %bitcast.17, bf16[3,16,32,1024]{3,2,1,0:T(8,128)(2,1)} %bitcast.13, f32[1,256]{1,0:T(1,128)S(1)} %copy-done.4, bf16[17,32,1024]{2,1,0:T(8,128)(2,1)S(1)} %collective-permute-done.left, ...), custom_call_target="tpu_custom_call" | custom-call | flops 80000000 | bytes 30000000 | tf_op jit(solution)/shard_map/field/pallas_call | solution.py:364
  48.7 0.0 copy-start.2
  48.7 6.3 %collective-permute-start.2 = (f32[2,128]{1,0:T(2,128)S(1)}, f32[2,128]{1,0:T(2,128)S(1)}, u32[]{:S(2)}, u32[]{:S(2)}) collective-permute-start(f32[2,128]{1,0:T(2,128)S(1)} %get-tuple-element.24), channel_id=1, source_target_pairs={{0,128},{128,0},{1,129},{129,1},{2,130},{130,2},{3,131},{131,3},{4... | collective-permute-start | bytes 3080 | tf_op jit(solution)/shard_map/ppermute | solution.py:658
  55.0 0.0 all-to-all-done.1.parts
  55.0 1.0 %collective-permute-done.2.rest_0_ = f32[2,128]{1,0:T(2,128)S(1)} collective-permute-done((f32[2,128]{1,0:T(2,128)S(1)}, f32[2,128]{1,0:T(2,128)S(1)}, u32[]{:S(2)}, u32[]{:S(2)}) %collective-permute-start.2) | collective-permute-done | bytes 1056 | tf_op jit(solution)/shard_map/ppermute | solution.py:658
  56.0 8.8 %all_to_all.20.gathered = f32[8,24,128]{2,1,0:T(8,128)S(1)} all-to-all(f32[8,24,128]{2,1,0:T(8,128)S(1)} %sum_wide.1), channel_id=1, replica_groups=mesh['half'=2,'pair'=16,'slab'=8] {'slab'}, dimensions={0} | all-to-all | bytes 196608 | tf_op jit(solution)/shard_map/all_to_all | solution.py:659
  64.8 0.0 copy-done.1
  64.8 0.0 copy-done.5
  64.8 1.3 %tilde.1 = (f32[1,256]{1,0:T(1,128)S(1)}, f32[256,1,128]{2,1,0:T(1,128)}) custom-call(f32[8,24,128]{2,1,0:T(8,128)S(1)} %all_to_all.20.gathered, s32[1,256]{1,0:T(1,128)S(1)} %copy-done.5, f32[1,256]{1,0:T(1,128)S(1)} %copy-done.4, f32[256,128]{1,0:T(8,128)S(1)} %bitcast.9), custom_call_target="tpu_custom_call" | custom-call | flops 9000000 | bytes 900000 | tf_op jit(solution)/shard_map/tilde/pallas_call | solution.py:467
  66.1 11.6 %all-to-all-start.3 = ((f32[256,1,128]{2,1,0:T(1,128)}), f32[256,1,128]{2,1,0:T(1,128)S(1)}, u32[]{:S(2)}, u32[]{:S(2)}) async-start(f32[256,1,128]{2,1,0:T(1,128)} %get-tuple-element.25), calls=%async_computation.3 | async-start | bytes 262144 | tf_op jit(solution)/shard_map/all_to_all | solution.py:665
  77.7 5.6 %factor.1 = (f32[128,128]{1,0:T(8,128)S(1)}, f32[256,128]{1,0:T(8,128)}) custom-call(f32[8,24,128]{2,1,0:T(8,128)S(1)} %all_to_all.20.gathered, f32[256,128]{1,0:T(8,128)S(1)} %bitcast.10), custom_call_target="tpu_custom_call" | custom-call | flops 30000000 | bytes 9000000 | tf_op jit(solution)/shard_map/factor/pallas_call | solution.py:578
  83.3 7.4 %all-to-all-done.3.parts = f32[256,1,128]{2,1,0:T(1,128)S(1)} async-done(((f32[256,1,128]{2,1,0:T(1,128)}), f32[256,1,128]{2,1,0:T(1,128)S(1)}, u32[]{:S(2)}, u32[]{:S(2)}) %all-to-all-start.3) | async-done | bytes 131104 | tf_op jit(solution)/shard_map/all_to_all | solution.py:665
  90.7 0.0 copy-done.2
  90.7 1.6 %update.1 = f32[1,256]{1,0:T(1,128)} custom-call(f32[256,1,128]{2,1,0:T(1,128)S(1)} %all-to-all-done.3.parts, f32[128,128]{1,0:T(8,128)S(1)} %get-tuple-element.26.inverse, f32[256,128]{1,0:T(8,128)S(1)} %bitcast.11, f32[1,256]{1,0:T(1,128)S(1)} %get-tuple-element.27.tilde), custom_call_target="tpu_custom_call" | custom-call | flops 9000000 | bytes 400000 | tf_op jit(solution)/shard_map/update/pallas_call | solution.py:611
  (3 shorter events, 0.0 us)
Async XLA Ops:
  0.6 0.9 copy-start
  2.5 11.5 %all-to-all-start = ((f32[8,16,128]{2,1,0:T(8,128)}), f32[8,16,128]{2,1,0:T(8,128)S(1)}, u32[]{:S(2)}, u32[]{:S(2)}) async-start(f32[8,16,128]{2,1,0:T(8,128)} %bitcast.4), calls=%async_computation | async-start | bytes 131072 | tf_op jit(solution)/shard_map/all_to_all | solution.py:648
  9.0 0.7 copy-start.3
  9.7 25.2 %copy-start.4 = (f32[1,256]{1,0:T(1,128)S(1)}, f32[1,256]{1,0:T(1,128)}, u32[]{:S(2)}) copy-start(f32[1,256]{1,0:T(1,128)} %guess.4) | copy-start | bytes 3076
  12.9 1.0 %copy-start.6 = (bf16[17,32,1024]{2,1,0:T(8,128)(2,1)}, bf16[17,32,1024]{2,1,0:T(8,128)(2,1)S(1)}, u32[]{:S(2)}) copy-start(bf16[17,32,1024]{2,1,0:T(8,128)(2,1)S(1)} %get-tuple-element.21) | copy-start | bytes 3342340
  14.0 16.7 %collective-permute-start = (bf16[17,32,1024]{2,1,0:T(8,128)(2,1)}, bf16[17,32,1024]{2,1,0:T(8,128)(2,1)S(1)}, u32[]{:S(2)}, u32[]{:S(2)}) collective-permute-start(bf16[17,32,1024]{2,1,0:T(8,128)(2,1)} %get-tuple-element.20), channel_id=1, source_target_pairs={{0,1},{1,2},{2,3},{3,4},{4,5},{5,6},{6,7},{8,9},{9,10},{10,11},{11... | collective-permute-start | bytes 3342344 | tf_op jit(solution)/shard_map/ppermute | solution.py:650
  17.5 17.3 %collective-permute-start.1 = (bf16[17,32,1024]{2,1,0:T(8,128)(2,1)}, bf16[17,32,1024]{2,1,0:T(8,128)(2,1)S(1)}, u32[]{:S(2)}, u32[]{:S(2)}) collective-permute-start(bf16[17,32,1024]{2,1,0:T(8,128)(2,1)} %copy-done.6), channel_id=1, source_target_pairs={{1,0},{2,1},{3,2},{4,3},{5,4},{6,5},{7,6},{9,8},{10,9},{11,10},{12... | collective-permute-start | bytes 3342344 | tf_op jit(solution)/shard_map/ppermute | solution.py:651
  20.2 34.8 %all-to-all-start.1 = ((f32[32,16,128]{2,1,0:T(8,128)}), f32[32,16,128]{2,1,0:T(8,128)S(1)}, u32[]{:S(2)}, u32[]{:S(2)}) async-start(f32[32,16,128]{2,1,0:T(8,128)} %sum_slab.1), calls=%async_computation.1 | async-start | bytes 524288 | tf_op jit(solution)/shard_map/all_to_all | solution.py:652
  30.7 34.1 %copy-start.1 = (f32[1,256,128]{2,1,0:T(8,128)S(1)}, f32[1,256,128]{2,1,0:T(8,128)}, u32[]{:S(2)}) copy-start(f32[1,256,128]{2,1,0:T(8,128)} %param.12) | copy-start | bytes 393220
  30.7 34.1 %copy-start.5 = (s32[1,256]{1,0:T(1,128)S(1)}, s32[1,256]{1,0:T(1,128)}, u32[]{:S(2)}) copy-start(s32[1,256]{1,0:T(1,128)} %partner_rows.1) | copy-start | bytes 3076
  48.7 42.0 %copy-start.2 = (f32[1,256,128]{2,1,0:T(8,128)S(1)}, f32[1,256,128]{2,1,0:T(8,128)}, u32[]{:S(2)}) copy-start(f32[1,256,128]{2,1,0:T(8,128)} %param.13) | copy-start | bytes 393220
  48.7 7.2 %collective-permute-start.2 = (f32[2,128]{1,0:T(2,128)S(1)}, f32[2,128]{1,0:T(2,128)S(1)}, u32[]{:S(2)}, u32[]{:S(2)}) collective-permute-start(f32[2,128]{1,0:T(2,128)S(1)} %get-tuple-element.24), channel_id=1, source_target_pairs={{0,128},{128,0},{1,129},{129,1},{2,130},{130,2},{3,131},{131,3},{4... | collective-permute-start | bytes 3080 | tf_op jit(solution)/shard_map/ppermute | solution.py:658
  66.1 24.6 %all-to-all-start.3 = ((f32[256,1,128]{2,1,0:T(1,128)}), f32[256,1,128]{2,1,0:T(1,128)S(1)}, u32[]{:S(2)}, u32[]{:S(2)}) async-start(f32[256,1,128]{2,1,0:T(1,128)} %get-tuple-element.25), calls=%async_computation.3 | async-start | bytes 262144 | tf_op jit(solution)/shard_map/all_to_all | solution.py:665

commit v5 on v4

--- a/solution.py
+++ b/solution.py
@@ -17,7 +17,7 @@
 SUBS = 8
 REACH = SWEEPS
 COEF_REACH = SWEEPS - 1
-FINE = 0
+FINE = 1
 FIELDS = 4
 SLOTS = REACH + FINE + FIELDS * COEF_REACH
 HIGHEST = lax.Precision.HIGHEST
@@ -47,7 +47,9 @@
     return row
 
 
-def pack_kernel(state, spread, flow, guess, right, left, planes, sems):
+def pack_kernel(
+    state, spread, flow, guess, right_out, left_out, right, left, planes, sems
+):
     count = state.shape[0]
     lane_blocks = state.shape[2] // LANES
     per_plane = guess.shape[1] // count
@@ -96,16 +98,24 @@
                 rest = value - lead.astype(jnp.float32)
                 out[REACH + plane - fine_first] = rest.astype(jnp.bfloat16)
     wait_all(started)
+    pushes = [
+        pltpu.make_async_copy(right, right_out, sems.at[8]),
+        pltpu.make_async_copy(left, left_out, sems.at[9]),
+    ]
+    start_all(pushes)
+    wait_all(pushes)
 
 
 def pack(state, spread, flow, guess):
     message = jax.ShapeDtypeStruct((SLOTS + 1, *state.shape[1:]), jnp.bfloat16)
     return pl.pallas_call(
         pack_kernel,
-        out_shape=(message, message),
+        out_shape=(pltpu.HBM(message.shape, message.dtype),) * 2,
         in_specs=[ANY, ANY, ANY, SCALARS],
-        out_specs=(WHOLE,) * 2,
+        out_specs=(pl.BlockSpec(memory_space=pltpu.HBM),) * 2,
         scratch_shapes=[
+            pltpu.VMEM(message.shape, message.dtype),
+            pltpu.VMEM(message.shape, message.dtype),
             pltpu.VMEM((2, REACH, *state.shape[1:]), jnp.float32),
             pltpu.SemaphoreType.DMA((10,)),
         ],
@@ -150,7 +160,7 @@
 UNROLL = 2
 
 
-def sweep(source, target, coefs, held, height, first, stop):
+def sweep(source, target, coefs, held, height, first, stop, shift=0):
     lane_blocks = source.shape[1]
     lane = lax.broadcasted_iota(jnp.int32, (SUBS, LANES), 1)
     zero = jnp.zeros((SUBS, LANES), jnp.float32)
@@ -197,7 +207,7 @@
                             packed = pl.ds(tile * SUBS - half, PACKED)
                             lanes = pl.ds(block * LANES, LANES)
                             kept[key] = [
-                                coefs[field, plane - 1, packed, lanes].astype(jnp.float32)
+                                coefs(field, plane, packed, lanes).astype(jnp.float32)
                                 for field in range(FIELDS)
                             ]
                         mode = FIELDS if held is None else held.shape[0]
@@ -210,39 +220,38 @@
                     if len(target.shape) == 4:
                         target[plane, block, pl.ds(FLOOR + tile * SUBS, SUBS), :] = value
                     else:
-                        target[plane - REACH, rows, pl.ds(block * LANES, LANES)] = value
+                        target[plane - shift, rows, pl.ds(block * LANES, LANES)] = value
         return carry
 
     assert (stop - first) % UNROLL == 0
     lax.fori_loop(0, (stop - first) // UNROLL, pair, 0)
 
 
-def set_rims(grids, guess, count, height):
-    per_plane = guess.shape[1] // count
+def set_rims(grids, guess, per_plane, spots, height):
     for grid in grids:
         for block in range(grid.shape[1]):
             grid[:, block, pl.ds(0, FLOOR), :] = jnp.zeros(
                 (grid.shape[0], FLOOR, LANES), jnp.float32
             )
-    for plane in range(count):
+    for at, plane in spots:
         for block in range(grids[0].shape[1]):
             line = ghost_line(guess, plane * per_plane, block)
             for grid in grids:
-                grid[REACH + plane, block, pl.ds(FLOOR + height, 1), :] = line
-
-
-def set_edges(grids, parts, count, height):
-    for side, first, fine_first in ((0, 0, REACH - FINE), (1, REACH + count, 0)):
+                grid[at, block, pl.ds(FLOOR + height, 1), :] = line
+
+
+def set_edges(grids, parts, right_first, height):
+    for side, first, fine_first in ((0, 0, REACH - FINE), (1, right_first, 0)):
         near = first + REACH - COEF_REACH if side == 0 else first
         for block in range(grids[0].shape[1]):
             lanes = pl.ds(block * LANES, LANES)
             for plane in range(REACH):
-                value = parts[side, plane, :, lanes].astype(jnp.float32)
+                value = parts[side][plane, :, lanes].astype(jnp.float32)
                 if fine_first <= plane < fine_first + FINE:
-                    rest = parts[side, REACH + plane - fine_first, :, lanes]
+                    rest = parts[side][REACH + plane - fine_first, :, lanes]
                     value = value + rest.astype(jnp.float32)
                 grids[0][first + plane, block, pl.ds(FLOOR, height), :] = value
-            tail = parts[side, REACH + FINE, pl.ds(0, PACKED), lanes].astype(jnp.float32)
+            tail = parts[side][SLOTS, pl.ds(0, PACKED), lanes].astype(jnp.float32)
             for plane in range(COEF_REACH):
                 row = tail[plane : plane + 1]
                 for part in (1, 2):
@@ -252,20 +261,27 @@
                     grid[near + plane, block, pl.ds(FLOOR + height, 1), :] = row
 
 
-def face_means(last, face, count, height):
-    lane_blocks = last.shape[2] // LANES
+def set_plane(grid, at, plain, plane, height):
+    for block in range(grid.shape[1]):
+        grid[at, block, pl.ds(FLOOR, height), :] = plain[plane, :, pl.ds(block * LANES, LANES)]
+
+
+def strip_means(last, first, count):
     lane = lax.broadcasted_iota(jnp.int32, (count, LANES), 1)
     means = jnp.zeros((count, LANES), jnp.float32)
     strips = LANES // INTERFACE_STRIP
-    for block in range(lane_blocks):
-        top = last[:, height - 1, pl.ds(block * LANES, LANES)]
+    for block in range(last.shape[2] // LANES):
+        top = last[pl.ds(first, count), last.shape[1] - 1, pl.ds(block * LANES, LANES)]
         for strip in range(strips):
             mine = (lane >= strip * INTERFACE_STRIP) & (lane < (strip + 1) * INTERFACE_STRIP)
             total = jnp.sum(jnp.where(mine, top, 0.0), axis=1, keepdims=True)
             means = jnp.where(lane == block * strips + strip, total / INTERFACE_STRIP, means)
+    return means
+
+
+def set_face(means, face, across):
     line = lax.broadcasted_iota(jnp.int32, (LANES, LANES), 0)
     column = lax.broadcasted_iota(jnp.int32, (LANES, LANES), 1)
-    across = lane_blocks * strips
     spread_out = jnp.dot(
         means,
         jnp.where(column % across == line, 1.0, 0.0),
@@ -280,110 +296,194 @@
         face[row] = jnp.sum(jnp.where(plane == spot, mine, 0.0), axis=0)
 
 
-HELD = 4
-
-
-def field_kernel(
-    state, spread, flow, guess, left, right, out, face, grid, other, plain, coefs, parts, *rest
+def inner_kernel(
+    state, spread, flow, guess, out, edges, means, grid, other, plain, begin, rates, held, sems
 ):
-    *held, sems = rest
-    held = held[0] if held else None
+    count, height = state.shape[0], state.shape[1]
+    fetch = pltpu.make_async_copy(state, begin, sems.at[0])
+    later = pltpu.make_async_copy(spread, rates, sems.at[1])
+    fetch.start()
+    later.start()
+
+    def coefs(field, plane, rows, lanes):
+        if field == 0:
+            return rates[plane, rows, lanes]
+        return flow[field - 1, plane, rows, lanes]
+
+    spots = [(plane, plane) for plane in range(count)]
+    set_rims((grid, other), guess, guess.shape[1] // count, spots, height)
+    fetch.wait()
+    for plane in range(count):
+        set_plane(grid, plane, begin, plane, height)
+    later.wait()
+    pair = (grid, other)
+    for step in range(1, SWEEPS):
+        target = pair[step % 2]
+        sweep(
+            pair[(step + 1) % 2],
+            target,
+            coefs if step == 1 else None,
+            held,
+            height,
+            step,
+            count - step,
+        )
+        for index, plane in enumerate((step, step + 1, count - 2 - step, count - 1 - step)):
+            edges[step - 1, index] = target[plane, :, pl.ds(FLOOR, height), :]
+    source = pair[(SWEEPS + 1) % 2]
+    sweep(source, plain, None, held, height, SWEEPS, count - SWEEPS, SWEEPS)
+    push = pltpu.make_async_copy(plain, out.at[pl.ds(SWEEPS, count - 2 * SWEEPS)], sems.at[0])
+    push.start()
+    means[...] = strip_means(plain, 0, count - 2 * SWEEPS)
+    push.wait()
+
+
+def inner_field(state, spread, flow, guess):
+    count, height, depth = state.shape
+    lane_blocks = depth // LANES
+    grid = pltpu.VMEM((count, lane_blocks, FLOOR + height + SUBS, LANES), jnp.float32)
+    return pl.pallas_call(
+        inner_kernel,
+        out_shape=(
+            jax.ShapeDtypeStruct(state.shape, jnp.float32),
+            jax.ShapeDtypeStruct((SWEEPS - 1, 4, lane_blocks, height, LANES), jnp.float32),
+            jax.ShapeDtypeStruct((count - 2 * SWEEPS, LANES), jnp.float32),
+        ),
+        in_specs=[ANY, ANY, WHOLE, SCALARS],
+        out_specs=(pl.BlockSpec(memory_space=pltpu.HBM), WHOLE, WHOLE),
+        scratch_shapes=[
+            grid,
+            grid,
+            pltpu.VMEM((count - 2 * SWEEPS, height, depth), jnp.float32),
+            pltpu.VMEM(state.shape, jnp.float32),
+            pltpu.VMEM(spread.shape, spread.dtype),
+            pltpu.VMEM((FIELDS, count - 2, lane_blocks, height, LANES), jnp.float32),
+            pltpu.SemaphoreType.DMA((2,)),
+        ],
+        compiler_params=pltpu.CompilerParams(vmem_limit_bytes=24 * 2**20),
+        cost_estimate=pl.CostEstimate(
+            flops=50_000_000, bytes_accessed=20_000_000, transcendentals=0
+        ),
+        name="inner_field",
+    )(state, spread, flow, guess)
+
+
+def outer_kernel(
+    state,
+    spread,
+    flow,
+    guess,
+    left,
+    right,
+    begun,
+    edges,
+    means,
+    out,
+    face,
+    grid,
+    other,
+    plain,
+    begin,
+    rates,
+    held,
+    sems,
+):
     count, height = state.shape[0], state.shape[1]
     lane_blocks = grid.shape[1]
-    inner = pl.ds(COEF_REACH, count)
-    parted = pl.ds(0, REACH + FINE)
-    early = [
-        pltpu.make_async_copy(state, plain, sems.at[0]),
-        pltpu.make_async_copy(left.at[parted], parts.at[0, parted], sems.at[1]),
-        pltpu.make_async_copy(right.at[parted], parts.at[1, parted], sems.at[2]),
-        pltpu.make_async_copy(left.at[SLOTS], parts.at[0, REACH + FINE], sems.at[3]),
-        pltpu.make_async_copy(right.at[SLOTS], parts.at[1, REACH + FINE], sems.at[4]),
+    low, high = pl.ds(0, SWEEPS), pl.ds(SWEEPS, SWEEPS)
+    last = pl.ds(count - SWEEPS, SWEEPS)
+    fetch = [
+        pltpu.make_async_copy(spread.at[low], rates.at[low], sems.at[0]),
+        pltpu.make_async_copy(spread.at[last], rates.at[high], sems.at[1]),
+        pltpu.make_async_copy(state.at[pl.ds(0, 2)], begin.at[pl.ds(0, 2)], sems.at[2]),
+        pltpu.make_async_copy(state.at[pl.ds(count - 2, 2)], begin.at[pl.ds(2, 2)], sems.at[3]),
     ]
-    later = [pltpu.make_async_copy(spread, coefs.at[0, inner], sems.at[5])]
-    for axis in range(3):
-        later.append(
-            pltpu.make_async_copy(flow.at[axis], coefs.at[1 + axis, inner], sems.at[6 + axis])
+    start_all(fetch)
+
+    def hold(at, planes):
+        for block in range(lane_blocks):
+            lanes = pl.ds(block * LANES, LANES)
+            fields = [ref[(*spot, slice(None), lanes)].astype(jnp.float32) for ref, spot in planes]
+            for index, value in enumerate(weights_of(FIELDS, *fields)):
+                held[index, at, block] = value
+
+    for message, first in ((left, 0), (right, count - 1)):
+        for plane in range(COEF_REACH):
+            slots = [REACH + FINE + field * COEF_REACH + plane for field in range(FIELDS)]
+            hold(first + plane, [(message, (slot,)) for slot in slots])
+    spots = [(REACH + plane, plane) for plane in range(SWEEPS)]
+    spots += [(plane, plane) for plane in range(count - SWEEPS, count)]
+    set_rims((grid, other), guess, guess.shape[1] // count, spots, height)
+    set_edges((grid, other), (left, right), count, height)
+    wait_all(fetch)
+    for index, (at, plane) in enumerate(spots):
+        hold(at - 1, [(rates, (index,))] + [(flow, (axis, plane)) for axis in range(3)])
+    for plane in range(2):
+        set_plane(grid, REACH + plane, begin, plane, height)
+        set_plane(grid, count - 2 + plane, begin, 2 + plane, height)
+    pair = (grid, other)
+    for step in range(1, SWEEPS):
+        source, target = pair[(step + 1) % 2], pair[step % 2]
+        sweep(source, target, None, held, height, step, step + SWEEPS)
+        right_first = count + REACH - SWEEPS - step
+        sweep(source, target, None, held, height, right_first, right_first + SWEEPS)
+        spots = (REACH + step, REACH + step + 1, count - 2 - step, count - 1 - step)
+        for index, at in enumerate(spots):
+            target[at, :, pl.ds(FLOOR, height), :] = edges[step - 1, index]
+    source = pair[(SWEEPS + 1) % 2]
+    pushes = []
+    for index, first in enumerate((SWEEPS, count - SWEEPS)):
+        kept = index * SWEEPS
+        sweep(source, plain, None, held, height, first, first + SWEEPS, first - kept)
+        final = 0 if index == 0 else count - SWEEPS
+        pushes.append(
+            pltpu.make_async_copy(
+                plain.at[pl.ds(kept, SWEEPS)], out.at[pl.ds(final, SWEEPS)], sems.at[index]
+            )
         )
-    for side, message, first in ((0, left, 0), (1, right, COEF_REACH + count)):
-        for field in range(FIELDS):
-            later.append(
-                pltpu.make_async_copy(
-                    message.at[pl.ds(REACH + FINE + field * COEF_REACH, COEF_REACH)],
-                    coefs.at[field, pl.ds(first, COEF_REACH)],
-                    sems.at[9 + side * FIELDS + field],
-                )
-            )
-    start_all(early)
-    start_all(later)
-    set_rims((grid, other), guess, count, height)
-    wait_all(early)
-    set_edges((grid, other), parts, count, height)
-    for plane in range(count):
-        for block in range(lane_blocks):
-            grid[REACH + plane, block, pl.ds(FLOOR, height), :] = plain[
-                plane, :, pl.ds(block * LANES, LANES)
-            ]
-    wait_all(later)
-    pair = (grid, other)
-    for step in range(SWEEPS - 1):
-        sweep(
-            pair[step % 2],
-            pair[(step + 1) % 2],
-            None if step and held is not None else coefs,
-            held,
-            height,
-            step + 1,
-            count + 2 * REACH - 1 - step,
-        )
-    pushes = []
-    pieces = 2
-    for piece in range(pieces):
-        first = piece * count // pieces
-        planes = pl.ds(first, count // pieces)
-        sweep(
-            pair[(SWEEPS - 1) % 2],
-            plain,
-            None if held is not None else coefs,
-            held,
-            height,
-            REACH + first,
-            REACH + first + count // pieces,
-        )
-        pushes.append(pltpu.make_async_copy(plain.at[planes], out.at[planes], sems.at[piece]))
         pushes[-1].start()
-    face_means(plain, face, count, height)
+    whole = [strip_means(plain, 0, SWEEPS), means[...], strip_means(plain, SWEEPS, SWEEPS)]
+    set_face(jnp.concatenate(whole, axis=0), face, state.shape[2] // INTERFACE_STRIP)
     wait_all(pushes)
 
 
-def field_and_face(state, spread, flow, guess, left, right):
+def outer_field(state, spread, flow, guess, left, right, begun, edges, means):
     count, height, depth = state.shape
-    extended = count + 2 * REACH
     lane_blocks = depth // LANES
-    tall = FLOOR + height + SUBS
-    held = [pltpu.VMEM((HELD, extended - 2, lane_blocks, height, LANES), jnp.float32)]
+    extended = count + REACH
+    grid = pltpu.VMEM((extended, lane_blocks, FLOOR + height + SUBS, LANES), jnp.float32)
     return pl.pallas_call(
-        field_kernel,
+        outer_kernel,
         out_shape=(
             jax.ShapeDtypeStruct(state.shape, jnp.float32),
             jax.ShapeDtypeStruct((guess.shape[1] // LANES, LANES), jnp.float32),
         ),
-        in_specs=[ANY, ANY, ANY, SCALARS, ANY, ANY],
+        in_specs=[
+            ANY,
+            ANY,
+            WHOLE,
+            SCALARS,
+            *[WHOLE] * 2,
+            pl.BlockSpec(memory_space=pltpu.HBM),
+            *[WHOLE] * 2,
+        ],
         out_specs=(pl.BlockSpec(memory_space=pltpu.HBM), WHOLE),
+        input_output_aliases={6: 0},
         scratch_shapes=[
-            pltpu.VMEM((extended, lane_blocks, tall, LANES), jnp.float32),
-            pltpu.VMEM((extended, lane_blocks, tall, LANES), jnp.float32),
-            pltpu.VMEM(state.shape, jnp.float32),
-            pltpu.VMEM((FIELDS, extended - 2, height, depth), jnp.bfloat16),
-            pltpu.VMEM((2, REACH + FINE + 1, height, depth), jnp.bfloat16),
-            *(held if HELD else []),
-            pltpu.SemaphoreType.DMA((17,)),
+            grid,
+            grid,
+            pltpu.VMEM((2 * SWEEPS, height, depth), jnp.float32),
+            pltpu.VMEM((4, height, depth), jnp.float32),
+            pltpu.VMEM((2 * SWEEPS, height, depth), spread.dtype),
+            pltpu.VMEM((FIELDS, extended - 2, lane_blocks, height, LANES), jnp.float32),
+            pltpu.SemaphoreType.DMA((4,)),
         ],
-        compiler_params=pltpu.CompilerParams(vmem_limit_bytes=(24 + 3 * HELD) * 2**20),
+        compiler_params=pltpu.CompilerParams(vmem_limit_bytes=24 * 2**20),
         cost_estimate=pl.CostEstimate(
-            flops=80_000_000, bytes_accessed=30_000_000, transcendentals=0
+            flops=35_000_000, bytes_accessed=15_000_000, transcendentals=0
         ),
-        name="field",
-    )(state, spread, flow, guess, left, right)
+        name="outer_field",
+    )(state, spread, flow, guess, left, right, begun, edges, means)
 
 
 def gram_kernel(panel, gram):
@@ -555,7 +655,7 @@
     return done
 
 
-def factor_kernel(total_rows, gathered, panel, inverse_out, basis):
+def factor_kernel(total_rows, gathered, panel, changes, inverse_out, basis, turned):
     slabs, rows, _ = gathered.shape
     tiles = [
         gathered[slab, pl.ds(first, SUBS), :]
@@ -564,6 +664,13 @@
     ]
     inverse = jnp.concatenate(inverse_factor(tiles), axis=0)
     inverse_out[...] = inverse
+    turned[...] = lax.dot_general(
+        changes[...],
+        inverse,
+        (((1,), (1,)), ((), ())),
+        precision=HIGHEST,
+        preferred_element_type=jnp.float32,
+    )
     basis[...] = lax.dot_general(
         panel[...],
         inverse * math.sqrt(total_rows),
@@ -573,41 +680,35 @@
     )
 
 
-def factor_and_basis(total_rows, gathered, panel):
+def factor_and_basis(total_rows, gathered, panel, changes):
     columns = panel.shape[1]
     return pl.pallas_call(
         functools.partial(factor_kernel, total_rows),
         out_shape=(
             jax.ShapeDtypeStruct((columns, columns), jnp.float32),
             jax.ShapeDtypeStruct(panel.shape, jnp.float32),
+            jax.ShapeDtypeStruct(changes.shape, jnp.float32),
         ),
-        in_specs=[WHOLE] * 2,
-        out_specs=(WHOLE,) * 2,
+        in_specs=[WHOLE] * 3,
+        out_specs=(WHOLE,) * 3,
         compiler_params=SMALL,
         cost_estimate=pl.CostEstimate(flops=30_000_000, bytes_accessed=9_000_000, transcendentals=0),
         name="factor",
-    )(gathered, panel)
-
-
-def update_kernel(parts, inverse, changes, tilde, guess):
+    )(gathered, panel, changes)
+
+
+def update_kernel(parts, inverse, turned, tilde, guess):
     projection = jnp.sum(parts[...], axis=0)
     across = (((1,), (1,)), ((), ()))
     half = lax.dot_general(
         projection, inverse[...], across, precision=HIGHEST, preferred_element_type=jnp.float32
     )
-    coefficients = -jnp.dot(
-        half, inverse[...], precision=HIGHEST, preferred_element_type=jnp.float32
-    )
-    guess[...] = tilde[...] + lax.dot_general(
-        coefficients,
-        changes[...],
-        across,
-        precision=HIGHEST,
-        preferred_element_type=jnp.float32,
-    )
-
-
-def update(parts, inverse, changes, tilde):
+    guess[...] = tilde[...] - lax.dot_general(
+        half, turned[...], across, precision=HIGHEST, preferred_element_type=jnp.float32
+    )
+
+
+def update(parts, inverse, turned, tilde):
     return pl.pallas_call(
         update_kernel,
         out_shape=jax.ShapeDtypeStruct(tilde.shape, jnp.float32),
@@ -616,7 +717,7 @@
         compiler_params=SMALL,
         cost_estimate=pl.CostEstimate(flops=9_000_000, bytes_accessed=400_000, transcendentals=0),
         name="update",
-    )(parts, inverse, changes, tilde)
+    )(parts, inverse, turned, tilde)
 
 
 def shards(
@@ -632,9 +733,9 @@
     spread = thermal_spreading_rate[0]
     flow = flow_speed_vector[:, 0]
     panel = mismatch_change_matrix[0]
-    state, spread, flow = (
+    far = [
         pltpu.with_memory_space_constraint(value, pltpu.HBM) for value in (state, spread, flow)
-    )
+    ]
     slabs = lax.axis_size("slab")
     wide = lax.axis_size("half") * lax.axis_size("pair")
 
@@ -643,8 +744,8 @@
     back = [(i + 1, i) for i in range(slabs - 1)]
 
     gram = local_gram(panel).reshape(slabs, -1, panel.shape[1])
-    gram, early_guess = lax.optimization_barrier((gram, interface_guess))
-    right, left = pack(state, spread, flow, early_guess)
+    gram, far[1] = lax.optimization_barrier((gram, far[1]))
+    right, left = pack(*far, interface_guess)
     gram_parts = lax.all_to_all(gram, "slab", 0, 0, tiled=True)
     right, left, gram_parts = lax.optimization_barrier((right, left, gram_parts))
     from_left = lax.ppermute(right, "slab", onward)
@@ -652,8 +753,9 @@
     gram_parts = lax.all_to_all(
         sum_and_copy("sum_slab", wide, gram_parts), ("half", "pair"), 0, 0, tiled=True
     )
-    temperature, face = field_and_face(
-        state, spread, flow, interface_guess, from_left, from_right
+    begun, edges, means = inner_field(*far[:2], flow, interface_guess)
+    temperature, face = outer_field(
+        *far[:2], flow, interface_guess, from_left, from_right, begun, edges, means
     )
     face = lax.ppermute(face, "half", [(0, 1), (1, 0)])
     gathered = lax.all_to_all(
@@ -663,8 +765,10 @@
         gathered, partner_facing_rows, interface_guess, panel, slabs * wide
     )
     share = lax.all_to_all(share, everyone, 0, 0, tiled=True)
-    inverse, basis = factor_and_basis(panel.shape[0] * slabs * wide, gathered, panel)
-    updated = update(share, inverse, output_change_matrix[0], tilde)
+    inverse, basis, turned = factor_and_basis(
+        panel.shape[0] * slabs * wide, gathered, panel, output_change_matrix[0]
+    )
+    updated = update(share, inverse, turned, tilde)
     return temperature[None], updated, basis[None]
 
 

time: 92.7 us -> 93.3 us (level)
  waiting for transfers between devices: 12.5 us -> 7.73 us
  Pallas kernels: 27.2 us -> 31.8 us
  blocking collectives: 8.84 us -> 11.1 us
  starting transfers between devices: 40.3 us -> 39 us
    pallas_call x2 -> x3, Pallas kernels: 17.1 us -> 21.6 us  [the longest x1 9.33 us: inner_field(): pl.pallas_call(inner_kernel, out_shape=(jax.ShapeDtypeStruct(state.shape,...]
    ppermute x1, waiting for transfers between devices: 4.13 us -> 0.01 us  [shards(): from_right = lax.ppermute(left, 'slab', back)]
    all_to_all x1, blocking collectives: 8.84 us -> 11.1 us  [shards(): lax.all_to_all(sum_and_copy('sum_wide', slabs, gram_parts, face), 'slab',...]
    ppermute x1, starting transfers between devices: 6.29 us -> 5.23 us  [shards(): face = lax.ppermute(face, 'half', [(0, 1), (1, 0)])]
    all_to_all x1, waiting for transfers between devices: 7.4 us -> 6.34 us  [shards(): share = lax.all_to_all(share, everyone, 0, 0, tiled=True)]
  transfers between devices with their start and end apart: 6 -> 6, of which waited for: 3 -> 3; matrix products, arithmetic and copies ran while one was open for 0% -> 0% of each run, Pallas kernels for 25% -> 30%
where the time goes in v5:
time: 93.3 us; the launch traced here: 92.8 us
  starting transfers between devices  39 us (42%)
  Pallas kernels  31.8 us (34%)
  blocking collectives  11.1 us (12%)
  waiting for transfers between devices  7.73 us (8%)
  local copies, waits for them, and re-layouts  2.5 us (3%)
    all_to_all x1, starting transfers between devices, shards(): share = lax.all_to_all(share, everyone, 0, 0, tiled=True)  11.4 us
    all_to_all x1, blocking collectives, shards(): lax.all_to_all(sum_and_copy('sum_wide', slabs, gram_parts, face), 'slab',...  11.1 us
    all_to_all x1, starting transfers between devices, shards(): lax.all_to_all(sum_and_copy('sum_slab', wide, gram_parts), ('half', 'pair...  10.5 us
    pallas_call x1, Pallas kernels, inner_field(): pl.pallas_call(inner_kernel, out_shape=(jax.ShapeDtypeStruct(state.shape,...  9.33 us
    pallas_call x1, Pallas kernels, outer_field(): pl.pallas_call(outer_kernel, out_shape=(jax.ShapeDtypeStruct(state.shape,...  8.28 us
    all_to_all x1, starting transfers between devices, shards(): gram_parts = lax.all_to_all(gram, 'slab', 0, 0, tiled=True)  6.49 us
    all_to_all x1, waiting for transfers between devices, shards(): share = lax.all_to_all(share, everyone, 0, 0, tiled=True)  6.34 us
    pallas_call x1, Pallas kernels, factor_and_basis(): pl.pallas_call(functools.partial(factor_kernel, total_rows), out_shape=(j...  5.73 us
  transfers between devices with their start and end apart: 6, of which 3 were waited for; matrix products, arithmetic and copies ran while one was open for 0% of the time, Pallas kernels for 30%

profile of v5, /device:TPU:1, one launch (start us, length us, event | category | flops | bytes accessed | tf_op | source)
XLA Modules:
  0.0 92.8 jit_solution(1089732898515942880)
XLA Ops:
  0.6 0.0 copy-start.1
  0.6 0.9 copy-done.1
  1.5 0.9 %gram.1 = f32[128,128]{1,0:T(8,128)} custom-call(f32[256,128]{1,0:T(8,128)S(1)} %bitcast.11), custom_call_target="tpu_custom_call" | custom-call | flops 9000000 | bytes 200000 | tf_op jit(solution)/shard_map/gram/pallas_call | solution.py:502
  2.5 6.5 %all-to-all-start = ((f32[8,16,128]{2,1,0:T(8,128)}), f32[8,16,128]{2,1,0:T(8,128)S(1)}, u32[]{:S(2)}, u32[]{:S(2)}) async-start(f32[8,16,128]{2,1,0:T(8,128)} %bitcast.2), calls=%async_computation | async-start | bytes 131072 | tf_op jit(solution)/shard_map/all_to_all | solution.py:749
  9.0 0.7 copy-done.4
  9.7 4.0 %pack_edges.1 = (bf16[18,32,1024]{2,1,0:T(8,128)(2,1)}, bf16[18,32,1024]{2,1,0:T(8,128)(2,1)}) custom-call(f32[16,32,1024]{2,1,0:T(8,128)} %bitcast.15, bf16[16,32,1024]{2,1,0:T(8,128)(2,1)} %bitcast.18, bf16[3,16,32,1024]{3,2,1,0:T(8,128)(2,1)} %bitcast.8, f32[1,256]{1,0:T(1,128)S(1)} %copy-done.4), custom_call_target="tpu_custom_call" | custom-call | flops 2000000 | bytes 9000000 | tf_op jit(solution)/shard_map/pack_edges/pallas_call | solution.py:111
  13.6 0.2 all-to-all-done.parts
  13.8 3.4 %collective-permute-start = (bf16[18,32,1024]{2,1,0:T(8,128)(2,1)}, bf16[18,32,1024]{2,1,0:T(8,128)(2,1)}, u32[]{:S(2)}, u32[]{:S(2)}) collective-permute-start(bf16[18,32,1024]{2,1,0:T(8,128)(2,1)} %get-tuple-element.24), channel_id=1, source_target_pairs={{0,1},{1,2},{2,3},{3,4},{4,5},{5,6},{6,7},{8,9},{9,10},{10,11},{11... | collective-permute-start | bytes 3538952 | tf_op jit(solution)/shard_map/ppermute | solution.py:751
  17.2 2.0 %collective-permute-start.1 = (bf16[18,32,1024]{2,1,0:T(8,128)(2,1)}, bf16[18,32,1024]{2,1,0:T(8,128)(2,1)}, u32[]{:S(2)}, u32[]{:S(2)}) collective-permute-start(bf16[18,32,1024]{2,1,0:T(8,128)(2,1)} %get-tuple-element.25), channel_id=1, source_target_pairs={{1,0},{2,1},{3,2},{4,3},{5,4},{6,5},{7,6},{9,8},{10,9},{11,10},{12... | collective-permute-start | bytes 3538952 | tf_op jit(solution)/shard_map/ppermute | solution.py:752
  19.2 0.8 sum_slab.1
  20.0 10.5 %all-to-all-start.1 = ((f32[32,16,128]{2,1,0:T(8,128)}), f32[32,16,128]{2,1,0:T(8,128)S(1)}, u32[]{:S(2)}, u32[]{:S(2)}) async-start(f32[32,16,128]{2,1,0:T(8,128)} %sum_slab.1), calls=%async_computation.1 | async-start | bytes 524288 | tf_op jit(solution)/shard_map/all_to_all | solution.py:753
  30.5 0.0 copy-done
  30.5 0.0 copy-done.5
  30.5 9.3 %inner_field.1 = (f32[16,32,1024]{2,1,0:T(8,128)}, f32[3,4,8,32,128]{4,3,2,1,0:T(8,128)S(1)}, f32[8,128]{1,0:T(8,128)S(1)}) custom-call(f32[16,32,1024]{2,1,0:T(8,128)} %bitcast.16, bf16[16,32,1024]{2,1,0:T(8,128)(2,1)} %bitcast.19, bf16[3,16,32,1024]{3,2,1,0:T(8,128)(2,1)S(1)} %bitcast.9, f32[1,256]{1,0:T(1,128)S(1)} %copy-done.5), custom_call_target="tpu_custom_call" | custom-call | flops 50000000 | bytes 20000000 | tf_op jit(solution)/shard_map/inner_field/pallas_call | solution.py:345
  39.8 0.0 collective-permute-done.left
  39.8 0.0 collective-permute-done.1.right
  39.8 0.0 copy-start.2
  39.8 0.0 copy-start.6
  39.9 8.3 %outer_field.1 = (f32[16,32,1024]{2,1,0:T(8,128)}, f32[2,128]{1,0:T(2,128)S(1)}) custom-call(f32[16,32,1024]{2,1,0:T(8,128)} %bitcast.17, bf16[16,32,1024]{2,1,0:T(8,128)(2,1)} %bitcast.20, bf16[3,16,32,1024]{3,2,1,0:T(8,128)(2,1)S(1)} %bitcast.10, f32[1,256]{1,0:T(1,128)S(1)} %copy-done.5, ...), custom_call_target="tpu_custom_call", output_to_operand_aliasing={{0}: (6, {})} | custom-call | flops 35000000 | bytes 15000000 | tf_op jit(solution)/shard_map/outer_field/pallas_call | solution.py:455
  48.1 5.2 %collective-permute-start.2 = (f32[2,128]{1,0:T(2,128)S(1)}, f32[2,128]{1,0:T(2,128)S(1)}, u32[]{:S(2)}, u32[]{:S(2)}) collective-permute-start(f32[2,128]{1,0:T(2,128)S(1)} %get-tuple-element.31), channel_id=1, source_target_pairs={{0,128},{128,0},{1,129},{129,1},{2,130},{130,2},{3,131},{131,3},{4... | collective-permute-start | bytes 3080 | tf_op jit(solution)/shard_map/ppermute | solution.py:760
  53.4 0.0 all-to-all-done.1.parts
  53.4 1.2 %collective-permute-done.2.rest_0_ = f32[2,128]{1,0:T(2,128)S(1)} collective-permute-done((f32[2,128]{1,0:T(2,128)S(1)}, f32[2,128]{1,0:T(2,128)S(1)}, u32[]{:S(2)}, u32[]{:S(2)}) %collective-permute-start.2) | collective-permute-done | bytes 1056 | tf_op jit(solution)/shard_map/ppermute | solution.py:760
  54.6 11.1 %all_to_all.20.gathered = f32[8,24,128]{2,1,0:T(8,128)S(1)} all-to-all(f32[8,24,128]{2,1,0:T(8,128)S(1)} %sum_wide.1), channel_id=1, replica_groups=mesh['half'=2,'pair'=16,'slab'=8] {'slab'}, dimensions={0} | all-to-all | bytes 196608 | tf_op jit(solution)/shard_map/all_to_all | solution.py:761
  65.7 0.0 copy-done.2
  65.7 0.0 copy-done.6
  65.7 1.3 %tilde.1 = (f32[1,256]{1,0:T(1,128)S(1)}, f32[256,1,128]{2,1,0:T(1,128)}) custom-call(f32[8,24,128]{2,1,0:T(8,128)S(1)} %all_to_all.20.gathered, s32[1,256]{1,0:T(1,128)S(1)} %copy-done.6, f32[1,256]{1,0:T(1,128)S(1)} %copy-done.5, f32[256,128]{1,0:T(8,128)S(1)} %bitcast.12), custom_call_target="tpu_custom_call" | custom-call | flops 9000000 | bytes 900000 | tf_op jit(solution)/shard_map/tilde/pallas_call | solution.py:567
  67.0 11.4 %all-to-all-start.3 = ((f32[256,1,128]{2,1,0:T(1,128)}), f32[256,1,128]{2,1,0:T(1,128)S(1)}, u32[]{:S(2)}, u32[]{:S(2)}) async-start(f32[256,1,128]{2,1,0:T(1,128)} %get-tuple-element.32), calls=%async_computation.3 | async-start | bytes 262144 | tf_op jit(solution)/shard_map/all_to_all | solution.py:767
  78.4 0.0 copy-start.3
  78.4 0.9 copy-done.3
  79.3 5.7 %factor.1 = (f32[128,128]{1,0:T(8,128)S(1)}, f32[256,128]{1,0:T(8,128)}, f32[256,128]{1,0:T(8,128)S(1)}) custom-call(f32[8,24,128]{2,1,0:T(8,128)S(1)} %all_to_all.20.gathered, f32[256,128]{1,0:T(8,128)S(1)} %bitcast.13, f32[256,128]{1,0:T(8,128)S(1)} %bitcast.14), custom_call_target="tpu_custom_call" | custom-call | flops 30000000 | bytes 9000000 | tf_op jit(solution)/shard_map/factor/pallas_call | solution.py:685
  85.0 6.3 %all-to-all-done.3.parts = f32[256,1,128]{2,1,0:T(1,128)S(1)} async-done(((f32[256,1,128]{2,1,0:T(1,128)}), f32[256,1,128]{2,1,0:T(1,128)S(1)}, u32[]{:S(2)}, u32[]{:S(2)}) %all-to-all-start.3) | async-done | bytes 131104 | tf_op jit(solution)/shard_map/all_to_all | solution.py:767
  91.4 1.4 %update.1 = f32[1,256]{1,0:T(1,128)} custom-call(f32[256,1,128]{2,1,0:T(1,128)S(1)} %all-to-all-done.3.parts, f32[128,128]{1,0:T(8,128)S(1)} %get-tuple-element.33.inverse, f32[256,128]{1,0:T(8,128)S(1)} %get-tuple-element.34.turned, f32[1,256]{1,0:T(1,128)S(1)} %get-tuple-element.35.tilde), custom_call_target="tpu_custom_call" | custom-call | flops 9000000 | bytes 400000 | tf_op jit(solution)/shard_map/update/pallas_call | solution.py:712
  (4 shorter events, 0.0 us)
Async XLA Ops:
  0.6 0.9 copy-start.1
  2.5 11.4 %all-to-all-start = ((f32[8,16,128]{2,1,0:T(8,128)}), f32[8,16,128]{2,1,0:T(8,128)S(1)}, u32[]{:S(2)}, u32[]{:S(2)}) async-start(f32[8,16,128]{2,1,0:T(8,128)} %bitcast.2), calls=%async_computation | async-start | bytes 131072 | tf_op jit(solution)/shard_map/all_to_all | solution.py:749
  9.0 0.7 copy-start.4
  9.7 20.8 %copy-start = (bf16[3,1,16,32,1024]{4,3,2,1,0:T(8,128)(2,1)S(1)}, bf16[3,1,16,32,1024]{4,3,2,1,0:T(8,128)(2,1)}, u32[]{:S(2)}) copy-start(bf16[3,1,16,32,1024]{4,3,2,1,0:T(8,128)(2,1)} %param.9) | copy-start | bytes 9437188
  9.7 20.8 %copy-start.5 = (f32[1,256]{1,0:T(1,128)S(1)}, f32[1,256]{1,0:T(1,128)}, u32[]{:S(2)}) copy-start(f32[1,256]{1,0:T(1,128)} %guess.7) | copy-start | bytes 3076
  13.8 26.0 %collective-permute-start = (bf16[18,32,1024]{2,1,0:T(8,128)(2,1)}, bf16[18,32,1024]{2,1,0:T(8,128)(2,1)}, u32[]{:S(2)}, u32[]{:S(2)}) collective-permute-start(bf16[18,32,1024]{2,1,0:T(8,128)(2,1)} %get-tuple-element.24), channel_id=1, source_target_pairs={{0,1},{1,2},{2,3},{3,4},{4,5},{5,6},{6,7},{8,9},{9,10},{10,11},{11... | collective-permute-start | bytes 3538952 | tf_op jit(solution)/shard_map/ppermute | solution.py:751
  17.2 22.6 %collective-permute-start.1 = (bf16[18,32,1024]{2,1,0:T(8,128)(2,1)}, bf16[18,32,1024]{2,1,0:T(8,128)(2,1)}, u32[]{:S(2)}, u32[]{:S(2)}) collective-permute-start(bf16[18,32,1024]{2,1,0:T(8,128)(2,1)} %get-tuple-element.25), channel_id=1, source_target_pairs={{1,0},{2,1},{3,2},{4,3},{5,4},{6,5},{7,6},{9,8},{10,9},{11,10},{12... | collective-permute-start | bytes 3538952 | tf_op jit(solution)/shard_map/ppermute | solution.py:752
  20.0 33.4 %all-to-all-start.1 = ((f32[32,16,128]{2,1,0:T(8,128)}), f32[32,16,128]{2,1,0:T(8,128)S(1)}, u32[]{:S(2)}, u32[]{:S(2)}) async-start(f32[32,16,128]{2,1,0:T(8,128)} %sum_slab.1), calls=%async_computation.1 | async-start | bytes 524288 | tf_op jit(solution)/shard_map/all_to_all | solution.py:753
  39.8 25.8 %copy-start.2 = (f32[1,256,128]{2,1,0:T(8,128)S(1)}, f32[1,256,128]{2,1,0:T(8,128)}, u32[]{:S(2)}) copy-start(f32[1,256,128]{2,1,0:T(8,128)} %param.12) | copy-start | bytes 393220
  39.8 25.8 %copy-start.6 = (s32[1,256]{1,0:T(1,128)S(1)}, s32[1,256]{1,0:T(1,128)}, u32[]{:S(2)}) copy-start(s32[1,256]{1,0:T(1,128)} %partner_rows.1) | copy-start | bytes 3076
  48.1 6.4 %collective-permute-start.2 = (f32[2,128]{1,0:T(2,128)S(1)}, f32[2,128]{1,0:T(2,128)S(1)}, u32[]{:S(2)}, u32[]{:S(2)}) collective-permute-start(f32[2,128]{1,0:T(2,128)S(1)} %get-tuple-element.31), channel_id=1, source_target_pairs={{0,128},{128,0},{1,129},{129,1},{2,130},{130,2},{3,131},{131,3},{4... | collective-permute-start | bytes 3080 | tf_op jit(solution)/shard_map/ppermute | solution.py:760
  67.0 24.4 %all-to-all-start.3 = ((f32[256,1,128]{2,1,0:T(1,128)}), f32[256,1,128]{2,1,0:T(1,128)S(1)}, u32[]{:S(2)}, u32[]{:S(2)}) async-start(f32[256,1,128]{2,1,0:T(1,128)} %get-tuple-element.32), calls=%async_computation.3 | async-start | bytes 262144 | tf_op jit(solution)/shard_map/all_to_all | solution.py:767
  78.4 0.9 copy-start.3

commit v6 on v5

--- a/solution.py
+++ b/solution.py
@@ -37,13 +37,20 @@
         copy.wait()
 
 
-def ghost_line(guess, first, block):
+def ghost_line(guess, first, block, in_lanes=False):
     lane = lax.broadcasted_iota(jnp.int32, (1, LANES), 1)
     strips = LANES // INTERFACE_STRIP
     at = first + block * strips
-    row = jnp.full((1, LANES), guess[0, at], jnp.float32)
+    def value(strip):
+        if in_lanes:
+            spot = guess[:, pl.ds(at // LANES * LANES, LANES)]
+            own = at % LANES + strip
+            return jnp.broadcast_to(spot[:, own : own + 1], (1, LANES))
+        return guess[0, at + strip]
+
+    row = jnp.broadcast_to(value(0), (1, LANES))
     for strip in range(1, strips):
-        row = jnp.where(lane < strip * INTERFACE_STRIP, row, guess[0, at + strip])
+        row = jnp.where(lane < strip * INTERFACE_STRIP, row, value(strip))
     return row
 
 
@@ -75,7 +82,7 @@
     for out, first in ((right, count - COEF_REACH), (left, 0)):
         for block in range(lane_blocks):
             lines = [
-                ghost_line(guess, (first + plane) * per_plane, block)
+                ghost_line(guess, (first + plane) * per_plane, block, in_lanes=True)
                 for plane in range(COEF_REACH)
             ]
             pieces = []
@@ -111,7 +118,7 @@
     return pl.pallas_call(
         pack_kernel,
         out_shape=(pltpu.HBM(message.shape, message.dtype),) * 2,
-        in_specs=[ANY, ANY, ANY, SCALARS],
+        in_specs=[ANY, ANY, ANY, WHOLE],
         out_specs=(pl.BlockSpec(memory_space=pltpu.HBM),) * 2,
         scratch_shapes=[
             pltpu.VMEM(message.shape, message.dtype),
@@ -157,16 +164,15 @@
 
 
 FLOOR = 8
-UNROLL = 2
-
-
-def sweep(source, target, coefs, held, height, first, stop, shift=0):
+
+
+def sweep(source, target, coefs, held, height, first, stop, shift=0, unroll=2):
     lane_blocks = source.shape[1]
     lane = lax.broadcasted_iota(jnp.int32, (SUBS, LANES), 1)
     zero = jnp.zeros((SUBS, LANES), jnp.float32)
 
     def pair(step, carry):
-        low = first + step * UNROLL
+        low = first + step * unroll
         kept = {}
 
         def load(offset, tile, block, shift=0):
@@ -184,7 +190,7 @@
 
         for block in range(lane_blocks):
             for tile in range(height // SUBS):
-                for offset in range(UNROLL):
+                for offset in range(unroll):
                     plane = low + offset
                     carry_in = rolled(offset, tile, block - 1, 1) if block else zero
                     minus_z = jnp.where(lane == 0, carry_in, rolled(offset, tile, block, 1))
@@ -223,8 +229,8 @@
                         target[plane - shift, rows, pl.ds(block * LANES, LANES)] = value
         return carry
 
-    assert (stop - first) % UNROLL == 0
-    lax.fori_loop(0, (stop - first) // UNROLL, pair, 0)
+    assert (stop - first) % unroll == 0
+    lax.fori_loop(0, (stop - first) // unroll, pair, 0)
 
 
 def set_rims(grids, guess, per_plane, spots, height):
@@ -424,9 +430,11 @@
     pair = (grid, other)
     for step in range(1, SWEEPS):
         source, target = pair[(step + 1) % 2], pair[step % 2]
-        sweep(source, target, None, held, height, step, step + SWEEPS)
+        sweep(source, target, None, held, height, step, step + SWEEPS, unroll=SWEEPS)
         right_first = count + REACH - SWEEPS - step
-        sweep(source, target, None, held, height, right_first, right_first + SWEEPS)
+        sweep(
+            source, target, None, held, height, right_first, right_first + SWEEPS, unroll=SWEEPS
+        )
         spots = (REACH + step, REACH + step + 1, count - 2 - step, count - 1 - step)
         for index, at in enumerate(spots):
             target[at, :, pl.ds(FLOOR, height), :] = edges[step - 1, index]
@@ -434,7 +442,7 @@
     pushes = []
     for index, first in enumerate((SWEEPS, count - SWEEPS)):
         kept = index * SWEEPS
-        sweep(source, plain, None, held, height, first, first + SWEEPS, first - kept)
+        sweep(source, plain, None, held, height, first, first + SWEEPS, first - kept, SWEEPS)
         final = 0 if index == 0 else count - SWEEPS
         pushes.append(
             pltpu.make_async_copy(

time: 93.3 us -> 91.6 us (0.982)
  Pallas kernels: 31.8 us -> 30.1 us
    pallas_call x1, Pallas kernels: 8.28 us -> 7.26 us  [outer_field(): pl.pallas_call(outer_kernel, out_shape=(jax.ShapeDtypeStruct(state.shape,...]
  transfers between devices with their start and end apart: 6 -> 6, of which waited for: 3 -> 3; matrix products, arithmetic and copies ran while one was open for 0% -> 0% of each run, Pallas kernels for 30% -> 29%
where the time goes in v6:
time: 91.6 us; the launch traced here: 91.1 us
  starting transfers between devices  39 us (43%)
  Pallas kernels  30.1 us (33%)
  blocking collectives  10.4 us (11%)
  waiting for transfers between devices  8.4 us (9%)
  local copies, waits for them, and re-layouts  2.5 us (3%)
    all_to_all x1, starting transfers between devices, shards(): share = lax.all_to_all(share, everyone, 0, 0, tiled=True)  11.4 us
    all_to_all x1, starting transfers between devices, shards(): lax.all_to_all(sum_and_copy('sum_slab', wide, gram_parts), ('half', 'pair...  10.5 us
    all_to_all x1, blocking collectives, shards(): lax.all_to_all(sum_and_copy('sum_wide', slabs, gram_parts, face), 'slab',...  10.4 us
    pallas_call x1, Pallas kernels, inner_field(): pl.pallas_call(inner_kernel, out_shape=(jax.ShapeDtypeStruct(state.shape,...  9.33 us
    pallas_call x1, Pallas kernels, outer_field(): pl.pallas_call(outer_kernel, out_shape=(jax.ShapeDtypeStruct(state.shape,...  7.26 us
    all_to_all x1, starting transfers between devices, shards(): gram_parts = lax.all_to_all(gram, 'slab', 0, 0, tiled=True)  6.49 us
    all_to_all x1, waiting for transfers between devices, shards(): share = lax.all_to_all(share, everyone, 0, 0, tiled=True)  6.34 us
    pallas_call x1, Pallas kernels, factor_and_basis(): pl.pallas_call(functools.partial(factor_kernel, total_rows), out_shape=(j...  5.73 us
  transfers between devices with their start and end apart: 6, of which 3 were waited for; matrix products, arithmetic and copies ran while one was open for 0% of the time, Pallas kernels for 29%

profile of v6, /device:TPU:1, one launch (start us, length us, event | category | flops | bytes accessed | tf_op | source)
XLA Modules:
  0.0 91.1 jit_solution(7346891324461651819)
XLA Ops:
  0.6 0.0 copy-start.1
  0.6 0.9 copy-done.1
  1.5 0.9 %gram.1 = f32[128,128]{1,0:T(8,128)} custom-call(f32[256,128]{1,0:T(8,128)S(1)} %bitcast.11), custom_call_target="tpu_custom_call" | custom-call | flops 9000000 | bytes 200000 | tf_op jit(solution)/shard_map/gram/pallas_call | solution.py:510
  2.5 6.5 %all-to-all-start = ((f32[8,16,128]{2,1,0:T(8,128)}), f32[8,16,128]{2,1,0:T(8,128)S(1)}, u32[]{:S(2)}, u32[]{:S(2)}) async-start(f32[8,16,128]{2,1,0:T(8,128)} %bitcast.2), calls=%async_computation | async-start | bytes 131072 | tf_op jit(solution)/shard_map/all_to_all | solution.py:757
  9.0 0.7 copy-done.4
  9.7 3.3 %pack_edges.1 = (bf16[18,32,1024]{2,1,0:T(8,128)(2,1)}, bf16[18,32,1024]{2,1,0:T(8,128)(2,1)}) custom-call(f32[16,32,1024]{2,1,0:T(8,128)} %bitcast.15, bf16[16,32,1024]{2,1,0:T(8,128)(2,1)} %bitcast.18, bf16[3,16,32,1024]{3,2,1,0:T(8,128)(2,1)} %bitcast.8, f32[1,256]{1,0:T(1,128)S(1)} %copy-done.4), custom_call_target="tpu_custom_call" | custom-call | flops 2000000 | bytes 9000000 | tf_op jit(solution)/shard_map/pack_edges/pallas_call | solution.py:118
  13.0 0.9 all-to-all-done.parts
  13.8 2.9 %collective-permute-start = (bf16[18,32,1024]{2,1,0:T(8,128)(2,1)}, bf16[18,32,1024]{2,1,0:T(8,128)(2,1)}, u32[]{:S(2)}, u32[]{:S(2)}) collective-permute-start(bf16[18,32,1024]{2,1,0:T(8,128)(2,1)} %get-tuple-element.24), channel_id=1, source_target_pairs={{0,1},{1,2},{2,3},{3,4},{4,5},{5,6},{6,7},{8,9},{9,10},{10,11},{11... | collective-permute-start | bytes 3538952 | tf_op jit(solution)/shard_map/ppermute | solution.py:759
  16.7 2.5 %collective-permute-start.1 = (bf16[18,32,1024]{2,1,0:T(8,128)(2,1)}, bf16[18,32,1024]{2,1,0:T(8,128)(2,1)}, u32[]{:S(2)}, u32[]{:S(2)}) collective-permute-start(bf16[18,32,1024]{2,1,0:T(8,128)(2,1)} %get-tuple-element.25), channel_id=1, source_target_pairs={{1,0},{2,1},{3,2},{4,3},{5,4},{6,5},{7,6},{9,8},{10,9},{11,10},{12... | collective-permute-start | bytes 3538952 | tf_op jit(solution)/shard_map/ppermute | solution.py:760
  19.2 0.8 sum_slab.1
  20.0 10.5 %all-to-all-start.1 = ((f32[32,16,128]{2,1,0:T(8,128)}), f32[32,16,128]{2,1,0:T(8,128)S(1)}, u32[]{:S(2)}, u32[]{:S(2)}) async-start(f32[32,16,128]{2,1,0:T(8,128)} %sum_slab.1), calls=%async_computation.1 | async-start | bytes 524288 | tf_op jit(solution)/shard_map/all_to_all | solution.py:761
  30.5 0.0 copy-done
  30.5 0.0 copy-done.5
  30.5 9.3 %inner_field.1 = (f32[16,32,1024]{2,1,0:T(8,128)}, f32[3,4,8,32,128]{4,3,2,1,0:T(8,128)S(1)}, f32[8,128]{1,0:T(8,128)S(1)}) custom-call(f32[16,32,1024]{2,1,0:T(8,128)} %bitcast.16, bf16[16,32,1024]{2,1,0:T(8,128)(2,1)} %bitcast.19, bf16[3,16,32,1024]{3,2,1,0:T(8,128)(2,1)S(1)} %bitcast.9, f32[1,256]{1,0:T(1,128)S(1)} %copy-done.5), custom_call_target="tpu_custom_call" | custom-call | flops 50000000 | bytes 20000000 | tf_op jit(solution)/shard_map/inner_field/pallas_call | solution.py:351
  39.8 0.0 collective-permute-done.left
  39.8 0.0 collective-permute-done.1.right
  39.8 0.0 copy-start.2
  39.8 0.0 copy-start.6
  39.9 7.3 %outer_field.1 = (f32[16,32,1024]{2,1,0:T(8,128)}, f32[2,128]{1,0:T(2,128)S(1)}) custom-call(f32[16,32,1024]{2,1,0:T(8,128)} %bitcast.17, bf16[16,32,1024]{2,1,0:T(8,128)(2,1)} %bitcast.20, bf16[3,16,32,1024]{3,2,1,0:T(8,128)(2,1)S(1)} %bitcast.10, f32[1,256]{1,0:T(1,128)S(1)} %copy-done.5, ...), custom_call_target="tpu_custom_call", output_to_operand_aliasing={{0}: (6, {})} | custom-call | flops 35000000 | bytes 15000000 | tf_op jit(solution)/shard_map/outer_field/pallas_call | solution.py:463
  47.1 5.2 %collective-permute-start.2 = (f32[2,128]{1,0:T(2,128)S(1)}, f32[2,128]{1,0:T(2,128)S(1)}, u32[]{:S(2)}, u32[]{:S(2)}) collective-permute-start(f32[2,128]{1,0:T(2,128)S(1)} %get-tuple-element.31), channel_id=1, source_target_pairs={{0,128},{128,0},{1,129},{129,1},{2,130},{130,2},{3,131},{131,3},{4... | collective-permute-start | bytes 3080 | tf_op jit(solution)/shard_map/ppermute | solution.py:768
  52.4 0.0 all-to-all-done.1.parts
  52.4 1.2 %collective-permute-done.2.rest_0_ = f32[2,128]{1,0:T(2,128)S(1)} collective-permute-done((f32[2,128]{1,0:T(2,128)S(1)}, f32[2,128]{1,0:T(2,128)S(1)}, u32[]{:S(2)}, u32[]{:S(2)}) %collective-permute-start.2) | collective-permute-done | bytes 1056 | tf_op jit(solution)/shard_map/ppermute | solution.py:768
  53.6 10.4 %all_to_all.20.gathered = f32[8,24,128]{2,1,0:T(8,128)S(1)} all-to-all(f32[8,24,128]{2,1,0:T(8,128)S(1)} %sum_wide.1), channel_id=1, replica_groups=mesh['half'=2,'pair'=16,'slab'=8] {'slab'}, dimensions={0} | all-to-all | bytes 196608 | tf_op jit(solution)/shard_map/all_to_all | solution.py:769
  64.0 0.0 copy-done.2
  64.0 0.0 copy-done.6
  64.0 1.3 %tilde.1 = (f32[1,256]{1,0:T(1,128)S(1)}, f32[256,1,128]{2,1,0:T(1,128)}) custom-call(f32[8,24,128]{2,1,0:T(8,128)S(1)} %all_to_all.20.gathered, s32[1,256]{1,0:T(1,128)S(1)} %copy-done.6, f32[1,256]{1,0:T(1,128)S(1)} %copy-done.5, f32[256,128]{1,0:T(8,128)S(1)} %bitcast.12), custom_call_target="tpu_custom_call" | custom-call | flops 9000000 | bytes 900000 | tf_op jit(solution)/shard_map/tilde/pallas_call | solution.py:575
  65.3 11.4 %all-to-all-start.3 = ((f32[256,1,128]{2,1,0:T(1,128)}), f32[256,1,128]{2,1,0:T(1,128)S(1)}, u32[]{:S(2)}, u32[]{:S(2)}) async-start(f32[256,1,128]{2,1,0:T(1,128)} %get-tuple-element.32), calls=%async_computation.3 | async-start | bytes 262144 | tf_op jit(solution)/shard_map/all_to_all | solution.py:775
  76.7 0.0 copy-start.3
  76.7 0.9 copy-done.3
  77.6 5.7 %factor.1 = (f32[128,128]{1,0:T(8,128)S(1)}, f32[256,128]{1,0:T(8,128)}, f32[256,128]{1,0:T(8,128)S(1)}) custom-call(f32[8,24,128]{2,1,0:T(8,128)S(1)} %all_to_all.20.gathered, f32[256,128]{1,0:T(8,128)S(1)} %bitcast.13, f32[256,128]{1,0:T(8,128)S(1)} %bitcast.14), custom_call_target="tpu_custom_call" | custom-call | flops 30000000 | bytes 9000000 | tf_op jit(solution)/shard_map/factor/pallas_call | solution.py:693
  83.3 6.3 %all-to-all-done.3.parts = f32[256,1,128]{2,1,0:T(1,128)S(1)} async-done(((f32[256,1,128]{2,1,0:T(1,128)}), f32[256,1,128]{2,1,0:T(1,128)S(1)}, u32[]{:S(2)}, u32[]{:S(2)}) %all-to-all-start.3) | async-done | bytes 131104 | tf_op jit(solution)/shard_map/all_to_all | solution.py:775
  89.7 1.4 %update.1 = f32[1,256]{1,0:T(1,128)} custom-call(f32[256,1,128]{2,1,0:T(1,128)S(1)} %all-to-all-done.3.parts, f32[128,128]{1,0:T(8,128)S(1)} %get-tuple-element.33.inverse, f32[256,128]{1,0:T(8,128)S(1)} %get-tuple-element.34.turned, f32[1,256]{1,0:T(1,128)S(1)} %get-tuple-element.35.tilde), custom_call_target="tpu_custom_call" | custom-call | flops 9000000 | bytes 400000 | tf_op jit(solution)/shard_map/update/pallas_call | solution.py:720
  (4 shorter events, 0.0 us)
Async XLA Ops:
  0.6 0.9 copy-start.1
  2.5 11.4 %all-to-all-start = ((f32[8,16,128]{2,1,0:T(8,128)}), f32[8,16,128]{2,1,0:T(8,128)S(1)}, u32[]{:S(2)}, u32[]{:S(2)}) async-start(f32[8,16,128]{2,1,0:T(8,128)} %bitcast.2), calls=%async_computation | async-start | bytes 131072 | tf_op jit(solution)/shard_map/all_to_all | solution.py:757
  9.0 0.7 copy-start.4
  9.7 20.8 %copy-start = (bf16[3,1,16,32,1024]{4,3,2,1,0:T(8,128)(2,1)S(1)}, bf16[3,1,16,32,1024]{4,3,2,1,0:T(8,128)(2,1)}, u32[]{:S(2)}) copy-start(bf16[3,1,16,32,1024]{4,3,2,1,0:T(8,128)(2,1)} %param.9) | copy-start | bytes 9437188
  9.7 20.8 %copy-start.5 = (f32[1,256]{1,0:T(1,128)S(1)}, f32[1,256]{1,0:T(1,128)}, u32[]{:S(2)}) copy-start(f32[1,256]{1,0:T(1,128)} %guess.7) | copy-start | bytes 3076
  13.8 26.0 %collective-permute-start = (bf16[18,32,1024]{2,1,0:T(8,128)(2,1)}, bf16[18,32,1024]{2,1,0:T(8,128)(2,1)}, u32[]{:S(2)}, u32[]{:S(2)}) collective-permute-start(bf16[18,32,1024]{2,1,0:T(8,128)(2,1)} %get-tuple-element.24), channel_id=1, source_target_pairs={{0,1},{1,2},{2,3},{3,4},{4,5},{5,6},{6,7},{8,9},{9,10},{10,11},{11... | collective-permute-start | bytes 3538952 | tf_op jit(solution)/shard_map/ppermute | solution.py:759
  16.7 23.1 %collective-permute-start.1 = (bf16[18,32,1024]{2,1,0:T(8,128)(2,1)}, bf16[18,32,1024]{2,1,0:T(8,128)(2,1)}, u32[]{:S(2)}, u32[]{:S(2)}) collective-permute-start(bf16[18,32,1024]{2,1,0:T(8,128)(2,1)} %get-tuple-element.25), channel_id=1, source_target_pairs={{1,0},{2,1},{3,2},{4,3},{5,4},{6,5},{7,6},{9,8},{10,9},{11,10},{12... | collective-permute-start | bytes 3538952 | tf_op jit(solution)/shard_map/ppermute | solution.py:760
  20.0 32.4 %all-to-all-start.1 = ((f32[32,16,128]{2,1,0:T(8,128)}), f32[32,16,128]{2,1,0:T(8,128)S(1)}, u32[]{:S(2)}, u32[]{:S(2)}) async-start(f32[32,16,128]{2,1,0:T(8,128)} %sum_slab.1), calls=%async_computation.1 | async-start | bytes 524288 | tf_op jit(solution)/shard_map/all_to_all | solution.py:761
  39.8 24.1 %copy-start.2 = (f32[1,256,128]{2,1,0:T(8,128)S(1)}, f32[1,256,128]{2,1,0:T(8,128)}, u32[]{:S(2)}) copy-start(f32[1,256,128]{2,1,0:T(8,128)} %param.12) | copy-start | bytes 393220
  39.8 24.1 %copy-start.6 = (s32[1,256]{1,0:T(1,128)S(1)}, s32[1,256]{1,0:T(1,128)}, u32[]{:S(2)}) copy-start(s32[1,256]{1,0:T(1,128)} %partner_rows.1) | copy-start | bytes 3076
  47.1 6.4 %collective-permute-start.2 = (f32[2,128]{1,0:T(2,128)S(1)}, f32[2,128]{1,0:T(2,128)S(1)}, u32[]{:S(2)}, u32[]{:S(2)}) collective-permute-start(f32[2,128]{1,0:T(2,128)S(1)} %get-tuple-element.31), channel_id=1, source_target_pairs={{0,128},{128,0},{1,129},{129,1},{2,130},{130,2},{3,131},{131,3},{4... | collective-permute-start | bytes 3080 | tf_op jit(solution)/shard_map/ppermute | solution.py:768
  65.3 24.4 %all-to-all-start.3 = ((f32[256,1,128]{2,1,0:T(1,128)}), f32[256,1,128]{2,1,0:T(1,128)S(1)}, u32[]{:S(2)}, u32[]{:S(2)}) async-start(f32[256,1,128]{2,1,0:T(1,128)} %get-tuple-element.32), calls=%async_computation.3 | async-start | bytes 262144 | tf_op jit(solution)/shard_map/all_to_all | solution.py:775
  76.7 0.9 copy-start.3
